TPU v7x, 32 devices: a whole 2x2x4 slice. The times are simulated.
32 devices in a mesh: seq: 16 (over z, y, x), head: 2 (over core).
Axes of the slice: x: 2, y: 2, z: 4, core: 2. Of those that a mesh axis runs over, the one named last changes fastest.
Arguments:
- tokens: bfloat16 [16384, 768], P(('seq', 'head')), may hold values from -6 to 6
- documents: int32 [16384], replicated, may hold values from 0 to 15, never falling along the last dimension, each value on 1 to 4096 neighbouring positions
- offsets: int32 [5, 16], P(None, 'head'), may hold values from 0 to 15, as said below
- in_proj: bfloat16 [3, 768, 768], P(None, None, 'head'), may hold values from -0.21875 to 0.21875
- out_proj: bfloat16 [768, 768], P('head'), may hold values from -4 to 4
- up_proj: bfloat16 [768, 3072], P(None, 'head'), may hold values from -0.21875 to 0.21875
- down_proj: bfloat16 [3072, 768], P('head'), may hold values from -0.109375 to 0.109375
- first_gain: float32 [768], replicated, may hold values from 0.25 to 1.75
- first_shift: float32 [768], replicated, may hold values from -3 to 3
- second_gain: float32 [768], replicated, may hold values from 0.25 to 1.75
- second_shift: float32 [768], replicated, may hold values from -3 to 3
- cotangent: bfloat16 [16384, 768], P(('seq', 'head')), may hold values from -6 to 6
Outputs:
- block_out: bfloat16 [16384, 768], P(('seq', 'head'))
- grad_tokens: float32 [16384, 768], P(('seq', 'head'))
- grad_in_proj: float32 [3, 768, 768], P(None, None, 'head')
- grad_out_proj: float32 [768, 768], P('head')
- grad_up_proj: float32 [768, 3072], P(None, 'head')
- grad_down_proj: float32 [3072, 768], P('head')
- grad_first_gain: float32 [768], replicated
- grad_first_shift: float32 [768], replicated
- grad_second_gain: float32 [768], replicated
- grad_second_shift: float32 [768], replicated
Inputs may be any that keep to these rules, and one draw needn't show every extreme that they name: `documents`: slide numbers of the packed tiles never fall; each slide covers 1 to 4096 tiles, one exactly 4096. offsets[b, h] lies in 0 to 2^b - 1; in every branch b some head has offset 2^b - 1.
All inputs are finite; a program needn't handle non-finite values.
Results may differ from a plain program's by a relative error of at most 0.015.
Values may be sent and summed in bfloat16 or wider, within the bound.
A program may use at most 256 MiB of HBM per device.

v0:
```python
from functools import partial

import jax
import jax.numpy as jnp
from jax import lax
from jax.sharding import PartitionSpec as P

E = 48
BRANCHES = 5
SEG0 = 1024


EPS = 1e-05
NEG = -1e30


def swapped(value, axis, bit):
    mask = 2**bit
    pairs = [(source, source ^ mask) for source in range(lax.axis_size(axis))]
    return lax.ppermute(value, axis, pairs)


def norm_rows(values, gain, shift):
    centre = jnp.mean(values, axis=-1, keepdims=True)
    centred = values - centre
    spread = jnp.mean(centred * centred, axis=-1, keepdims=True)
    return centred * lax.rsqrt(spread + EPS) * gain + shift


def stride_mask(stride, chosen_at, ndim):
    slot_ids = jnp.arange(stride, dtype=jnp.int32)[None, :]
    chosen = slot_ids == chosen_at[:, None]
    return chosen.reshape((chosen_at.shape[0],) + (1,) * (ndim - 1) + (stride,))


def pick_cols(values, stride, chosen_at):
    if stride == 1:
        return values
    shape_in = values.shape
    blocked = values.reshape(shape_in[:-1] + (shape_in[-1] // stride, stride))
    chosen = stride_mask(stride, chosen_at, len(shape_in))
    picked = jnp.sum(jnp.where(chosen, blocked, jnp.zeros((), values.dtype)), axis=-1)
    return picked


def place_cols(values, stride, chosen_at, filler):
    if stride == 1:
        return values
    shape_in = values.shape
    chosen = stride_mask(stride, chosen_at, len(shape_in))
    spread = jnp.where(chosen, values[..., None], filler)
    return spread.reshape(shape_in[:-1] + (shape_in[-1] * stride,))


def branch_shape(branch, seq_len):
    stride = 2**branch
    seg_span = SEG0 * stride
    local_len = min(seg_span, seq_len)
    members = seg_span // local_len
    return (stride, seg_span, seq_len // local_len, members, members.bit_length() - 1)


def group_gather(pair, levels, seq_id):
    for bit_pos in range(levels):
        partner = swapped(pair, "seq", bit_pos)
        upper = seq_id // 2**bit_pos % 2 == 1
        pair = jnp.where(
            upper,
            jnp.concatenate([partner, pair], axis=-1),
            jnp.concatenate([pair, partner], axis=-1),
        )
    return pair


def group_reduce(grads, levels, seq_id):
    for bit_pos in reversed(range(levels)):
        half_cols = grads.shape[-1] // 2
        upper = seq_id // 2**bit_pos % 2 == 1
        lower_part = grads[..., :half_cols]
        upper_part = grads[..., half_cols:]
        outgoing = jnp.where(upper, lower_part, upper_part)
        staying = jnp.where(upper, upper_part, lower_part)
        grads = staying + swapped(outgoing.astype(jnp.bfloat16), "seq", bit_pos).astype(
            outgoing.dtype
        )
    return grads


def to_blocks(values, n_local):
    shape_in = values.shape
    split = values.reshape(shape_in[:-1] + (n_local, shape_in[-1] // n_local))
    return jnp.moveaxis(split, -2, 0)


def from_blocks(values):
    joined = jnp.moveaxis(values, 0, -2)
    shape_in = joined.shape
    return joined.reshape(shape_in[:-2] + (shape_in[-2] * shape_in[-1],))


def attend_block(q_blk, k_blk, q_docs, k_docs):
    scores = jnp.einsum("heq,hek->hqk", q_blk, k_blk, preferred_element_type=jnp.float32)
    same_doc = q_docs[:, :, None] == k_docs[:, None, :]
    scores = jnp.where(same_doc, scores, NEG)
    row_top = jnp.max(scores, axis=-1, keepdims=True)
    row_sum = jnp.sum(jnp.exp(scores - row_top), axis=-1, keepdims=True)
    log_sum = row_top + jnp.log(row_sum)
    return (jnp.exp(scores - log_sum), log_sum[..., 0])


def seg_forward(items):
    q_blk, k_blk, v_blk, q_docs, k_docs = items
    prob_rows, log_sum = attend_block(q_blk, k_blk, q_docs, k_docs)
    result = jnp.einsum(
        "hqk,hek->heq", prob_rows.astype(jnp.bfloat16), v_blk, preferred_element_type=jnp.float32
    )
    return (result, log_sum)


def seg_backward(items):
    q_blk, k_blk, v_blk, q_docs, k_docs, go_blk, gl_blk = items
    prob_rows, log_sum = attend_block(q_blk, k_blk, q_docs, k_docs)
    grad_p = jnp.einsum("heq,hek->hqk", go_blk, v_blk, preferred_element_type=jnp.float32)
    inner = jnp.sum(prob_rows * grad_p, axis=-1, keepdims=True)
    grad_s = (prob_rows * (grad_p - inner + gl_blk[:, :, None])).astype(jnp.bfloat16)
    grad_q = jnp.einsum("hqk,hek->heq", grad_s, k_blk, preferred_element_type=jnp.float32)
    grad_k = jnp.einsum("hqk,heq->hek", grad_s, q_blk, preferred_element_type=jnp.float32)
    grad_v = jnp.einsum(
        "hqk,heq->hek", prob_rows.astype(jnp.bfloat16), go_blk, preferred_element_type=jnp.float32
    )
    return (grad_q, grad_k, grad_v)


def local(
    tokens,
    documents,
    offsets,
    in_proj,
    out_proj,
    up_proj,
    down_proj,
    first_gain,
    first_shift,
    second_gain,
    second_shift,
    cotangent,
):
    head_count = lax.axis_size("head")
    seq_id = lax.axis_index("seq")
    row_count = tokens.shape[0]
    seq_len = row_count * head_count
    heads_local = offsets.shape[1]
    scaling = E ** (-0.5)
    gelu_exact = partial(jax.nn.gelu, approximate=False)
    x_rows = tokens.astype(jnp.float32)
    normed_one = norm_rows(x_rows, first_gain, first_shift)
    gathered_one = lax.all_gather(normed_one.astype(jnp.bfloat16), "head", axis=0, tiled=True)
    projected = jnp.einsum("td,jdc->jct", gathered_one, in_proj, preferred_element_type=jnp.float32)
    queries = (projected[0] * scaling).astype(jnp.bfloat16).reshape(heads_local, E, seq_len)
    keys = projected[1].astype(jnp.bfloat16).reshape(heads_local, E, seq_len)
    values = projected[2].astype(jnp.bfloat16).reshape(heads_local, E, seq_len)
    my_docs = lax.dynamic_slice_in_dim(documents, seq_id * seq_len, seq_len)
    my_head_docs = jnp.broadcast_to(my_docs[None, :], (heads_local, seq_len))
    saved = []
    out_list = []
    lse_list = []
    for branch in range(BRANCHES):
        stride, seg_span, n_local, members, levels = branch_shape(branch, seq_len)
        chosen_at = offsets[branch]
        q_sel = to_blocks(pick_cols(queries, stride, chosen_at), n_local)
        pair_own = jnp.stack(
            [pick_cols(keys, stride, chosen_at), pick_cols(values, stride, chosen_at)]
        )
        pair_all = to_blocks(group_gather(pair_own, levels, seq_id), n_local)
        group_start = seq_id // members * members * seq_len
        group_docs = lax.dynamic_slice_in_dim(documents, group_start, members * seq_len)
        group_head_docs = jnp.broadcast_to(group_docs[None, :], (heads_local, members * seq_len))
        key_docs = to_blocks(pick_cols(group_head_docs, stride, chosen_at), n_local)
        query_docs = to_blocks(pick_cols(my_head_docs, stride, chosen_at), n_local)
        out_sel, lse_sel = lax.map(
            seg_forward, (q_sel, pair_all[:, 0], pair_all[:, 1], query_docs, key_docs)
        )
        out_list.append(place_cols(from_blocks(out_sel), stride, chosen_at, 0.0))
        lse_list.append(place_cols(from_blocks(lse_sel), stride, chosen_at, NEG))
        saved.append((q_sel, pair_own, pair_all, query_docs, key_docs))
    lse_stack = jnp.stack(lse_list)
    lse_top = jnp.max(lse_stack, axis=0)
    lse_all = lse_top + jnp.log(jnp.sum(jnp.exp(lse_stack - lse_top), axis=0))
    mix_weights = jnp.exp(lse_stack - lse_all)
    merged = mix_weights[0][:, None, :] * out_list[0]
    for branch in range(1, BRANCHES):
        merged = merged + mix_weights[branch][:, None, :] * out_list[branch]
    mixed = merged.reshape(heads_local * E, seq_len).astype(jnp.bfloat16)
    part = mixed
    hidden_one = x_rows + lax.psum_scatter(
        jnp.einsum("ct,cd->td", part, out_proj, preferred_element_type=jnp.float32).astype(
            jnp.bfloat16
        ),
        "head",
        scatter_dimension=0,
        tiled=True,
    ).astype(jnp.float32)
    normed_two = norm_rows(hidden_one, second_gain, second_shift)
    normed_low = normed_two.astype(jnp.bfloat16)
    gathered_two = lax.all_gather(normed_low, "head", axis=0, tiled=True)
    pre_act = jnp.dot(gathered_two, up_proj, preferred_element_type=jnp.float32)
    hidden, gelu_pull = jax.vjp(gelu_exact, pre_act)
    hidden = hidden.astype(jnp.bfloat16)
    part = lax.slice_in_dim(hidden, 0, row_count * lax.axis_size("head"), axis=0)
    block_rows = hidden_one + lax.psum_scatter(
        jnp.dot(part, down_proj, preferred_element_type=jnp.float32).astype(jnp.bfloat16),
        "head",
        scatter_dimension=0,
        tiled=True,
    ).astype(jnp.float32)
    cot_all = lax.all_gather(cotangent, "head", axis=0, tiled=True)
    grad_down = jnp.einsum("tf,td->fd", hidden, cot_all, preferred_element_type=jnp.float32)
    grad_hidden_act = jnp.einsum(
        "td,fd->tf", cot_all, down_proj, preferred_element_type=jnp.float32
    )
    grad_pre = gelu_pull(grad_hidden_act)[0].astype(jnp.bfloat16)
    grad_up = jnp.einsum("td,tf->df", gathered_two, grad_pre, preferred_element_type=jnp.float32)
    part = grad_pre
    grad_normed_two = lax.psum_scatter(
        jnp.einsum("tf,df->td", part, up_proj, preferred_element_type=jnp.float32).astype(
            jnp.bfloat16
        ),
        "head",
        scatter_dimension=0,
        tiled=True,
    ).astype(jnp.float32)
    pull_two = jax.vjp(norm_rows, hidden_one, second_gain, second_shift)[1]
    grad_ln_two, grad_gain_two, grad_shift_two = pull_two(grad_normed_two)
    grad_hidden_one = cotangent.astype(jnp.float32) + grad_ln_two
    grad_attn = lax.all_gather(grad_hidden_one.astype(jnp.bfloat16), "head", axis=0, tiled=True)
    grad_out = jnp.einsum("ct,td->cd", mixed, grad_attn, preferred_element_type=jnp.float32)
    grad_merged = jnp.einsum("td,cd->ct", grad_attn, out_proj, preferred_element_type=jnp.float32)
    grad_merged = grad_merged.reshape(heads_local, E, seq_len)
    merged_dot = jnp.sum(grad_merged * merged, axis=1)
    grad_query = jnp.zeros((heads_local, E, seq_len), jnp.float32)
    grad_pair = jnp.zeros((2, heads_local, E, seq_len), jnp.float32)
    for branch in range(BRANCHES):
        stride, seg_span, n_local, members, levels = branch_shape(branch, seq_len)
        chosen_at = offsets[branch]
        q_sel, pair_own, pair_kept, query_docs, key_docs = saved[branch]
        pair_all = to_blocks(group_gather(pair_own, levels, seq_id), n_local)
        weight_b = mix_weights[branch]
        branch_dot = jnp.sum(grad_merged * out_list[branch], axis=1)
        grad_lse = weight_b * (branch_dot - merged_dot)
        grad_out_b = (weight_b[:, None, :] * grad_merged).astype(jnp.bfloat16)
        go_sel = to_blocks(pick_cols(grad_out_b, stride, chosen_at), n_local)
        gl_sel = to_blocks(pick_cols(grad_lse, stride, chosen_at), n_local)
        gq_sel, gk_sel, gv_sel = lax.map(
            seg_backward,
            (q_sel, pair_all[:, 0], pair_all[:, 1], query_docs, key_docs, go_sel, gl_sel),
        )
        pair_grad = jnp.stack([from_blocks(gk_sel), from_blocks(gv_sel)])
        pair_grad = group_reduce(pair_grad, levels, seq_id)
        grad_query = grad_query + place_cols(from_blocks(gq_sel), stride, chosen_at, 0.0)
        grad_pair = grad_pair + jnp.stack(
            [
                place_cols(pair_grad[0], stride, chosen_at, 0.0),
                place_cols(pair_grad[1], stride, chosen_at, 0.0),
            ]
        )
    grad_qkv = jnp.stack(
        [
            (grad_query * scaling).astype(jnp.bfloat16),
            grad_pair[0].astype(jnp.bfloat16),
            grad_pair[1].astype(jnp.bfloat16),
        ]
    )
    grad_qkv = grad_qkv.reshape(3, heads_local * E, seq_len)
    grad_in = jnp.einsum("td,jct->jdc", gathered_one, grad_qkv, preferred_element_type=jnp.float32)
    part = grad_qkv
    grad_normed_one = lax.psum_scatter(
        jnp.einsum("jct,jdc->td", part, in_proj, preferred_element_type=jnp.float32).astype(
            jnp.bfloat16
        ),
        "head",
        scatter_dimension=0,
        tiled=True,
    ).astype(jnp.float32)
    pull_one = jax.vjp(norm_rows, x_rows, first_gain, first_shift)[1]
    grad_ln_one, grad_gain_one, grad_shift_one = pull_one(grad_normed_one)
    grad_tokens = grad_hidden_one + grad_ln_one
    summed = lax.psum(
        (
            grad_in,
            grad_out,
            grad_up,
            grad_down,
            grad_gain_one,
            grad_shift_one,
            grad_gain_two,
            grad_shift_two,
        ),
        "seq",
    )
    gains = lax.psum((summed[4], summed[5], summed[6], summed[7]), "head")
    return (
        block_rows.astype(jnp.bfloat16),
        grad_tokens,
        summed[0],
        summed[1],
        summed[2],
        summed[3],
        gains[0],
        gains[1],
        gains[2],
        gains[3],
    )


def solution(mesh):
    placed = (
        P(("seq", "head"), None),
        P(),
        P(None, "head"),
        P(None, None, "head"),
        P("head", None),
        P(None, "head"),
        P("head", None),
        P(),
        P(),
        P(),
        P(),
        P(("seq", "head"), None),
    )
    return jax.shard_map(
        local,
        mesh=mesh,
        in_specs=placed,
        out_specs=(
            P(("seq", "head"), None),
            P(("seq", "head"), None),
            P(None, None, "head"),
            P("head", None),
            P(None, "head"),
            P("head", None),
            P(),
            P(),
            P(),
            P(),
        ),
        check_vma=False,
    )
```

profile of v0, /device:TPU:0, one launch (start us, length us, event | category | flops | bytes accessed | tf_op | source)
XLA Modules:
  0.0 1434.0 jit_solution(4574814471280006634)
XLA Ops:
  126.3 6.4 select_reduce_fusion.5
  136.3 6.9 select_reduce_fusion.8
  148.6 7.5 select_reduce_fusion.11
  165.0 13.7 fusion.6
  184.6 14.7 %exponential_reduce_fusion = f32[8,1024]{1,0:T(8,128)} fusion(f32[8,1024,1024]{1,2,0:T(8,128)} %get-tuple-element.440, f32[8,1024]{1,0:T(8,128)S(1)} %get-tuple-element.439, s32[1024]{0:T(1024)S(1)} %dynamic_slice.149), kind=kLoop, calls=%fused_computation.9 | loop fusion | flops 33546240 | bytes 33624064 | tf_op jit(solution)/shard_map/while/body/eval_jaxpr/reduce_sum | solution.py:106
  240.9 8.6 fusion.176
  317.8 19.1 %fusion.9 = bf16[8,1024,1024]{1,2,0:T(8,128)(2,1)} fusion(f32[8,1024,1024]{1,2,0:T(8,128)} %get-tuple-element.440, f32[8,1024]{1,0:T(8,128)S(1)} %get-tuple-element.389, s32[1024]{0:T(1024)S(1)} %dynamic_slice.149), kind=kLoop, calls=%fused_computation.12 | loop fusion | flops 33554432 | bytes 50368512 | tf_op jit(solution)/shard_map/while/body/eval_jaxpr/convert_element_type | solution.py:115
  345.5 13.4 fusion.230
  362.1 7.6 reduce-scatter.5.cloned.1.call-done
  373.6 10.6 all-gather.7.cloned.1.call-done
  384.2 7.5 fusion.236
  396.7 19.1 %add_convert_fusion = (bf16[1024,1536]{1,0:T(8,128)(2,1)S(1)}, f32[1024,1536]{1,0:T(8,128)}) fusion(f32[1024,1536]{1,0:T(8,128)} %fusion.236, bf16[1024,768]{1,0:T(8,128)(2,1)} %all-gather.9.cloned.1.call-done, bf16[1536,768]{1,0:T(8,128)(2,1)S(1)} %copy-done), kind=kOutput, calls=%fused_computation.45 | convolution fusion | flops 2529165312 | bytes 19660800 | tf_op jit(solution)/shard_map/td,fd->tf/dot_general | solution.py:218
  421.2 6.2 multiply_convert_fusion.3
  436.4 7.5 reduce-scatter.7.cloned.1.call-done
  453.1 6.4 all-gather.11.cloned.1.call-done
  475.3 12.1 convolution_bitcast_fusion.6
  497.2 6.6 fusion.121
  503.9 7.1 fusion.145
  527.6 14.0 fusion.98
  541.6 13.5 fusion.148
  577.7 20.8 %fusion.62 = f32[8,48,256]{2,1,0:T(8,128)} fusion(f32[8,256,1024]{2,1,0:T(8,128)} %fusion.177, f32[8,256,1024]{2,1,0:T(8,128)} %copy-done.6, f32[8,256]{1,0:T(8,128)S(1)} %copy.397, f32[8,256]{1,0:T(8,128)S(1)} %copy-done.148, s32[8,1024]{1,0:T(8,128)S(1)} %copy-done.104, s32[8,256]{1,0:T(8,128)S(1)} %copy-done.128, ...), kind=kOutput, calls=%fused_computation.63 | convolution fusion | flops 224398336 | bytes 34840576 | tf_op jit(solution)/shard_map/while/body/eval_jaxpr/hqk,hek->heq/dot_general | solution.py:126
  598.5 20.5 %fusion.151 = f32[1,8,48,1024]{3,2,1,0:T(8,128)} fusion(bf16[8,48,256]{2,1,0:T(8,128)(2,1)S(1)} %copy-done.82, f32[8,256,1024]{2,1,0:T(8,128)} %fusion.177, f32[8,256,1024]{2,1,0:T(8,128)} %copy-done.6, f32[8,256]{1,0:T(8,128)S(1)} %copy.397, f32[8,256]{1,0:T(8,128)S(1)} %copy-done.148, s32[8,1024]{1,0:T(8,128)S(1)} %copy-done.104, ...), kind=kOutput, calls=%fused_computation.215 | convolution fusion | flops 224398336 | bytes 18604032 | tf_op jit(solution)/shard_map/while/body/eval_jaxpr/hqk,heq->hek/dot_general | solution.py:127
  623.6 9.1 convolution_bitcast_fusion.5
  632.8 8.1 fusion.175
  644.1 39.7 %fusion.42 = f32[8,48,512]{2,1,0:T(8,128)} fusion(f32[8,512,1024]{2,1,0:T(8,128)} %fusion.175, f32[8,512]{1,0:T(8,128)S(1)} %copy.390, f32[8,512,1024]{2,1,0:T(8,128)} %copy-done.4, f32[8,512]{1,0:T(8,128)S(1)} %copy-done.130, s32[8,1024]{1,0:T(8,128)S(1)} %copy-done.102, s32[8,512]{1,0:T(8,128)S(1)} %copy-done.114, ...), kind=kOutput, calls=%fused_computation.33 | convolution fusion | flops 448795648 | bytes 68829184 | tf_op jit(solution)/shard_map/while/body/eval_jaxpr/hqk,hek->heq/dot_general | solution.py:126
  683.8 41.0 %fusion.142 = f32[1,8,48,1024]{3,2,1,0:T(8,128)} fusion(bf16[8,48,512]{2,1,0:T(8,128)(2,1)} %copy.340, f32[8,512,1024]{2,1,0:T(8,128)} %fusion.175, f32[8,512]{1,0:T(8,128)S(1)} %copy.390, f32[8,512]{1,0:T(8,128)S(1)} %copy-done.130, f32[8,512,1024]{2,1,0:T(8,128)} %copy-done.4, s32[8,1024]{1,0:T(8,128)S(1)} %copy-done.102, s32[8,512]{1,0:T(8,128)S(1)} %copy-done.114), kind=kOutput, calls=%fused_computation.212 | convolution fusion | flops 448795648 | bytes 35602432 | tf_op jit(solution)/shard_map/while/body/eval_jaxpr/hqk,heq->hek/dot_general | solution.py:127
  724.8 13.2 fusion.173
  804.3 44.3 %fusion.14 = f32[8,48,1024]{2,1,0:T(8,128)} fusion(f32[8,1024,1024]{1,2,0:T(8,128)} %fusion.173, f32[8,1024,1024]{1,2,0:T(8,128)} %get-tuple-element.440, f32[8,1024]{1,0:T(8,128)S(1)} %copy-done.146, f32[8,1024]{1,0:T(8,128)S(1)} %copy-done.106, s32[1024]{0:T(1024)S(1)} %copy-done.84, bf16[1,2,8,48,1024]{4,3,2,1,0:T(8,128)(2,1)S(1)} %copy-done.11), kind=kOutput, calls=%fused_computation.14 | convolution fusion | flops 897590272 | bytes 136691712 | tf_op jit(solution)/shard_map/while/body/eval_jaxpr/hqk,hek->heq/dot_general | solution.py:126
  855.1 45.0 %fusion.154 = f32[1,8,48,1024]{3,2,1,0:T(8,128)} fusion(bf16[8,48,1024]{2,1,0:T(8,128)(2,1)} %bitcast.302, f32[8,1024,1024]{1,2,0:T(8,128)} %fusion.173, f32[8,1024,1024]{1,2,0:T(8,128)} %get-tuple-element.440, f32[8,1024]{1,0:T(8,128)S(1)} %copy-done.146, f32[8,1024]{1,0:T(8,128)S(1)} %copy-done.106, s32[1024]{0:T(1024)S(1)} %copy-done.84), kind=kOutput, calls=%fused_computation.221 | convolution fusion | flops 897590272 | bytes 69537792 | tf_op jit(solution)/shard_map/while/body/eval_jaxpr/hqk,heq->hek/dot_general | solution.py:127
  996.7 7.4 fusion.240
  1020.3 78.5 %all-reduce = (f32[768]{0:T(1024)S(1)}, f32[768]{0:T(1024)S(1)}, f32[768]{0:T(1024)S(1)}, f32[768]{0:T(1024)S(1)}) all-reduce(f32[768]{0:T(1024)S(1)} %get-tuple-element.314, f32[768]{0:T(1024)S(1)} %get-tuple-element.323, f32[768]{0:T(1024)S(1)} %copy-done.165, f32[768]{0:T(1024)S(1)} %copy-done.166), channel_id=1, replica_groups=mesh['seq'=16,'head'=2] {'seq'}, use_global_device_ids=true, to_apply=%region_67.68 | all-reduce | flops 3072 | bytes 24576 | tf_op jit(solution)/shard_map/psum | solution.py:287
  1105.6 306.3 %all-reduce.5.cloned.1.call-done = (f32[3,768,384]{1,2,0:T(8,128)}, f32[384,768]{1,0:T(8,128)}, f32[768,1536]{1,0:T(8,128)}, f32[1536,768]{1,0:T(8,128)}) async-done(((f32[3,768,384]{1,2,0:T(8,128)}, f32[384,768]{1,0:T(8,128)}, f32[768,1536]{1,0:T(8,128)}, f32[1536,768]{1,0:T(8,128)}), (f32[3,768,384]{1,2,0:T(8,128)}, f32[384,768]{1,0:T(8,128)}, f32[768,1536]{1,0:T(8,128)}, ...) | async-done | bytes 14155792 | tf_op jit(solution)/shard_map/psum | solution.py:287
  (707 shorter events, 575.2 us)
Async XLA Ops:
  7.2 389.5 %copy-start = (bf16[1536,768]{1,0:T(8,128)(2,1)S(1)}, bf16[1536,768]{1,0:T(8,128)(2,1)}, u32[]{:S(2)}) copy-start(bf16[1536,768]{1,0:T(8,128)(2,1)} %param.18) | copy-start | bytes 7077892
  7.2 44.0 %all-gather.5.cloned.1.call-start = ((), (), s32[]{:S(2)}) async-start(), calls=%async_computation.4 | async-start | bytes 2359296 | tf_op jit(solution)/shard_map/all_gather | solution.py:157
  13.4 356.3 %reduce-scatter.5.cloned.1.call-start = ((), (), s32[]{:S(2)}) async-start(), calls=%async_computation.5 | async-start | bytes 2359296 | tf_op jit(solution)/shard_map/reduce_scatter | solution.py:195
  14.2 303.6 %copy-start.83 = (s32[1024]{0:T(1024)}, s32[1024]{0:T(1024)S(1)}, u32[]{:S(2)}) copy-start(s32[1024]{0:T(1024)S(1)} %dynamic_slice.149) | copy-start | bytes 12292
  50.5 248.6 %copy-start.132 = (s32[8,128]{1,0:T(8,128)}, s32[8,128]{1,0:T(8,128)S(1)}, u32[]{:S(2)}) copy-start(s32[8,128]{1,0:T(8,128)S(1)} %select_reduce_fusion.16) | copy-start | bytes 12292
  123.4 55.3 %collective-permute-start.6 = (bf16[2,8,48,64]{3,2,1,0:T(8,128)(2,1)}, bf16[2,8,48,64]{3,2,1,0:T(8,128)(2,1)}, u32[]{:S(2)}, u32[]{:S(2)}) collective-permute-start(bf16[2,8,48,64]{3,2,1,0:T(8,128)(2,1)} %pad_maximum_fusion.10), channel_id=1, source_target_pairs={{0,2},{2,0},{4,6},{6,4},{8,10},{10,8},{12,14},{14,12},{16,18},{18,... | collective-permute-start | bytes 294920 | tf_op jit(solution)/shard_map/ppermute | solution.py:20
  136.3 45.8 %collective-permute-start.3 = (bf16[2,8,48,128]{3,2,1,0:T(8,128)(2,1)}, bf16[2,8,48,128]{3,2,1,0:T(8,128)(2,1)}, u32[]{:S(2)}, u32[]{:S(2)}) collective-permute-start(bf16[2,8,48,128]{3,2,1,0:T(8,128)(2,1)} %pad_maximum_fusion.9), channel_id=1, source_target_pairs={{0,2},{2,0},{4,6},{6,4},{8,10},{10,8},{12,14},{14,12},{16,18},{18,... | collective-permute-start | bytes 589832 | tf_op jit(solution)/shard_map/ppermute | solution.py:20
  146.6 63.6 %collective-permute-start.1 = (bf16[2,8,48,256]{3,2,1,0:T(8,128)(2,1)}, bf16[2,8,48,256]{3,2,1,0:T(8,128)(2,1)}, u32[]{:S(2)}, u32[]{:S(2)}) collective-permute-start(bf16[2,8,48,256]{3,2,1,0:T(8,128)(2,1)} %pad_maximum_fusion.8), channel_id=1, source_target_pairs={{0,2},{2,0},{4,6},{6,4},{8,10},{10,8},{12,14},{14,12},{16,18},{18,... | collective-permute-start | bytes 1179656 | tf_op jit(solution)/shard_map/ppermute | solution.py:20
  163.8 59.0 %collective-permute-start = (bf16[2,8,48,512]{3,2,1,0:T(8,128)(2,1)}, bf16[2,8,48,512]{3,2,1,0:T(8,128)(2,1)}, u32[]{:S(2)}, u32[]{:S(2)}) collective-permute-start(bf16[2,8,48,512]{3,2,1,0:T(8,128)(2,1)} %get-tuple-element.399), channel_id=1, source_target_pairs={{0,2},{2,0},{4,6},{6,4},{8,10},{10,8},{12,14},{14,12},{16,18},{18,... | collective-permute-start | bytes 2359304 | tf_op jit(solution)/shard_map/ppermute | solution.py:20
  180.7 26.7 %collective-permute-start.7 = (bf16[2,8,48,128]{3,2,1,0:T(8,128)(2,1)}, bf16[2,8,48,128]{3,2,1,0:T(8,128)(2,1)}, u32[]{:S(2)}, u32[]{:S(2)}) collective-permute-start(bf16[2,8,48,128]{3,2,1,0:T(8,128)(2,1)} %maximum_select_fusion.9), channel_id=1, source_target_pairs={{0,4},{2,6},{4,0},{6,2},{8,12},{10,14},{12,8},{14,10},{16,20},{18,... | collective-permute-start | bytes 589832 | tf_op jit(solution)/shard_map/ppermute | solution.py:20
  184.0 32.1 %collective-permute-start.4 = (bf16[2,8,48,256]{3,2,1,0:T(8,128)(2,1)}, bf16[2,8,48,256]{3,2,1,0:T(8,128)(2,1)}, u32[]{:S(2)}, u32[]{:S(2)}) collective-permute-start(bf16[2,8,48,256]{3,2,1,0:T(8,128)(2,1)} %maximum_select_fusion.7), channel_id=1, source_target_pairs={{0,4},{2,6},{4,0},{6,2},{8,12},{10,14},{12,8},{14,10},{16,20},{18,... | collective-permute-start | bytes 1179656 | tf_op jit(solution)/shard_map/ppermute | solution.py:20
  208.7 10.4 collective-permute-start.8
  212.4 47.9 %collective-permute-start.2 = (bf16[2,8,48,512]{3,2,1,0:T(8,128)(2,1)}, bf16[2,8,48,512]{3,2,1,0:T(8,128)(2,1)}, u32[]{:S(2)}, u32[]{:S(2)}) collective-permute-start(bf16[2,8,48,512]{3,2,1,0:T(8,128)(2,1)} %maximum_select_fusion.4), channel_id=1, source_target_pairs={{0,4},{2,6},{4,0},{6,2},{8,12},{10,14},{12,8},{14,10},{16,20},{18,... | collective-permute-start | bytes 2359304 | tf_op jit(solution)/shard_map/ppermute | solution.py:20
  218.6 68.9 %collective-permute-start.5 = (bf16[2,8,48,512]{3,2,1,0:T(8,128)(2,1)}, bf16[2,8,48,512]{3,2,1,0:T(8,128)(2,1)}, u32[]{:S(2)}, u32[]{:S(2)}) collective-permute-start(bf16[2,8,48,512]{3,2,1,0:T(8,128)(2,1)} %maximum_select_fusion.5), channel_id=1, source_target_pairs={{0,8},{2,10},{4,12},{6,14},{8,0},{10,2},{12,4},{14,6},{16,24},{18,... | collective-permute-start | bytes 2359304 | tf_op jit(solution)/shard_map/ppermute | solution.py:20
  220.2 88.5 %collective-permute-start.9 = (bf16[2,8,48,512]{3,2,1,0:T(8,128)(2,1)}, bf16[2,8,48,512]{3,2,1,0:T(8,128)(2,1)}, u32[]{:S(2)}, u32[]{:S(2)}) collective-permute-start(bf16[2,8,48,512]{3,2,1,0:T(8,128)(2,1)} %maximum_select_fusion.6), channel_id=1, source_target_pairs={{0,16},{2,18},{4,20},{6,22},{8,24},{10,26},{12,28},{14,30},{16,0},... | collective-permute-start | bytes 2359304 | tf_op jit(solution)/shard_map/ppermute | solution.py:20
  362.1 22.1 %all-gather.7.cloned.1.call-start = ((), (), s32[]{:S(2)}) async-start(), calls=%async_computation.6 | async-start | bytes 2359296 | tf_op jit(solution)/shard_map/all_gather | solution.py:205
  373.0 23.7 %all-gather.9.cloned.1.call-start = ((), (), s32[]{:S(2)}) async-start(), calls=%async_computation.8 | async-start | bytes 2359296 | tf_op jit(solution)/shard_map/all_gather | solution.py:216
  373.6 59.3 %reduce-scatter.9.cloned.1.call-start = ((), (), s32[]{:S(2)}) async-start(), calls=%async_computation.9 | async-start | bytes 2359296 | tf_op jit(solution)/shard_map/reduce_scatter | solution.py:224
  421.2 22.8 %reduce-scatter.7.cloned.1.call-start = ((), (), s32[]{:S(2)}) async-start(), calls=%async_computation.7 | async-start | bytes 2359296 | tf_op jit(solution)/shard_map/reduce_scatter | solution.py:210
  432.8 26.6 %all-gather.11.cloned.1.call-start = ((), (), s32[]{:S(2)}) async-start(), calls=%async_computation.10 | async-start | bytes 2359296 | tf_op jit(solution)/shard_map/all_gather | solution.py:235
  448.2 566.9 %reduce-scatter.11.cloned.1.call-start = ((), (), s32[]{:S(2)}) async-start(), calls=%async_computation.11 | async-start | bytes 2359296 | tf_op jit(solution)/shard_map/reduce_scatter | solution.py:276
  741.2 159.0 %collective-permute-start.16 = (bf16[2,8,48,512]{3,2,1,0:T(8,128)(2,1)}, bf16[2,8,48,512]{3,2,1,0:T(8,128)(2,1)}, u32[]{:S(2)}, u32[]{:S(2)}) collective-permute-start(bf16[2,8,48,512]{3,2,1,0:T(8,128)(2,1)} %select_convert_fusion), channel_id=1, source_target_pairs={{0,16},{2,18},{4,20},{6,22},{8,24},{10,26},{12,28},{14,30},{16,0},... | collective-permute-start | bytes 2359304 | tf_op jit(solution)/shard_map/ppermute | solution.py:20
  757.5 146.3 %collective-permute-start.13 = (bf16[2,8,48,512]{3,2,1,0:T(8,128)(2,1)}, bf16[2,8,48,512]{3,2,1,0:T(8,128)(2,1)}, u32[]{:S(2)}, u32[]{:S(2)}) collective-permute-start(bf16[2,8,48,512]{3,2,1,0:T(8,128)(2,1)} %select_convert_fusion.1), channel_id=1, source_target_pairs={{0,8},{2,10},{4,12},{6,14},{8,0},{10,2},{12,4},{14,6},{16,24},{18,... | collective-permute-start | bytes 2359304 | tf_op jit(solution)/shard_map/ppermute | solution.py:20
  773.8 133.4 %collective-permute-start.11 = (bf16[2,8,48,512]{3,2,1,0:T(8,128)(2,1)}, bf16[2,8,48,512]{3,2,1,0:T(8,128)(2,1)}, u32[]{:S(2)}, u32[]{:S(2)}) collective-permute-start(bf16[2,8,48,512]{3,2,1,0:T(8,128)(2,1)} %select_convert_fusion.2), channel_id=1, source_target_pairs={{0,4},{2,6},{4,0},{6,2},{8,12},{10,14},{12,8},{14,10},{16,20},{18,... | collective-permute-start | bytes 2359304 | tf_op jit(solution)/shard_map/ppermute | solution.py:20
  788.1 122.4 %collective-permute-start.10 = (bf16[2,8,48,512]{3,2,1,0:T(8,128)(2,1)}, bf16[2,8,48,512]{3,2,1,0:T(8,128)(2,1)}, u32[]{:S(2)}, u32[]{:S(2)}) collective-permute-start(bf16[2,8,48,512]{3,2,1,0:T(8,128)(2,1)} %select_convert_fusion.3), channel_id=1, source_target_pairs={{0,2},{2,0},{4,6},{6,4},{8,10},{10,8},{12,14},{14,12},{16,18},{18,... | collective-permute-start | bytes 2359304 | tf_op jit(solution)/shard_map/ppermute | solution.py:20
  903.3 25.1 %collective-permute-start.17 = (bf16[2,8,48,256]{3,2,1,0:T(8,128)(2,1)}, bf16[2,8,48,256]{3,2,1,0:T(8,128)(2,1)}, u32[]{:S(2)}, u32[]{:S(2)}) collective-permute-start(bf16[2,8,48,256]{3,2,1,0:T(8,128)(2,1)} %select_convert_fusion.4), channel_id=1, source_target_pairs={{0,8},{2,10},{4,12},{6,14},{8,0},{10,2},{12,4},{14,6},{16,24},{18,... | collective-permute-start | bytes 1179656 | tf_op jit(solution)/shard_map/ppermute | solution.py:20
  906.6 24.9 %collective-permute-start.14 = (bf16[2,8,48,256]{3,2,1,0:T(8,128)(2,1)}, bf16[2,8,48,256]{3,2,1,0:T(8,128)(2,1)}, u32[]{:S(2)}, u32[]{:S(2)}) collective-permute-start(bf16[2,8,48,256]{3,2,1,0:T(8,128)(2,1)} %select_convert_fusion.5), channel_id=1, source_target_pairs={{0,4},{2,6},{4,0},{6,2},{8,12},{10,14},{12,8},{14,10},{16,20},{18,... | collective-permute-start | bytes 1179656 | tf_op jit(solution)/shard_map/ppermute | solution.py:20
  910.0 25.0 %collective-permute-start.12 = (bf16[2,8,48,256]{3,2,1,0:T(8,128)(2,1)}, bf16[2,8,48,256]{3,2,1,0:T(8,128)(2,1)}, u32[]{:S(2)}, u32[]{:S(2)}) collective-permute-start(bf16[2,8,48,256]{3,2,1,0:T(8,128)(2,1)} %select_convert_fusion.6), channel_id=1, source_target_pairs={{0,2},{2,0},{4,6},{6,4},{8,10},{10,8},{12,14},{14,12},{16,18},{18,... | collective-permute-start | bytes 1179656 | tf_op jit(solution)/shard_map/ppermute | solution.py:20
  930.4 24.5 %collective-permute-start.18 = (bf16[2,8,48,128]{3,2,1,0:T(8,128)(2,1)}, bf16[2,8,48,128]{3,2,1,0:T(8,128)(2,1)}, u32[]{:S(2)}, u32[]{:S(2)}) collective-permute-start(bf16[2,8,48,128]{3,2,1,0:T(8,128)(2,1)} %select_convert_fusion.8), channel_id=1, source_target_pairs={{0,4},{2,6},{4,0},{6,2},{8,12},{10,14},{12,8},{14,10},{16,20},{18,... | collective-permute-start | bytes 589832 | tf_op jit(solution)/shard_map/ppermute | solution.py:20
  933.5 23.8 %collective-permute-start.15 = (bf16[2,8,48,128]{3,2,1,0:T(8,128)(2,1)}, bf16[2,8,48,128]{3,2,1,0:T(8,128)(2,1)}, u32[]{:S(2)}, u32[]{:S(2)}) collective-permute-start(bf16[2,8,48,128]{3,2,1,0:T(8,128)(2,1)} %select_convert_fusion.9), channel_id=1, source_target_pairs={{0,2},{2,0},{4,6},{6,4},{8,10},{10,8},{12,14},{14,12},{16,18},{18,... | collective-permute-start | bytes 589832 | tf_op jit(solution)/shard_map/ppermute | solution.py:20
  956.7 14.0 collective-permute-start.19
  996.6 415.4 %all-reduce.5.cloned.1.call-start = ((), (), s32[]{:S(2)}) async-start(), calls=%async_computation.12 | async-start | bytes 28311552 | tf_op jit(solution)/shard_map/psum | solution.py:287
  (177 other events, 1469.7 us)
Sparse Core Ops, SparseCore 0:
  13.5 12.5 all-gather.4
  362.2 7.4 reduce-scatter.4
  373.1 11.0 all-gather.6
  385.6 10.9 all-gather.8
  421.3 10.2 reduce-scatter.8
  433.6 10.2 reduce-scatter.6
  448.4 11.0 all-gather.10
  996.7 7.1 reduce-scatter.10
  1015.2 396.7 all-reduce.4
where the time goes:
time: 1440 us; the launch traced here: 1430 us
  matrix products  435 us (30%)
  waiting for transfers between devices  344 us (24%)
  local copies, waits for them, and re-layouts  315 us (22%)
  other arithmetic  216 us (15%)
  blocking collectives  82.4 us (6%)
  starting transfers between devices  25.5 us (2%)
  between operations  16.2 us (1%)
    psum x1, waiting for transfers between devices, local(): lax.psum((grad_in, grad_out, grad_up, grad_down, grad_gain_one, grad_shif...  306 us
    broadcast_in_dim x65, local copies, waits for them, and re-layouts, place_cols(): spread = jnp.where(chosen, values[..., None], filler)  139 us
    dot_general x5, matrix products, seg_backward(): jnp.einsum('hqk,heq->hek', grad_s, q_blk, preferred_element_type=jnp.floa...  127 us
    dot_general x5, matrix products, seg_backward(): jnp.einsum('hqk,hek->heq', grad_s, k_blk, preferred_element_type=jnp.floa...  125 us
    psum x1, blocking collectives, local(): lax.psum((grad_in, grad_out, grad_up, grad_down, grad_gain_one, grad_shif...  78.5 us
    reduce_sum x20, other arithmetic, pick_cols(): jnp.sum(jnp.where(chosen, blocked, jnp.zeros((), values.dtype)), axis=-1)  55.6 us
    dot_general x5, matrix products, seg_backward(): jnp.einsum('hqk,heq->hek', prob_rows.astype(jnp.bfloat16), go_blk, prefer...  35.3 us
    unnamed x366, local copies, waits for them, and re-layouts  33.4 us
  transfers between devices with their start and end apart: 29, of which 6 were waited for; matrix products, arithmetic and copies ran while one was open for 33% of the time, Pallas kernels for 0%

commit v1 on v0

v1 whole, which is shorter than its diff:
```python
import math
from functools import partial

import jax
import jax.numpy as jnp
from jax import lax
from jax.experimental import pallas as pl
from jax.experimental.pallas import tpu as pltpu
from jax.sharding import PartitionSpec as P

E = 48
BRANCHES = 5
SEG0 = 1024
SLOTS = 16
BIT_ROWS = 16
DOC_BITS = 6
ROWS_IN = 3 * E + BIT_ROWS
ROWS_OUT = E + BIT_ROWS
EPS = 1e-05
FAR = 1e30
LOG2E = math.log2(math.e)
LN2 = math.log(2.0)
BF = jnp.bfloat16
F32 = jnp.float32
VMEM_LIMIT = 48 * 2**20


def params(**more):
    return pltpu.CompilerParams(vmem_limit_bytes=VMEM_LIMIT, **more)


def norm_rows(values, gain, shift):
    centre = jnp.mean(values, axis=-1, keepdims=True)
    centred = values - centre
    spread = jnp.mean(centred * centred, axis=-1, keepdims=True)
    return centred * lax.rsqrt(spread + EPS) * gain + shift


def reversed_bits(value, count):
    out = jnp.zeros_like(value)
    for bit in range(count):
        out = out * 2 + value // 2**bit % 2
    return out


def bit_reversed(value, count):
    return int(format(value, f"0{count}b")[::-1], 2)


def branch_shape(branch, heads):
    stride = 2**branch
    return (stride, SEG0 // stride, max(1, heads // stride), max(1, stride // heads))


def pieces_of(value):
    high = value.astype(BF).astype(F32)
    rest = value - high
    middle = rest.astype(BF).astype(F32)
    return high, middle, (rest - middle).astype(BF).astype(F32)


def row_block(placed, columns):
    ids = lax.broadcasted_iota(jnp.int32, (BIT_ROWS, columns), 0)
    block = jnp.zeros((BIT_ROWS, columns), F32)
    for row, value in placed.items():
        block = jnp.where(ids == row, value, block)
    return block


def lane_block(ref, lead, rows, start, count):
    if count >= 128:
        return ref[lead + (rows, pl.ds(pl.multiple_of(start * count, 128), count))]
    per = 128 // count
    wide = ref[lead + (rows, pl.ds(pl.multiple_of(start // per * 128, 128), 128))].astype(F32)
    out = wide[:, :count]
    for part in range(1, per):
        out = jnp.where(start % per == part, wide[:, part * count : (part + 1) * count], out)
    return out.astype(ref.dtype)


def pack_kernel(heads, starts, proj, bits, own, *sends):
    head = pl.program_id(0)
    for j in range(3):
        own[0, 0, j * E : (j + 1) * E, :] = proj[j]
    own[0, 0, 3 * E :, :] = bits[...]
    for branch in range(1, BRANCHES):
        send = sends[branch - 1]
        count = send.shape[-1]
        block = lane_block(own, (0, 0), slice(None), starts[branch, head], count)
        for copy in range(send.shape[0]):
            send[copy, 0] = block


def pack_heads(heads, starts, proj, bits):
    span = proj.shape[-1]
    outs = [jax.ShapeDtypeStruct((1, heads, ROWS_IN, span), BF)]
    specs = [pl.BlockSpec((1, 1, ROWS_IN, span), lambda h, s: (0, h, 0, 0))]
    for branch in range(1, BRANCHES):
        stride, count, per, split = branch_shape(branch, heads)
        outs.append(jax.ShapeDtypeStruct((stride, per, ROWS_IN, count), BF))
        specs.append(
            pl.BlockSpec((split, 1, ROWS_IN, count), lambda h, s, per=per: (h // per, h % per, 0, 0))
        )
    return pl.pallas_call(
        partial(pack_kernel, heads),
        grid_spec=pltpu.PrefetchScalarGridSpec(
            num_scalar_prefetch=1,
            grid=(heads,),
            in_specs=[
                pl.BlockSpec((3, E, span), lambda h, s: (0, h, 0)),
                pl.BlockSpec((BIT_ROWS, span), lambda h, s: (0, 0)),
            ],
            out_specs=specs,
        ),
        out_shape=outs,
        compiler_params=params(),
        name="pack_heads",
    )(starts, proj, bits)


def joined(ref, low, high):
    if ref.shape[0] == 1:
        return ref[0, 0, low:high, :]
    return jnp.concatenate([ref[m, 0, low:high, :] for m in range(ref.shape[0])], axis=1)


def split_out(ref, rows, value, column, count):
    width = ref.shape[-1]
    if ref.shape[0] == 1:
        ref[0, 0, rows, pl.ds(column, count)] = value
        return
    size = min(width, count)
    for start in range(column, column + count, size):
        lanes = slice(start % width, start % width + size)
        ref[start // width, 0, rows, lanes] = value[:, start - column : start - column + size]


def query_side(part, x, queries, split):
    bits = joined(x, 3 * E, ROWS_IN)
    if split == 1:
        return joined(x, 0, E), bits, bits
    lanes = pl.ds(pl.multiple_of(part[0] * queries, 128), queries)
    return x[0, 0, 0:E, lanes], x[0, 0, 3 * E : ROWS_IN, lanes], bits


def forward_kernel(queries, split, tile, part, x, out, q_aug):
    q, q_bits, bits = query_side(part, x, queries, split)
    q_aug[0:E, :] = q
    q_aug[E:, :] = (q_bits.astype(F32) * -FAR).astype(BF)
    k_bits = (1.0 - bits.astype(F32)).astype(BF)
    k_rows = jnp.concatenate([joined(x, E, 2 * E), k_bits], axis=0).T
    v_aug = jnp.concatenate([joined(x, 2 * E, 3 * E), jnp.ones_like(bits)], axis=0)
    base = 0
    if split > 1:
        base = pl.multiple_of(part[0] * queries, 128)
        out[0, 0, 0:E, :] = jnp.zeros((E, out.shape[-1]), BF)
        out[0, 0, E:, :] = row_block({0: -FAR}, out.shape[-1]).astype(BF)
    for step in range(queries // tile):
        column = step * tile
        s = jnp.dot(k_rows, q_aug[:, column : column + tile], preferred_element_type=F32)
        top = jnp.max(s, axis=0, keepdims=True)
        p = jnp.exp2(s - top).astype(BF)
        o = jnp.dot(v_aug, p, preferred_element_type=F32)
        total = o[E : E + 1]
        lse = top + jnp.log2(total)
        high, middle, low = pieces_of(lse)
        split_out(out, slice(0, E), (o[:E] * (1.0 / total)).astype(BF), base + column, tile)
        block = row_block({0: high, 1: middle, 2: low}, tile).astype(BF)
        split_out(out, slice(E, None), block, base + column, tile)


def backward_kernel(queries, split, tile, part, x, g, out, q_aug, g_aug, gk, gv):
    q, q_bits, bits = query_side(part, x, queries, split)
    if split == 1:
        g_aug[...] = joined(g, 0, ROWS_OUT)
    else:
        g_aug[...] = g[0, 0, :, pl.ds(pl.multiple_of(part[0] * queries, 128), queries)]
    extra = g_aug[E:, :].astype(F32)
    ids = lax.broadcasted_iota(jnp.int32, extra.shape, 0)
    q_aug[0:E, :] = q
    q_aug[E:, :] = jnp.where(ids >= 12, extra, q_bits.astype(F32) * -FAR).astype(BF)
    k_bits = (1.0 - bits.astype(F32)).astype(BF)
    k_aug = jnp.concatenate([joined(x, E, 2 * E), k_bits], axis=0)
    k_rows = k_aug.T
    v_ids = lax.broadcasted_iota(jnp.int32, bits.shape, 0)
    v_bits = jnp.where(v_ids < 3, 1.0, 0.0).astype(BF)
    v_rows = jnp.concatenate([joined(x, 2 * E, 3 * E), v_bits], axis=0).T
    q_rows = jnp.concatenate([q, jnp.zeros((BIT_ROWS, queries), BF)], axis=0).T
    g_rows = g_aug[...].T
    base = 0
    if split > 1:
        base = pl.multiple_of(part[0] * queries, 128)
        out[0, 0, 0:E, :] = jnp.zeros((E, out.shape[-1]), BF)
    for step in range(queries // tile):
        column = step * tile
        span = slice(column, column + tile)
        p = jnp.exp2(jnp.dot(k_rows, q_aug[:, span], preferred_element_type=F32))
        gs = p * jnp.dot(v_rows, g_aug[:, span], preferred_element_type=F32)
        p, gs = p.astype(BF), gs.astype(BF)
        gq = jnp.dot(k_aug, gs, preferred_element_type=F32)[:E]
        split_out(out, slice(0, E), gq.astype(BF), base + column, tile)
        new_k = jnp.dot(gs, q_rows[span], preferred_element_type=F32)
        new_v = jnp.dot(p, g_rows[span], preferred_element_type=F32)
        if step == 0:
            gk[...] = new_k
            gv[...] = new_v
        else:
            gk[...] += new_k
            gv[...] += new_v
    width = out.shape[-1]
    k_cols = (gk[...].T[:E] * LN2).astype(BF)
    v_cols = gv[...].T[:E].astype(BF)
    split_out(out, slice(E, 2 * E), k_cols, 0, k_cols.shape[1])
    split_out(out, slice(2 * E, 3 * E), v_cols, 0, k_cols.shape[1])


def unit_spec(array):
    members, _, rows, width = array.shape
    return pl.BlockSpec((members, 1, rows, width), lambda u, p: (0, u, 0, 0))


def unit_cost(units, keys, queries, dots):
    return pl.CostEstimate(
        flops=dots * 2 * units * keys * queries * 256,
        transcendentals=units * keys * queries,
        bytes_accessed=units * keys * 1000,
    )


def attend_forward(part, x, split):
    members, units, _, width = x.shape
    keys = members * width
    queries = keys // split
    out = jax.ShapeDtypeStruct((members, units, ROWS_OUT, width), BF)
    return pl.pallas_call(
        partial(forward_kernel, queries, split, min(256, queries)),
        grid_spec=pltpu.PrefetchScalarGridSpec(
            num_scalar_prefetch=1,
            grid=(units,),
            in_specs=[unit_spec(x)],
            out_specs=unit_spec(out),
            scratch_shapes=[pltpu.VMEM((ROWS_OUT, queries), BF)],
        ),
        out_shape=out,
        compiler_params=params(),
        cost_estimate=unit_cost(units, keys, queries, 2),
        name="attend_forward",
    )(part, x)


def attend_backward(part, x, g, split):
    members, units, _, width = x.shape
    keys = members * width
    queries = keys // split
    out = jax.ShapeDtypeStruct((members, units, 3 * E, width), BF)
    return pl.pallas_call(
        partial(backward_kernel, queries, split, min(256, queries)),
        grid_spec=pltpu.PrefetchScalarGridSpec(
            num_scalar_prefetch=1,
            grid=(units,),
            in_specs=[unit_spec(x), unit_spec(g)],
            out_specs=unit_spec(out),
            scratch_shapes=[
                pltpu.VMEM((ROWS_OUT, queries), BF),
                pltpu.VMEM((ROWS_OUT, queries), BF),
                pltpu.VMEM((keys, ROWS_OUT), F32),
                pltpu.VMEM((keys, ROWS_OUT), F32),
            ],
        ),
        out_shape=out,
        compiler_params=params(),
        cost_estimate=unit_cost(units, keys, queries, 5),
        name="attend_backward",
    )(part, x, g)


def spread_lanes(value, start, count):
    if count >= 128:
        return value, None
    per = 128 // count
    lanes = lax.broadcasted_iota(jnp.int32, (1, 128), 1)
    return jnp.concatenate([value] * per, axis=1), lanes // count == start % per


def aligned(start, count):
    if count >= 128:
        return pl.ds(pl.multiple_of(start * count, 128), count)
    return pl.ds(pl.multiple_of(start // (128 // count) * 128, 128), 128)


def merge_kernel(heads, starts, first, *refs):
    seconds, (mixed, merged, lse) = refs[: BRANCHES - 1], refs[BRANCHES - 1 :]
    head = pl.program_id(0)
    extra = first[0, 0, E:, :].astype(F32)
    merged[0] = first[0, 0, :E, :].astype(F32)
    lse[0] = extra[0:1] + extra[1:2] + extra[2:3]
    for branch in range(1, BRANCHES):
        got = seconds[branch - 1]
        count = got.shape[-1]
        start = starts[branch, head]
        lanes = aligned(start, count)
        for copy in range(got.shape[0]):
            value, mask = spread_lanes(got[copy, 0].astype(F32), start, count)
            new_lse = value[E : E + 1] + value[E + 1 : E + 2] + value[E + 2 : E + 3]
            if mask is not None:
                new_lse = jnp.where(mask, new_lse, -FAR)
            old_lse = lse[0, :, lanes]
            top = jnp.maximum(old_lse, new_lse)
            both = top + jnp.log2(jnp.exp2(old_lse - top) + jnp.exp2(new_lse - top))
            old_w = jnp.exp2(old_lse - both)
            new_w = jnp.exp2(new_lse - both)
            merged[0, :, lanes] = merged[0, :, lanes] * old_w + value[:E] * new_w
            lse[0, :, lanes] = both
    mixed[...] = merged[0].astype(BF)


def merge_heads(heads, starts, first, seconds):
    span = first.shape[-1]
    specs = [pl.BlockSpec((1, 1, ROWS_OUT, span), lambda h, s: (0, h, 0, 0))]
    for branch in range(1, BRANCHES):
        stride, count, per, split = branch_shape(branch, heads)
        specs.append(
            pl.BlockSpec((split, 1, ROWS_OUT, count), lambda h, s, per=per: (h // per, h % per, 0, 0))
        )
    return pl.pallas_call(
        partial(merge_kernel, heads),
        grid_spec=pltpu.PrefetchScalarGridSpec(
            num_scalar_prefetch=1,
            grid=(heads,),
            in_specs=specs,
            out_specs=[
                pl.BlockSpec((E, span), lambda h, s: (h, 0)),
                pl.BlockSpec((1, E, span), lambda h, s: (h, 0, 0)),
                pl.BlockSpec((1, 1, span), lambda h, s: (h, 0, 0)),
            ],
        ),
        out_shape=[
            jax.ShapeDtypeStruct((heads * E, span), BF),
            jax.ShapeDtypeStruct((heads, E, span), F32),
            jax.ShapeDtypeStruct((heads, 1, span), F32),
        ],
        compiler_params=params(),
        name="merge_heads",
    )(starts, first, *seconds)


def spread_kernel(heads, starts, grad, merged, lse, own, *sends):
    head = pl.program_id(0)
    low = grad[...].astype(BF)
    dots = jnp.sum(low.astype(F32) * merged[0], axis=0, keepdims=True)
    own[0, 0, :E, :] = low
    d = pieces_of(-dots)
    m = pieces_of(-lse[0])
    placed = {0: d[0], 1: d[1], 2: d[2], 12: m[0], 13: m[1], 14: m[2]}
    own[0, 0, E:, :] = row_block(placed, grad.shape[-1]).astype(BF)
    for branch in range(1, BRANCHES):
        send = sends[branch - 1]
        count = send.shape[-1]
        block = lane_block(own, (0, 0), slice(None), starts[branch, head], count)
        for copy in range(send.shape[0]):
            send[copy, 0] = block


def spread_heads(heads, starts, grad, merged, lse):
    span = grad.shape[-1]
    outs = [jax.ShapeDtypeStruct((1, heads, ROWS_OUT, span), BF)]
    specs = [pl.BlockSpec((1, 1, ROWS_OUT, span), lambda h, s: (0, h, 0, 0))]
    for branch in range(1, BRANCHES):
        stride, count, per, split = branch_shape(branch, heads)
        outs.append(jax.ShapeDtypeStruct((stride, per, ROWS_OUT, count), BF))
        specs.append(
            pl.BlockSpec((split, 1, ROWS_OUT, count), lambda h, s, per=per: (h // per, h % per, 0, 0))
        )
    return pl.pallas_call(
        partial(spread_kernel, heads),
        grid_spec=pltpu.PrefetchScalarGridSpec(
            num_scalar_prefetch=1,
            grid=(heads,),
            in_specs=[
                pl.BlockSpec((E, span), lambda h, s: (h, 0)),
                pl.BlockSpec((1, E, span), lambda h, s: (h, 0, 0)),
                pl.BlockSpec((1, 1, span), lambda h, s: (h, 0, 0)),
            ],
            out_specs=specs,
        ),
        out_shape=outs,
        compiler_params=params(),
        name="spread_heads",
    )(starts, grad, merged, lse)


def gather_kernel(heads, starts, first, *refs):
    seconds, (out, total) = refs[: BRANCHES - 1], refs[BRANCHES - 1 :]
    head = pl.program_id(0)
    total[...] = first[0, 0].astype(F32)
    for branch in range(1, BRANCHES):
        got = seconds[branch - 1]
        count = got.shape[-1]
        start = starts[branch, head]
        lanes = aligned(start, count)
        value = got[0, 0].astype(F32)
        for copy in range(1, got.shape[0]):
            value += got[copy, 0].astype(F32)
        value, mask = spread_lanes(value, start, count)
        if mask is not None:
            value = jnp.where(mask, value, 0.0)
        total[:, lanes] += value
    out[0] = (total[0:E, :] * E ** (-0.5)).astype(BF)
    out[1] = total[E : 2 * E, :].astype(BF)
    out[2] = total[2 * E :, :].astype(BF)


def gather_heads(heads, starts, first, seconds):
    span = first.shape[-1]
    specs = [pl.BlockSpec((1, 1, 3 * E, span), lambda h, s: (0, h, 0, 0))]
    for branch in range(1, BRANCHES):
        stride, count, per, split = branch_shape(branch, heads)
        specs.append(
            pl.BlockSpec((split, 1, 3 * E, count), lambda h, s, per=per: (h // per, h % per, 0, 0))
        )
    return pl.pallas_call(
        partial(gather_kernel, heads),
        grid_spec=pltpu.PrefetchScalarGridSpec(
            num_scalar_prefetch=1,
            grid=(heads,),
            in_specs=specs,
            out_specs=pl.BlockSpec((3, E, span), lambda h, s: (0, h, 0)),
            scratch_shapes=[pltpu.VMEM((3 * E, span), F32)],
        ),
        out_shape=jax.ShapeDtypeStruct((3, heads * E, span), BF),
        compiler_params=params(),
        name="gather_heads",
    )(starts, first, *seconds)


def exchange(value, branch):
    size = lax.axis_size("seq")
    stride = 2**branch
    groups = None
    if stride != size:
        groups = [[g * stride + i for i in range(stride)] for g in range(size // stride)]
    return lax.all_to_all(value, "seq", 0, 0, axis_index_groups=groups, tiled=True)


def to_unit(value, whole):
    if not whole:
        return value
    members, units, rows, width = value.shape
    return value.transpose(1, 2, 0, 3).reshape(1, units, rows, members * width)


def from_unit(value, members, whole):
    if not whole:
        return value
    _, units, rows, width = value.shape
    return value.reshape(units, rows, members, width // members).transpose(2, 0, 1, 3)


def rolled(value, step):
    size = lax.axis_size("head")
    return lax.ppermute(value, "head", [(s, (s + step) % size) for s in range(size)])


def all_rows(own):
    size = lax.axis_size("head")
    me = lax.axis_index("head")
    got = [own] + [rolled(own, step) for step in range(1, size)]
    if size == 2:
        return [jnp.where(me == 0, got[0], got[1]), jnp.where(me == 0, got[1], got[0])]
    stacked = jnp.stack(got)
    return [stacked[(me - place) % size] for place in range(size)]


def sum_rows(parts):
    size = lax.axis_size("head")
    me = lax.axis_index("head")
    total = lax.dynamic_index_in_dim(parts, me, 0, keepdims=False).astype(F32)
    for step in range(1, size):
        sent = lax.dynamic_index_in_dim(parts, (me + step) % size, 0, keepdims=False)
        total = total + rolled(sent, step).astype(F32)
    return total


def sum_seq(value):
    size = lax.axis_size("seq")
    got = lax.all_to_all(value.astype(BF), "seq", 0, 0, tiled=True)
    mine = got.reshape((size, value.shape[0] // size) + value.shape[1:]).astype(F32).sum(0)
    full = jnp.broadcast_to(mine.astype(BF)[None], (size,) + mine.shape)
    return lax.all_to_all(full, "seq", 0, 0, tiled=True).reshape(value.shape).astype(F32)


def local(
    tokens,
    documents,
    offsets,
    in_proj,
    out_proj,
    up_proj,
    down_proj,
    first_gain,
    first_shift,
    second_gain,
    second_shift,
    cotangent,
):
    head_count = lax.axis_size("head")
    seq_id = lax.axis_index("seq")
    row_count, width = tokens.shape
    seq_len = row_count * head_count
    heads = offsets.shape[1]
    per_slot = row_count // SLOTS
    gelu_exact = partial(jax.nn.gelu, approximate=False)

    ids = lax.broadcasted_iota(jnp.int32, (row_count, row_count), 0)
    slot = reversed_bits(ids // per_slot, 4)
    source = ids % per_slot * SLOTS + slot
    order = (source == lax.broadcasted_iota(jnp.int32, (row_count, row_count), 1)).astype(BF)

    def sorted_rows(values):
        return jnp.dot(order, values, preferred_element_type=F32)

    def shard_rows(own):
        parts = [part.reshape(SLOTS, per_slot, -1) for part in all_rows(own)]
        return jnp.stack(parts, axis=1).reshape(seq_len, -1)

    def device_parts(values):
        split = values.reshape(SLOTS, head_count, per_slot, -1)
        return jnp.moveaxis(split, 1, 0).reshape(head_count, row_count, -1)

    x_rows = sorted_rows(tokens)
    cot_low = sorted_rows(cotangent).astype(BF)
    normed_one = norm_rows(x_rows, first_gain, first_shift)
    gathered_one = shard_rows(normed_one.astype(BF))
    cot_all = shard_rows(cot_low)

    my_docs = lax.dynamic_slice_in_dim(documents, seq_id * seq_len, seq_len)
    my_docs = my_docs.reshape(head_count, per_slot, 2, 2, 2, 2).transpose(5, 4, 3, 2, 0, 1).reshape(seq_len)
    bit_ids = jnp.arange(BIT_ROWS, dtype=jnp.int32)[:, None]
    doc_bit = my_docs[None, :] // 2 ** (bit_ids % DOC_BITS) % 2
    bits = jnp.where(bit_ids < DOC_BITS, doc_bit, jnp.where(bit_ids < 2 * DOC_BITS, 1 - doc_bit, 0))
    bits = bits.astype(BF)
    starts = jnp.stack([reversed_bits(offsets[b], b) for b in range(BRANCHES)])

    scales = jnp.array([E ** (-0.5) * LOG2E, 1.0, 1.0], F32)[:, None, None]
    projected = jnp.einsum("td,jdc->jct", gathered_one, in_proj, preferred_element_type=F32)
    projected = (projected * scales).astype(BF)
    own, *sends = pack_heads(heads, starts, projected, bits)

    shapes = [branch_shape(b, heads) for b in range(BRANCHES)]
    whole = [s[3] > 1 or s[1] < 128 for s in shapes]
    places = [(seq_id % s[0] % s[3]).astype(jnp.int32).reshape(1) for s in shapes]

    received = [None] + [exchange(sends[b - 1], b) for b in range(1, BRANCHES)]
    first_out = attend_forward(places[0], own, 1)
    units = [own]
    outs = []
    for b in range(1, BRANCHES):
        unit = to_unit(received[b], whole[b])
        units.append(unit)
        result = attend_forward(places[b], unit, shapes[b][3])
        outs.append(exchange(from_unit(result, shapes[b][0], whole[b]), b))
    mixed, merged, lse = merge_heads(heads, starts, first_out, outs)

    attn_part = jnp.einsum("ct,cd->td", mixed, out_proj, preferred_element_type=F32).astype(BF)
    hidden_one = x_rows + sum_rows(device_parts(attn_part))
    normed_two = norm_rows(hidden_one, second_gain, second_shift)
    gathered_two = shard_rows(normed_two.astype(BF))
    pre_act = jnp.dot(gathered_two, up_proj, preferred_element_type=F32)
    hidden, gelu_pull = jax.vjp(gelu_exact, pre_act)
    hidden = hidden.astype(BF)
    down_part = jnp.dot(hidden, down_proj, preferred_element_type=F32).astype(BF)
    block_rows = hidden_one + sum_rows(device_parts(down_part))
    block_out = jnp.dot(order.T, block_rows.astype(BF), preferred_element_type=F32).astype(BF)

    grad_down = jnp.einsum("tf,td->fd", hidden, cot_all, preferred_element_type=F32).astype(BF)
    grad_act = jnp.einsum("td,fd->tf", cot_all, down_proj, preferred_element_type=F32)
    grad_pre = gelu_pull(grad_act)[0].astype(BF)
    grad_up = jnp.einsum("td,tf->df", gathered_two, grad_pre, preferred_element_type=F32).astype(BF)
    norm_part = jnp.einsum("tf,df->td", grad_pre, up_proj, preferred_element_type=F32).astype(BF)
    grad_normed_two = sum_rows(device_parts(norm_part))
    pull_two = jax.vjp(norm_rows, hidden_one, second_gain, second_shift)[1]
    grad_ln_two, grad_gain_two, grad_shift_two = pull_two(grad_normed_two)
    grad_hidden_one = cot_low.astype(F32) + grad_ln_two
    grad_attn = shard_rows(grad_hidden_one.astype(BF))
    grad_out = jnp.einsum("ct,td->cd", mixed, grad_attn, preferred_element_type=F32).astype(BF)
    grad_merged = jnp.einsum("td,cd->ct", grad_attn, out_proj, preferred_element_type=F32)

    own_g, *sends_g = spread_heads(heads, starts, grad_merged, merged, lse)
    received_g = [None] + [exchange(sends_g[b - 1], b) for b in range(1, BRANCHES)]
    first_grad = attend_backward(places[0], own, own_g, 1)
    grads = []
    for b in range(1, BRANCHES):
        unit_g = to_unit(received_g[b], whole[b])
        result = attend_backward(places[b], units[b], unit_g, shapes[b][3])
        grads.append(exchange(from_unit(result, shapes[b][0], whole[b]), b))
    grad_qkv = gather_heads(heads, starts, first_grad, grads)

    grad_in = jnp.einsum("td,jct->jdc", gathered_one, grad_qkv, preferred_element_type=F32)
    one_part = jnp.einsum("jct,jdc->td", grad_qkv, in_proj, preferred_element_type=F32).astype(BF)
    grad_normed_one = sum_rows(device_parts(one_part))
    pull_one = jax.vjp(norm_rows, x_rows, first_gain, first_shift)[1]
    grad_ln_one, grad_gain_one, grad_shift_one = pull_one(grad_normed_one)
    grad_tokens = jnp.dot(
        order.T.astype(F32),
        grad_hidden_one + grad_ln_one,
        precision=lax.Precision.HIGHEST,
        preferred_element_type=F32,
    )

    middle = lax.psum((grad_out, grad_up, grad_down), "seq")
    flat_in = grad_in.reshape(3 * width, heads * E)
    grad_in = sum_seq(flat_in).reshape(3, width, heads * E)
    gains = jnp.stack([grad_gain_one, grad_shift_one, grad_gain_two, grad_shift_two])
    gains = lax.psum(gains, ("seq", "head"))
    return (
        block_out,
        grad_tokens,
        grad_in,
        middle[0].astype(F32),
        middle[1].astype(F32),
        middle[2].astype(F32),
        gains[0],
        gains[1],
        gains[2],
        gains[3],
    )


def solution(mesh):
    placed = (
        P(("seq", "head"), None),
        P(),
        P(None, "head"),
        P(None, None, "head"),
        P("head", None),
        P(None, "head"),
        P("head", None),
        P(),
        P(),
        P(),
        P(),
        P(("seq", "head"), None),
    )
    return jax.shard_map(
        local,
        mesh=mesh,
        in_specs=placed,
        out_specs=(
            P(("seq", "head"), None),
            P(("seq", "head"), None),
            P(None, None, "head"),
            P("head", None),
            P(None, "head"),
            P("head", None),
            P(),
            P(),
            P(),
            P(),
        ),
        check_vma=False,
    )
```

time: 1440 us -> 649 us (0.45)
  matrix products: 435 us -> 64.3 us
  local copies, waits for them, and re-layouts: 315 us -> 61.6 us
  waiting for transfers between devices: 344 us -> 147 us
  other arithmetic: 216 us -> 35.8 us
  Pallas kernels: 0 us -> 114 us
  starting transfers between devices: 25.5 us -> 82.4 us
  blocking collectives: 82.4 us -> 118 us
    dot_general x41 -> x15, matrix products: 431 us -> 61.1 us  [the longest x1 18.3 us: local(): jnp.einsum('td,fd->tf', cot_all, down_proj, preferred_element_type=F32)]
    psum x1, waiting for transfers between devices: 306 us -> 94.3 us  [local(): middle = lax.psum((grad_out, grad_up, grad_down), 'seq')]
    broadcast_in_dim x81 -> x1, local copies, waits for them, and re-layouts: 153 us -> 1.36 us  [sum_seq(): full = jnp.broadcast_to(mine.astype(BF)[None], (size,) + mine.shape)]
    pallas_call x0 -> x14, Pallas kernels: none -> 114 us  [the longest x5 51 us: attend_backward(): pl.pallas_call(partial(backward_kernel, queries, split, min(256, queries)...]
    reduce_sum x27 -> x1, other arithmetic: 84.7 us -> 1.74 us  [sum_seq(): got.reshape((size, value.shape[0] // size) + value.shape[1:]).astype(F32)]
    all_to_all x0 -> x14, starting transfers between devices: none -> 80.7 us  [the longest x12 50.6 us: exchange(): lax.all_to_all(value, 'seq', 0, 0, axis_index_groups=groups, tiled=True)]
    all_to_all x0 -> x4, blocking collectives: none -> 55.6 us  [exchange(): lax.all_to_all(value, 'seq', 0, 0, axis_index_groups=groups, tiled=True)]
    convert_element_type x15 -> x1, local copies, waits for them, and re-layouts: 57.7 us -> 3.84 us  [sum_seq(): got = lax.all_to_all(value.astype(BF), 'seq', 0, 0, tiled=True)]
  transfers between devices with their start and end apart: 29 -> 23, of which waited for: 6 -> 11; matrix products, arithmetic and copies ran while one was open for 33% -> 12% of each run, Pallas kernels for 0% -> 15%
where the time goes in v1:
time: 649 us; the launch traced here: 639 us
  waiting for transfers between devices  147 us (23%)
  blocking collectives  118 us (18%)
  Pallas kernels  114 us (18%)
  starting transfers between devices  82.4 us (13%)
  matrix products  64.3 us (10%)
  local copies, waits for them, and re-layouts  61.6 us (9%)
  other arithmetic  35.8 us (6%)
  between operations  15.7 us (2%)
    psum x1, waiting for transfers between devices, local(): middle = lax.psum((grad_out, grad_up, grad_down), 'seq')  94.3 us
    psum x1, blocking collectives, local(): gains = lax.psum(gains, ('seq', 'head'))  62.6 us
    all_to_all x4, blocking collectives, exchange(): lax.all_to_all(value, 'seq', 0, 0, axis_index_groups=groups, tiled=True)  55.6 us
    pallas_call x5, Pallas kernels, attend_backward(): pl.pallas_call(partial(backward_kernel, queries, split, min(256, queries)...  51 us
    all_to_all x12, starting transfers between devices, exchange(): lax.all_to_all(value, 'seq', 0, 0, axis_index_groups=groups, tiled=True)  50.6 us
    pallas_call x5, Pallas kernels, attend_forward(): pl.pallas_call(partial(forward_kernel, queries, split, min(256, queries))...  47 us
    unnamed x196, local copies, waits for them, and re-layouts  41.4 us
    all_to_all x1, waiting for transfers between devices, sum_seq(): got = lax.all_to_all(value.astype(BF), 'seq', 0, 0, tiled=True)  28.8 us
  transfers between devices with their start and end apart: 23, of which 11 were waited for; matrix products, arithmetic and copies ran while one was open for 12% of the time, Pallas kernels for 15%

profile of v1, /device:TPU:0, one launch (start us, length us, event | category | flops | bytes accessed | tf_op | source)
XLA Modules:
  0.0 638.7 jit_solution(11155921136361482678)
XLA Ops:
  21.6 4.1 pack_heads.1
  27.6 15.1 %all_to_all.91.x = bf16[4,2,160,256]{3,2,1,0:T(8,128)(2,1)S(1)} all-to-all(bf16[4,2,160,256]{3,2,1,0:T(8,128)(2,1)S(1)} %get-tuple-element.25), channel_id=1, replica_groups={{0,2,4,6},{8,10,12,14},{16,18,20,22},{24,26,28,30},{1,3,5,7},{9,11,13,1..., dimensions={0} | all-to-all | bytes 1310720 | tf_op jit(solution)/shard_map/all_to_all | solution.py:442
  48.4 4.6 all-to-all-done.4.x
  53.0 18.1 %all_to_all.92 = bf16[16,1,160,64]{2,3,1,0:T(8,128)(2,1)} all-to-all(bf16[16,1,160,64]{2,3,1,0:T(8,128)(2,1)} %copy.56), channel_id=1, replica_groups=mesh['seq'=16,'head'=2] {'seq'}, dimensions={0} | all-to-all | bytes 655360 | tf_op jit(solution)/shard_map/all_to_all | solution.py:442
  71.1 4.6 all-to-all-start
  75.7 5.9 attend_forward.7
  82.3 5.5 all-to-all-done.x
  96.7 5.3 all-to-all-start.5
  108.1 6.6 %all-to-all-start.7 = ((bf16[16,2,2048]{2,1,0:T(2,128)(2,1)}), bf16[16,2,2048]{2,1,0:T(2,128)(2,1)S(1)}, u32[]{:S(2)}, u32[]{:S(2)}) async-start(bf16[16,2,2048]{2,1,0:T(2,128)(2,1)} %reshape.295), calls=%async_computation.7 | async-start | bytes 262144 | tf_op jit(solution)/shard_map/all_to_all | solution.py:442
  114.7 12.7 %attend_forward.6 = bf16[2,4,64,512]{3,2,1,0:T(8,128)(2,1)S(1)} custom-call(s32[1]{0:T(128)} %constant.420.clone.1.part, bf16[2,4,160,512]{3,2,1,0:T(8,128)(2,1)} %all-to-all-done.x), custom_call_target="tpu_custom_call" | custom-call | flops 4294967296 | bytes 4096000 | tf_op jit(solution)/shard_map/attend_forward/pallas_call | solution.py:235
  134.3 23.3 %attend_forward.5.first = bf16[1,8,64,1024]{3,2,1,0:T(8,128)(2,1)S(1)} custom-call(s32[1]{0:T(128)} %constant.420.clone.1.part, bf16[1,8,160,1024]{3,2,1,0:T(8,128)(2,1)S(1)} %copy-done.33), custom_call_target="tpu_custom_call" | custom-call | flops 8589934592 | bytes 8192000 | tf_op jit(solution)/shard_map/attend_forward/pallas_call | solution.py:235
  179.8 18.3 %add_convert_fusion = (bf16[1024,1536]{1,0:T(8,128)(2,1)S(1)}, f32[1024,1536]{1,0:T(8,128)}) fusion(f32[1024,1536]{1,0:T(8,128)S(1)} %fusion.82, bf16[1024,768]{1,0:T(8,128)(2,1)S(1)} %bitcast.150, bf16[1536,768]{1,0:T(8,128)(2,1)S(1)} %copy-done), kind=kOutput, calls=%fused_computation.2 | convolution fusion | flops 2529165312 | bytes 19660800 | tf_op jit(solution)/shard_map/td,fd->tf/dot_general | solution.py:576
  216.4 10.8 %all_to_all.93.g = bf16[4,2,64,256]{3,2,1,0:T(8,128)(2,1)} all-to-all(bf16[4,2,64,256]{3,2,1,0:T(8,128)(2,1)S(1)} %get-tuple-element.33), channel_id=1, replica_groups={{0,2,4,6},{8,10,12,14},{16,18,20,22},{24,26,28,30},{1,3,5,7},{9,11,13,1..., dimensions={0} | all-to-all | bytes 524288 | tf_op jit(solution)/shard_map/all_to_all | solution.py:442
  230.8 5.8 all-to-all-done.12.g
  236.6 11.6 %all_to_all.94 = bf16[16,2,2048]{2,1,0:T(2,128)(2,1)} all-to-all(bf16[16,2,2048]{2,1,0:T(2,128)(2,1)S(1)} %reshape.297), channel_id=1, replica_groups=mesh['seq'=16,'head'=2] {'seq'}, dimensions={0} | all-to-all | bytes 262144 | tf_op jit(solution)/shard_map/all_to_all | solution.py:442
  252.7 6.4 %attend_backward.7 = bf16[4,2,144,256]{3,2,1,0:T(8,128)(2,1)S(1)} custom-call(s32[1]{0:T(128)} %constant.420.clone.1.part, bf16[4,2,160,256]{3,2,1,0:T(8,128)(2,1)S(1)} %copy-done.15, bf16[4,2,64,256]{3,2,1,0:T(8,128)(2,1)S(1)} %copy-done.27), custom_call_target="tpu_custom_call" | custom-call | flops 5368709120 | bytes 2048000 | tf_op jit(solution)/shard_map/attend_backward/pallas_call | solution.py:256
  275.1 6.4 %convolution_convert_fusion.1 = bf16[768,1536]{1,0:T(8,128)(2,1)} fusion(bf16[1024,768]{1,0:T(8,128)(2,1)} %bitcast.155, bf16[1024,1536]{1,0:T(8,128)(2,1)} %copy-done.95), kind=kOutput, calls=%fused_computation.19 | convolution fusion | flops 2417098752 | bytes 7077888 | tf_op jit(solution)/shard_map/td,tf->df/dot_general | solution.py:578
  289.2 5.6 all-to-all-start.15
  294.8 13.7 %attend_backward.6 = bf16[2,4,144,512]{3,2,1,0:T(8,128)(2,1)S(1)} custom-call(s32[1]{0:T(128)} %constant.420.clone.1.part, bf16[2,4,160,512]{3,2,1,0:T(8,128)(2,1)} %all-to-all-done.x, bf16[2,4,64,512]{3,2,1,0:T(8,128)(2,1)S(1)} %copy-done.19), custom_call_target="tpu_custom_call" | custom-call | flops 10737418240 | bytes 4096000 | tf_op jit(solution)/shard_map/attend_backward/pallas_call | solution.py:256
  316.1 25.3 %attend_backward.5.first = bf16[1,8,144,1024]{3,2,1,0:T(8,128)(2,1)S(1)} custom-call(s32[1]{0:T(128)} %constant.420.clone.1.part, bf16[1,8,160,1024]{3,2,1,0:T(8,128)(2,1)S(1)} %copy-done.34, bf16[1,8,64,1024]{3,2,1,0:T(8,128)(2,1)S(1)} %copy-done.36), custom_call_target="tpu_custom_call" | custom-call | flops 21474836480 | bytes 8192000 | tf_op jit(solution)/shard_map/attend_backward/pallas_call | solution.py:256
  348.1 5.7 gather_heads.1
  362.3 7.4 %all-to-all-start.16 = ((bf16[16,144,384]{2,1,0:T(8,128)(2,1)}), bf16[16,144,384]{2,1,0:T(8,128)(2,1)}, u32[]{:S(2)}, u32[]{:S(2)}) async-start(bf16[16,144,384]{2,1,0:T(8,128)(2,1)} %bitcast.133), calls=%async_computation.16 | async-start | bytes 3538944 | tf_op jit(solution)/shard_map/all_to_all | solution.py:486
  369.8 6.3 multiply_convert_fusion
  376.1 4.0 convolution_convert_fusion
  381.8 4.5 convolution_convert_fusion.4
  388.5 28.8 %all-to-all-done.16 = bf16[16,144,384]{2,1,0:T(8,128)(2,1)} async-done(((bf16[16,144,384]{2,1,0:T(8,128)(2,1)}), bf16[16,144,384]{2,1,0:T(8,128)(2,1)}, u32[]{:S(2)}, u32[]{:S(2)}) %all-to-all-start.16) | async-done | bytes 1769504 | tf_op jit(solution)/shard_map/all_to_all | solution.py:486
  420.4 22.7 %all-to-all-start.17 = ((bf16[16,144,384]{2,1,0:T(8,128)(2,1)}), bf16[16,144,384]{2,1,0:T(8,128)(2,1)}, u32[]{:S(2)}, u32[]{:S(2)}) async-start(bf16[16,144,384]{2,1,0:T(8,128)(2,1)} %broadcast_in_dim.38), calls=%async_computation.17 | async-start | bytes 3538944 | tf_op jit(solution)/shard_map/all_to_all | solution.py:489
  443.1 4.4 bitcast_convert_fusion
  454.6 62.6 %psum.31 = f32[4,768]{1,0:T(4,128)S(1)} all-reduce(f32[4,768]{1,0:T(4,128)S(1)} %pad_maximum_fusion.4), channel_id=1, replica_groups=mesh['seq'=16,'head'=2] {'seq','head'}, use_global_device_ids=true, to_apply=%region_16.17 | all-reduce | flops 3072 | bytes 24576 | tf_op jit(solution)/shard_map/psum | solution.py:614
  520.4 4.0 fusion.10
  524.4 94.3 %all-reduce.3.cloned.1.call-done = (bf16[384,768]{1,0:T(8,128)(2,1)}, bf16[768,1536]{1,0:T(8,128)(2,1)}, bf16[1536,768]{1,0:T(8,128)(2,1)}) async-done(((bf16[384,768]{1,0:T(8,128)(2,1)}, bf16[768,1536]{1,0:T(8,128)(2,1)}, bf16[1536,768]{1,0:T(8,128)(2,1)}), (bf16[384,768]{1,0:T(8,128)(2,1)}, bf16[768,1536]{1,0:T(8,128)(2,1)}, bf16[1536,768]{1,0:T(8,128)(2,1)})) %all-reduce.3.cloned.1.call-update) | async-done | bytes 5308432 | tf_op jit(solution)/shard_map/psum | solution.py:610
  620.9 4.6 convert_element_type.158
  (318 shorter events, 163.9 us)
Async XLA Ops:
  7.2 172.6 %copy-start = (bf16[1536,768]{1,0:T(8,128)(2,1)S(1)}, bf16[1536,768]{1,0:T(8,128)(2,1)}, u32[]{:S(2)}) copy-start(bf16[1536,768]{1,0:T(8,128)(2,1)} %param.19) | copy-start | bytes 7077892
  7.2 158.2 %copy-start.73 = (s32[512]{0:T(512)}, s32[512]{0:T(512)S(1)}, u32[]{:S(2)}) copy-start(s32[512]{0:T(512)S(1)} %get-tuple-element.77) | copy-start | bytes 6148
  7.2 158.2 %copy-start.75 = (s32[512]{0:T(512)}, s32[512]{0:T(512)S(1)}, u32[]{:S(2)}) copy-start(s32[512]{0:T(512)S(1)} %get-tuple-element.78) | copy-start | bytes 6148
  7.3 158.2 %copy-start.77 = (s32[512]{0:T(512)}, s32[512]{0:T(512)S(1)}, u32[]{:S(2)}) copy-start(s32[512]{0:T(512)S(1)} %get-tuple-element.75) | copy-start | bytes 6148
  12.6 2.8 collective-permute-start
  42.8 10.3 %all-to-all-start.4 = ((bf16[8,1,160,128]{3,2,1,0:T(8,128)(2,1)}), bf16[8,1,160,128]{3,2,1,0:T(8,128)(2,1)S(1)}, u32[]{:S(2)}, u32[]{:S(2)}) async-start(bf16[8,1,160,128]{3,2,1,0:T(8,128)(2,1)} %copy-done.26), calls=%async_computation.4 | async-start | bytes 655360 | tf_op jit(solution)/shard_map/all_to_all | solution.py:442
  53.0 38.4 %copy-start.22 = (bf16[8,1,160,128]{3,2,1,0:T(8,128)(2,1)}, bf16[8,1,160,128]{3,2,1,0:T(8,128)(2,1)S(1)}, u32[]{:S(2)}) copy-start(bf16[8,1,160,128]{3,2,1,0:T(8,128)(2,1)S(1)} %all-to-all-done.4.x) | copy-start | bytes 983044
  71.1 16.7 %all-to-all-start = ((bf16[2,4,160,512]{3,2,1,0:T(8,128)(2,1)}), bf16[2,4,160,512]{3,2,1,0:T(8,128)(2,1)}, u32[]{:S(2)}, u32[]{:S(2)}) async-start(bf16[2,4,160,512]{3,2,1,0:T(8,128)(2,1)} %copy-done.8), calls=%async_computation | async-start | bytes 2621440 | tf_op jit(solution)/shard_map/all_to_all | solution.py:442
  87.8 8.9 %all-to-all-start.3 = ((bf16[4,2,64,256]{3,2,1,0:T(8,128)(2,1)}), bf16[4,2,64,256]{3,2,1,0:T(8,128)(2,1)S(1)}, u32[]{:S(2)}, u32[]{:S(2)}) async-start(bf16[4,2,64,256]{3,2,1,0:T(8,128)(2,1)} %copy-done.28), calls=%async_computation.3 | async-start | bytes 524288 | tf_op jit(solution)/shard_map/all_to_all | solution.py:442
  96.7 11.4 %all-to-all-start.5 = ((bf16[8,1,64,128]{3,2,1,0:T(8,128)(2,1)}), bf16[8,1,64,128]{3,2,1,0:T(8,128)(2,1)S(1)}, u32[]{:S(2)}, u32[]{:S(2)}) async-start(bf16[8,1,64,128]{3,2,1,0:T(8,128)(2,1)} %attend_forward.8), calls=%async_computation.5 | async-start | bytes 262144 | tf_op jit(solution)/shard_map/all_to_all | solution.py:442
  108.1 20.1 %all-to-all-start.7 = ((bf16[16,2,2048]{2,1,0:T(2,128)(2,1)}), bf16[16,2,2048]{2,1,0:T(2,128)(2,1)S(1)}, u32[]{:S(2)}, u32[]{:S(2)}) async-start(bf16[16,2,2048]{2,1,0:T(2,128)(2,1)} %reshape.295), calls=%async_computation.7 | async-start | bytes 262144 | tf_op jit(solution)/shard_map/all_to_all | solution.py:442
  128.8 30.8 %all-to-all-start.1 = ((bf16[2,4,64,512]{3,2,1,0:T(8,128)(2,1)}), bf16[2,4,64,512]{3,2,1,0:T(8,128)(2,1)S(1)}, u32[]{:S(2)}, u32[]{:S(2)}) async-start(bf16[2,4,64,512]{3,2,1,0:T(8,128)(2,1)} %copy-done.21), calls=%async_computation.1 | async-start | bytes 1048576 | tf_op jit(solution)/shard_map/all_to_all | solution.py:442
  165.4 3.2 collective-permute-start.1
  168.5 36.4 %copy-start.50 = (bf16[512,768]{1,0:T(8,128)(2,1)}, bf16[512,768]{1,0:T(8,128)(2,1)S(1)}, u32[]{:S(2)}) copy-start(bf16[512,768]{1,0:T(8,128)(2,1)S(1)} %convolution_convert_fusion.5) | copy-start | bytes 2359300
  168.5 3.9 collective-permute-start.4
  171.0 33.2 %copy-start.41 = (f32[512,768]{1,0:T(8,128)}, f32[512,768]{1,0:T(8,128)S(1)}, u32[]{:S(2)}) copy-start(f32[512,768]{1,0:T(8,128)S(1)} %get-tuple-element.56) | copy-start | bytes 4718596
  172.1 2.4 collective-permute-start.2
  201.0 2.4 collective-permute-start.5
  206.1 2.3 collective-permute-start.6
  216.4 35.3 %copy-start.15 = (bf16[4,2,160,256]{3,2,1,0:T(8,128)(2,1)S(1)}, bf16[4,2,160,256]{3,2,1,0:T(8,128)(2,1)}, u32[]{:S(2)}) copy-start(bf16[4,2,160,256]{3,2,1,0:T(8,128)(2,1)} %copy-done.14) | copy-start | bytes 1966084
  227.2 9.4 %all-to-all-start.12 = ((bf16[8,1,64,128]{3,2,1,0:T(8,128)(2,1)}), bf16[8,1,64,128]{3,2,1,0:T(8,128)(2,1)S(1)}, u32[]{:S(2)}, u32[]{:S(2)}) async-start(bf16[8,1,64,128]{3,2,1,0:T(8,128)(2,1)} %get-tuple-element.34), calls=%async_computation.12 | async-start | bytes 262144 | tf_op jit(solution)/shard_map/all_to_all | solution.py:442
  248.2 11.7 %all-to-all-start.8 = ((bf16[2,4,64,512]{3,2,1,0:T(8,128)(2,1)}), bf16[2,4,64,512]{3,2,1,0:T(8,128)(2,1)S(1)}, u32[]{:S(2)}, u32[]{:S(2)}) async-start(bf16[2,4,64,512]{3,2,1,0:T(8,128)(2,1)} %copy-done.20), calls=%async_computation.8 | async-start | bytes 1048576 | tf_op jit(solution)/shard_map/all_to_all | solution.py:442
  260.8 10.4 %all-to-all-start.11 = ((bf16[4,2,144,256]{3,2,1,0:T(8,128)(2,1)}), bf16[4,2,144,256]{3,2,1,0:T(8,128)(2,1)S(1)}, u32[]{:S(2)}, u32[]{:S(2)}) async-start(bf16[4,2,144,256]{3,2,1,0:T(8,128)(2,1)} %copy-done.17), calls=%async_computation.11 | async-start | bytes 1179648 | tf_op jit(solution)/shard_map/all_to_all | solution.py:442
  271.2 18.1 %all-to-all-start.13 = ((bf16[8,1,144,128]{3,2,1,0:T(8,128)(2,1)}), bf16[8,1,144,128]{3,2,1,0:T(8,128)(2,1)S(1)}, u32[]{:S(2)}, u32[]{:S(2)}) async-start(bf16[8,1,144,128]{3,2,1,0:T(8,128)(2,1)} %attend_backward.8), calls=%async_computation.13 | async-start | bytes 589824 | tf_op jit(solution)/shard_map/all_to_all | solution.py:442
  289.2 20.3 %all-to-all-start.15 = ((bf16[16,1,144,64]{2,3,1,0:T(8,128)(2,1)}), bf16[16,1,144,64]{2,3,1,0:T(8,128)(2,1)}, u32[]{:S(2)}, u32[]{:S(2)}) async-start(bf16[16,1,144,64]{2,3,1,0:T(8,128)(2,1)} %copy.70), calls=%async_computation.15 | async-start | bytes 1048576 | tf_op jit(solution)/shard_map/all_to_all | solution.py:442
  309.5 35.4 %all-to-all-start.9 = ((bf16[2,4,144,512]{3,2,1,0:T(8,128)(2,1)}), bf16[2,4,144,512]{3,2,1,0:T(8,128)(2,1)S(1)}, u32[]{:S(2)}, u32[]{:S(2)}) async-start(bf16[2,4,144,512]{3,2,1,0:T(8,128)(2,1)} %copy-done.11), calls=%async_computation.9 | async-start | bytes 2359296 | tf_op jit(solution)/shard_map/all_to_all | solution.py:442
  362.3 55.0 %all-to-all-start.16 = ((bf16[16,144,384]{2,1,0:T(8,128)(2,1)}), bf16[16,144,384]{2,1,0:T(8,128)(2,1)}, u32[]{:S(2)}, u32[]{:S(2)}) async-start(bf16[16,144,384]{2,1,0:T(8,128)(2,1)} %bitcast.133), calls=%async_computation.16 | async-start | bytes 3538944 | tf_op jit(solution)/shard_map/all_to_all | solution.py:486
  369.7 249.0 %all-reduce.3.cloned.1.call-start = ((), (), s32[]{:S(2)}) async-start(), calls=%async_computation.18 | async-start | bytes 10616832 | tf_op jit(solution)/shard_map/psum | solution.py:610
  388.4 59.5 %collective-permute-start.3 = (bf16[512,768]{1,0:T(8,128)(2,1)}, bf16[512,768]{1,0:T(8,128)(2,1)}, u32[]{:S(2)}, u32[]{:S(2)}) collective-permute-start(bf16[512,768]{1,0:T(8,128)(2,1)} %dynamic-slice_bitcast_fusion.2), channel_id=1, source_target_pairs={{0,1},{1,0},{2,3},{3,2},{4,5},{5,4},{6,7},{7,6},{8,9},{9,8},{10,11... | collective-permute-start | bytes 2359304 | tf_op jit(solution)/shard_map/ppermute | solution.py:461
  420.4 207.7 %all-to-all-start.17 = ((bf16[16,144,384]{2,1,0:T(8,128)(2,1)}), bf16[16,144,384]{2,1,0:T(8,128)(2,1)}, u32[]{:S(2)}, u32[]{:S(2)}) async-start(bf16[16,144,384]{2,1,0:T(8,128)(2,1)} %broadcast_in_dim.38), calls=%async_computation.17 | async-start | bytes 3538944 | tf_op jit(solution)/shard_map/all_to_all | solution.py:489
  447.9 5.9 collective-permute-start.7
  453.7 64.1 %copy-start.70 = (f32[512]{0:T(512)S(1)}, f32[512]{0:T(512)}, u32[]{:S(2)}) copy-start(f32[512]{0:T(512)} %copy-done.69) | copy-start | bytes 6148
  (87 other events, 302.0 us)
Sparse Core Ops, SparseCore 0:
  381.9 236.8 all-reduce.2

commit v2 on v1

v2 whole, which is shorter than its diff:
```python
import math
from functools import partial

import jax
import jax.numpy as jnp
from jax import lax
from jax.experimental import pallas as pl
from jax.experimental.pallas import tpu as pltpu
from jax.sharding import PartitionSpec as P

E = 48
BRANCHES = 5
SEG0 = 1024
SLOTS = 16
BIT_ROWS = 16
DOC_BITS = 6
ROWS_IN = 3 * E + BIT_ROWS
ROWS_OUT = E + BIT_ROWS
EPS = 1e-05
FAR = 1e30
LOG2E = math.log2(math.e)
LN2 = math.log(2.0)
BF = jnp.bfloat16
F32 = jnp.float32
VMEM_LIMIT = 48 * 2**20


def params(**more):
    return pltpu.CompilerParams(vmem_limit_bytes=VMEM_LIMIT, **more)


def norm_rows(values, gain, shift):
    centre = jnp.mean(values, axis=-1, keepdims=True)
    centred = values - centre
    spread = jnp.mean(centred * centred, axis=-1, keepdims=True)
    return centred * lax.rsqrt(spread + EPS) * gain + shift


def reversed_bits(value, count):
    out = jnp.zeros_like(value)
    for bit in range(count):
        out = out * 2 + value // 2**bit % 2
    return out


def bit_reversed(value, count):
    return int(format(value, f"0{count}b")[::-1], 2)


def branch_shape(branch, heads):
    stride = 2**branch
    return (stride, SEG0 // stride, max(1, heads // stride), max(1, stride // heads))


def pieces_of(value):
    high = value.astype(BF).astype(F32)
    rest = value - high
    middle = rest.astype(BF).astype(F32)
    return high, middle, (rest - middle).astype(BF).astype(F32)


def row_block(placed, columns):
    ids = lax.broadcasted_iota(jnp.int32, (BIT_ROWS, columns), 0)
    block = jnp.zeros((BIT_ROWS, columns), F32)
    for row, value in placed.items():
        block = jnp.where(ids == row, value, block)
    return block


def lane_block(ref, rows, start, count):
    return ref[0, 0, rows, aligned(start, count)]


def aligned(start, count):
    if count >= 128:
        return pl.ds(pl.multiple_of(start * count, 128), count)
    return pl.ds(pl.multiple_of(start // (128 // count) * 128, 128), 128)


def moved_part(block, count, source, target):
    per = 128 // count
    lanes = lax.broadcasted_iota(jnp.int32, (1, 128), 1)
    out = block
    for shift in range(1, per):
        turned = jnp.concatenate([block[:, -shift * count :], block[:, : -shift * count]], axis=1)
        out = jnp.where((target - source) % per == shift, turned, out)
    return jnp.where(lanes // count == target, out, 0.0)


def pack_kernel(heads, starts, place, proj, bits, own, *sends):
    head = pl.program_id(0)
    for j in range(3):
        own[0, 0, j * E : (j + 1) * E, :] = proj[j]
    own[0, 0, 3 * E :, :] = bits[...]
    send_blocks(heads, head, starts, place, own, sends)


def send_blocks(heads, head, starts, place, own, sends):
    for branch in range(1, BRANCHES):
        count = branch_shape(branch, heads)[1]
        send = sends[branch - 1]
        start = starts[branch, head]
        block = lane_block(own, slice(None), start, count)
        if count < 128:
            per = 128 // count
            block = moved_part(block.astype(F32), count, start % per, place[0] % per).astype(BF)
        for copy in range(send.shape[0]):
            send[copy, 0] = block


def send_shapes(heads, rows):
    outs, specs = [], []
    for branch in range(1, BRANCHES):
        stride, count, per, split = branch_shape(branch, heads)
        count = max(count, 128)
        outs.append(jax.ShapeDtypeStruct((stride, per, rows, count), BF))
        specs.append(
            pl.BlockSpec((split, 1, rows, count), lambda h, s, t, per=per: (h // per, h % per, 0, 0))
        )
    return outs, specs


def pack_heads(heads, starts, place, proj, bits):
    span = proj.shape[-1]
    sends, send_specs = send_shapes(heads, ROWS_IN)
    return pl.pallas_call(
        partial(pack_kernel, heads),
        grid_spec=pltpu.PrefetchScalarGridSpec(
            num_scalar_prefetch=2,
            grid=(heads,),
            in_specs=[
                pl.BlockSpec((3, E, span), lambda h, s, t: (0, h, 0)),
                pl.BlockSpec((BIT_ROWS, span), lambda h, s, t: (0, 0)),
            ],
            out_specs=[pl.BlockSpec((1, 1, ROWS_IN, span), lambda h, s, t: (0, h, 0, 0))] + send_specs,
        ),
        out_shape=[jax.ShapeDtypeStruct((1, heads, ROWS_IN, span), BF)] + sends,
        compiler_params=params(),
        name="pack_heads",
    )(starts, place, proj, bits)


def load_unit(ref, unit, count, x):
    if ref.shape[0] == 1:
        x[...] = ref[0, unit]
        return
    width = ref.shape[-1]
    per = width // count
    for block in range(ref.shape[0] // per):
        value = ref[block * per, unit]
        for other in range(1, per):
            value = value + ref[block * per + other, unit]
        x[:, block * width : (block + 1) * width] = value


def store_unit(ref, unit, rows, value, column, count):
    width = ref.shape[-1]
    size = min(width, count)
    for start in range(column, column + count, size):
        lanes = slice(start % width, start % width + size)
        ref[start // width, unit, rows, lanes] = value[:, start - column : start - column + size]


def forward_unit(x, q_aug, base, queries, tile, put):
    if isinstance(base, int):
        lanes = slice(base, base + queries)
    else:
        lanes = pl.ds(pl.multiple_of(base, 128), queries)
    q_aug[0:E, :queries] = x[0:E, lanes]
    q_aug[E:, :queries] = (x[3 * E :, lanes].astype(F32) * -FAR).astype(BF)
    bits = x[3 * E :, :].astype(F32)
    k_rows = jnp.concatenate([x[E : 2 * E, :], (1.0 - bits).astype(BF)], axis=0).T
    v_aug = jnp.concatenate([x[2 * E : 3 * E, :], jnp.ones(bits.shape, BF)], axis=0)
    for step in range(queries // tile):
        column = step * tile
        s = jnp.dot(k_rows, q_aug[:, column : column + tile], preferred_element_type=F32)
        top = jnp.max(s, axis=0, keepdims=True)
        p = jnp.exp2(s - top).astype(BF)
        o = jnp.dot(v_aug, p, preferred_element_type=F32)
        total = o[E : E + 1]
        high, middle, low = pieces_of(top + jnp.log2(total))
        block = row_block({0: high, 1: middle, 2: low}, tile)
        put(column, jnp.concatenate([o[:E] * (1.0 / total), block], axis=0).astype(BF))


def group_place(branch):
    stride = 2**branch
    me = lax.axis_index("seq")
    return me // stride * stride, me % stride


def meet_group():
    base, place = group_place(BRANCHES - 1)
    size = 2 ** (BRANCHES - 1)
    barrier = pltpu.get_barrier_semaphore()

    @pl.loop(1, size)
    def _(step):
        pl.semaphore_signal(
            barrier,
            inc=1,
            device_id={"seq": base + (place + step) % size},
            device_id_type=pl.DeviceIdType.MESH,
        )

    pl.semaphore_wait(barrier, size - 1)


def group_copies(branch, source, target, source_block, send_sems, recv_sems, local_sem):
    stride = 2**branch
    base, place = group_place(branch)
    first = stride - branch - 2
    copies = [
        pltpu.make_async_copy(source.at[source_block(place)], target.at[place], local_sem.at[branch - 1])
    ]
    for step in range(1, stride):
        member = (place + step) % stride
        copies.append(
            pltpu.make_async_remote_copy(
                src_ref=source.at[source_block(member)],
                dst_ref=target.at[place],
                send_sem=send_sems.at[first + step],
                recv_sem=recv_sems.at[first + step],
                device_id={"seq": base + member},
                device_id_type=pl.DeviceIdType.MESH,
            )
        )
    return copies


def exchange_forward_kernel(heads, own, *refs):
    count = BRANCHES - 1
    sends, refs = refs[:count], refs[count:]
    first, refs = refs[0], refs[1:]
    gots, refs = refs[:count], refs[count:]
    backs, refs = refs[:count], refs[count:]
    outs, refs = refs[:count], refs[count:]
    x, q_aug, in_send, in_recv, in_local, out_send, out_recv, out_local = refs
    tile = 256
    meet_group()
    coming = {}
    for branch in range(1, BRANCHES):
        coming[branch] = group_copies(
            branch, sends[branch - 1], gots[branch - 1], lambda m: m, in_send, in_recv, in_local
        )
        for copy in coming[branch]:
            copy.start()

    @pl.loop(0, heads)
    def _(head):
        x[...] = own[0, head]

        def put(column, value):
            first[0, head, :, column : column + tile] = value

        forward_unit(x, q_aug, 0, SEG0, tile, put)

    leaving = []
    for branch in range(1, BRANCHES):
        stride, lanes, units, split = branch_shape(branch, heads)
        got, out = gots[branch - 1], outs[branch - 1]
        for copy in coming[branch]:
            copy.wait()
        queries = SEG0 // split
        base = 0 if split == 1 else lax.axis_index("seq") % split * queries

        @pl.loop(0, units)
        def _(unit):
            load_unit(got, unit, lanes, x)
            if split == 1:

                def put(column, value):
                    store_unit(out, unit, slice(None), value, column, value.shape[1])

            else:
                empty = row_block({0: -FAR}, 128)
                empty = jnp.concatenate([jnp.zeros((E, 128), F32), empty], axis=0).astype(BF)
                for block in range(SEG0 // 128):
                    store_unit(out, unit, slice(None), empty, block * 128, 128)

                def put(column, value):
                    width = out.shape[-1]
                    for start in range(0, value.shape[1], width):
                        block = (base + column + start) // width
                        out[block, unit] = value[:, start : start + width]

            forward_unit(x, q_aug, base, queries, min(tile, queries), put)

        per = out.shape[-1] // lanes
        copies = group_copies(
            branch, out, backs[branch - 1], lambda m: m // per, out_send, out_recv, out_local
        )
        for copy in copies:
            copy.start()
        leaving += copies
    for copy in leaving:
        copy.wait()


def exchange_scratch():
    copies = 2**BRANCHES - 2 - BRANCHES + 1
    one = [
        pltpu.SemaphoreType.DMA((copies,)),
        pltpu.SemaphoreType.DMA((copies,)),
        pltpu.SemaphoreType.DMA((BRANCHES - 1,)),
    ]
    return one + one


def unit_cost(units, dots):
    return pl.CostEstimate(
        flops=dots * 2 * units * SEG0 * SEG0 * 256,
        transcendentals=units * SEG0 * SEG0,
        bytes_accessed=units * SEG0 * 1000,
    )


def vmem_specs(count):
    return [pl.BlockSpec(memory_space=pltpu.VMEM)] * count


def out_blocks(heads, rows):
    shapes = []
    for branch in range(1, BRANCHES):
        stride, count, units, split = branch_shape(branch, heads)
        width = max(count, 128)
        shapes.append((SEG0 // width, units, rows, width))
    return shapes


def exchange_forward(heads, own, sends):
    backs = send_shapes(heads, ROWS_OUT)[0]
    gots = send_shapes(heads, ROWS_IN)[0]
    first = jax.ShapeDtypeStruct((1, heads, ROWS_OUT, SEG0), BF)
    results = pl.pallas_call(
        partial(exchange_forward_kernel, heads),
        in_specs=vmem_specs(1 + len(sends)),
        out_specs=vmem_specs(1 + len(gots) + len(backs)),
        out_shape=[first] + gots + backs,
        scratch_shapes=[pltpu.VMEM(shape, BF) for shape in out_blocks(heads, ROWS_OUT)]
        + [pltpu.VMEM((ROWS_IN, SEG0), BF), pltpu.VMEM((ROWS_OUT, SEG0), BF)]
        + exchange_scratch(),
        compiler_params=params(collective_id=0, has_side_effects=True),
        cost_estimate=unit_cost(2 * heads, 2),
        name="exchange_forward",
    )(own, *sends)
    return results[0], results[1 : 1 + len(gots)], results[1 + len(gots) :]


def backward_unit(x, g, q_aug, gk, gv, base, queries, tile, put):
    if isinstance(base, int):
        lanes = slice(base, base + queries)
    else:
        lanes = pl.ds(pl.multiple_of(base, 128), queries)
    extra = g[E:, lanes].astype(F32)
    ids = lax.broadcasted_iota(jnp.int32, extra.shape, 0)
    q = x[0:E, lanes]
    q_aug[0:E, :queries] = q
    q_aug[E:, :queries] = jnp.where(ids >= 12, extra, x[3 * E :, lanes].astype(F32) * -FAR).astype(BF)
    bits = x[3 * E :, :].astype(F32)
    k_aug = jnp.concatenate([x[E : 2 * E, :], (1.0 - bits).astype(BF)], axis=0)
    k_rows = k_aug.T
    v_ids = lax.broadcasted_iota(jnp.int32, bits.shape, 0)
    v_bits = jnp.where(v_ids < 3, 1.0, 0.0).astype(BF)
    v_rows = jnp.concatenate([x[2 * E : 3 * E, :], v_bits], axis=0).T
    q_rows = jnp.concatenate([q, jnp.zeros((BIT_ROWS, queries), BF)], axis=0).T
    g_all = g[:, lanes]
    g_rows = g_all.T
    for step in range(queries // tile):
        column = step * tile
        span = slice(column, column + tile)
        p = jnp.exp2(jnp.dot(k_rows, q_aug[:, span], preferred_element_type=F32))
        gs = p * jnp.dot(v_rows, g_all[:, span], preferred_element_type=F32)
        p, gs = p.astype(BF), gs.astype(BF)
        put(column, jnp.dot(k_aug, gs, preferred_element_type=F32)[:E].astype(BF))
        new_k = jnp.dot(gs, q_rows[span], preferred_element_type=F32)
        new_v = jnp.dot(p, g_rows[span], preferred_element_type=F32)
        if step == 0:
            gk[...] = new_k
            gv[...] = new_v
        else:
            gk[...] += new_k
            gv[...] += new_v
    return (gk[...].T[:E] * LN2).astype(BF), gv[...].T[:E].astype(BF)


def exchange_backward_kernel(heads, own, own_g, *refs):
    count = BRANCHES - 1
    units_in, refs = refs[:count], refs[count:]
    sends, refs = refs[:count], refs[count:]
    first, refs = refs[0], refs[1:]
    backs, refs = refs[:count], refs[count:]
    gots, refs = refs[:count], refs[count:]
    outs, refs = refs[:count], refs[count:]
    x, g, q_aug, gk, gv, in_send, in_recv, in_local, out_send, out_recv, out_local = refs
    tile = 256
    meet_group()
    coming = {}
    for branch in range(1, BRANCHES):
        coming[branch] = group_copies(
            branch, sends[branch - 1], gots[branch - 1], lambda m: m, in_send, in_recv, in_local
        )
        for copy in coming[branch]:
            copy.start()

    def own_heads(low, high):
        @pl.loop(low, high)
        def _(head):
            x[...] = own[0, head]
            g[...] = own_g[0, head]

            def put(column, value):
                first[0, head, :E, column : column + tile] = value

            k_cols, v_cols = backward_unit(x, g, q_aug, gk, gv, 0, SEG0, tile, put)
            first[0, head, E : 2 * E, :] = k_cols
            first[0, head, 2 * E :, :] = v_cols

    own_heads(0, heads // 2)
    leaving = []
    for branch in range(1, BRANCHES):
        stride, lanes, units, split = branch_shape(branch, heads)
        got, out, unit_in = gots[branch - 1], outs[branch - 1], units_in[branch - 1]
        for copy in coming[branch]:
            copy.wait()
        queries = SEG0 // split
        base = 0 if split == 1 else lax.axis_index("seq") % split * queries

        @pl.loop(0, units)
        def _(unit):
            load_unit(unit_in, unit, lanes, x)
            load_unit(got, unit, lanes, g)
            if split == 1:

                def put(column, value):
                    store_unit(out, unit, slice(0, E), value, column, value.shape[1])

            else:
                empty = jnp.zeros((E, 128), BF)
                for block in range(SEG0 // 128):
                    store_unit(out, unit, slice(0, E), empty, block * 128, 128)

                def put(column, value):
                    width = out.shape[-1]
                    for start in range(0, value.shape[1], width):
                        block = (base + column + start) // width
                        out[block, unit, :E, :] = value[:, start : start + width]

            k_cols, v_cols = backward_unit(x, g, q_aug, gk, gv, base, queries, min(tile, queries), put)
            store_unit(out, unit, slice(E, 2 * E), k_cols, 0, SEG0)
            store_unit(out, unit, slice(2 * E, 3 * E), v_cols, 0, SEG0)

        per = out.shape[-1] // lanes
        copies = group_copies(
            branch, out, backs[branch - 1], lambda m: m // per, out_send, out_recv, out_local
        )
        for copy in copies:
            copy.start()
        leaving += copies
    own_heads(heads // 2, heads)
    for copy in leaving:
        copy.wait()


def exchange_backward(heads, own, own_g, units, sends):
    backs = send_shapes(heads, 3 * E)[0]
    first = jax.ShapeDtypeStruct((1, heads, 3 * E, SEG0), BF)
    results = pl.pallas_call(
        partial(exchange_backward_kernel, heads),
        in_specs=vmem_specs(2 + len(units) + len(sends)),
        out_specs=vmem_specs(1 + len(backs)),
        out_shape=[first] + backs,
        scratch_shapes=[pltpu.VMEM(shape.shape, BF) for shape in send_shapes(heads, ROWS_OUT)[0]]
        + [pltpu.VMEM(shape, BF) for shape in out_blocks(heads, 3 * E)]
        + [
            pltpu.VMEM((ROWS_IN, SEG0), BF),
            pltpu.VMEM((ROWS_OUT, SEG0), BF),
            pltpu.VMEM((ROWS_OUT, SEG0), BF),
            pltpu.VMEM((SEG0, ROWS_OUT), F32),
            pltpu.VMEM((SEG0, ROWS_OUT), F32),
        ]
        + exchange_scratch(),
        compiler_params=params(collective_id=1, has_side_effects=True),
        cost_estimate=unit_cost(2 * heads, 5),
        name="exchange_backward",
    )(own, own_g, *units, *sends)
    return results[0], results[1:]


def placed_part(value, count, start, place):
    if count >= 128:
        return value, None
    per = 128 // count
    lanes = lax.broadcasted_iota(jnp.int32, (1, 128), 1)
    return moved_part(value, count, place % per, start % per), lanes // count == start % per


def merge_kernel(heads, starts, place, first, *refs):
    seconds, (mixed, merged, lse) = refs[: BRANCHES - 1], refs[BRANCHES - 1 :]
    head = pl.program_id(0)
    extra = first[0, 0, E:, :].astype(F32)
    merged[0] = first[0, 0, :E, :].astype(F32)
    lse[0] = extra[0:1] + extra[1:2] + extra[2:3]
    for branch in range(1, BRANCHES):
        got = seconds[branch - 1]
        count = branch_shape(branch, heads)[1]
        start = starts[branch, head]
        lanes = aligned(start, count)
        for copy in range(got.shape[0]):
            value, mask = placed_part(got[copy, 0].astype(F32), count, start, place[0])
            new_lse = value[E : E + 1] + value[E + 1 : E + 2] + value[E + 2 : E + 3]
            if mask is not None:
                new_lse = jnp.where(mask, new_lse, -FAR)
            old_lse = lse[0, :, lanes]
            top = jnp.maximum(old_lse, new_lse)
            both = top + jnp.log2(jnp.exp2(old_lse - top) + jnp.exp2(new_lse - top))
            old_w = jnp.exp2(old_lse - both)
            new_w = jnp.exp2(new_lse - both)
            merged[0, :, lanes] = merged[0, :, lanes] * old_w + value[:E] * new_w
            lse[0, :, lanes] = both
    mixed[...] = merged[0].astype(BF)


def merge_heads(heads, starts, place, first, seconds):
    span = first.shape[-1]
    return pl.pallas_call(
        partial(merge_kernel, heads),
        grid_spec=pltpu.PrefetchScalarGridSpec(
            num_scalar_prefetch=2,
            grid=(heads,),
            in_specs=[pl.BlockSpec((1, 1, ROWS_OUT, span), lambda h, s, t: (0, h, 0, 0))]
            + send_shapes(heads, ROWS_OUT)[1],
            out_specs=[
                pl.BlockSpec((E, span), lambda h, s, t: (h, 0)),
                pl.BlockSpec((1, E, span), lambda h, s, t: (h, 0, 0)),
                pl.BlockSpec((1, 1, span), lambda h, s, t: (h, 0, 0)),
            ],
        ),
        out_shape=[
            jax.ShapeDtypeStruct((heads * E, span), BF),
            jax.ShapeDtypeStruct((heads, E, span), F32),
            jax.ShapeDtypeStruct((heads, 1, span), F32),
        ],
        compiler_params=params(),
        name="merge_heads",
    )(starts, place, first, *seconds)


def spread_kernel(heads, starts, place, grad, merged, lse, own, *sends):
    head = pl.program_id(0)
    low = grad[...].astype(BF)
    dots = jnp.sum(low.astype(F32) * merged[0], axis=0, keepdims=True)
    own[0, 0, :E, :] = low
    d = pieces_of(-dots)
    m = pieces_of(-lse[0])
    placed = {0: d[0], 1: d[1], 2: d[2], 12: m[0], 13: m[1], 14: m[2]}
    own[0, 0, E:, :] = row_block(placed, grad.shape[-1]).astype(BF)
    send_blocks(heads, head, starts, place, own, sends)


def spread_heads(heads, starts, place, grad, merged, lse):
    span = grad.shape[-1]
    sends, send_specs = send_shapes(heads, ROWS_OUT)
    return pl.pallas_call(
        partial(spread_kernel, heads),
        grid_spec=pltpu.PrefetchScalarGridSpec(
            num_scalar_prefetch=2,
            grid=(heads,),
            in_specs=[
                pl.BlockSpec((E, span), lambda h, s, t: (h, 0)),
                pl.BlockSpec((1, E, span), lambda h, s, t: (h, 0, 0)),
                pl.BlockSpec((1, 1, span), lambda h, s, t: (h, 0, 0)),
            ],
            out_specs=[pl.BlockSpec((1, 1, ROWS_OUT, span), lambda h, s, t: (0, h, 0, 0))] + send_specs,
        ),
        out_shape=[jax.ShapeDtypeStruct((1, heads, ROWS_OUT, span), BF)] + sends,
        compiler_params=params(),
        name="spread_heads",
    )(starts, place, grad, merged, lse)


def gather_kernel(heads, starts, place, first, *refs):
    seconds, (out, total) = refs[: BRANCHES - 1], refs[BRANCHES - 1 :]
    head = pl.program_id(0)
    total[...] = first[0, 0].astype(F32)
    for branch in range(1, BRANCHES):
        got = seconds[branch - 1]
        count = branch_shape(branch, heads)[1]
        start = starts[branch, head]
        lanes = aligned(start, count)
        value = got[0, 0].astype(F32)
        for copy in range(1, got.shape[0]):
            value += got[copy, 0].astype(F32)
        value = placed_part(value, count, start, place[0])[0]
        total[:, lanes] += value
    out[0] = (total[0:E, :] * E ** (-0.5)).astype(BF)
    out[1] = total[E : 2 * E, :].astype(BF)
    out[2] = total[2 * E :, :].astype(BF)


def gather_heads(heads, starts, place, first, seconds):
    span = first.shape[-1]
    return pl.pallas_call(
        partial(gather_kernel, heads),
        grid_spec=pltpu.PrefetchScalarGridSpec(
            num_scalar_prefetch=2,
            grid=(heads,),
            in_specs=[pl.BlockSpec((1, 1, 3 * E, span), lambda h, s, t: (0, h, 0, 0))]
            + send_shapes(heads, 3 * E)[1],
            out_specs=pl.BlockSpec((3, E, span), lambda h, s, t: (0, h, 0)),
            scratch_shapes=[pltpu.VMEM((3 * E, span), F32)],
        ),
        out_shape=jax.ShapeDtypeStruct((3, heads * E, span), BF),
        compiler_params=params(),
        name="gather_heads",
    )(starts, place, first, *seconds)


def rolled(value, step):
    size = lax.axis_size("head")
    return lax.ppermute(value, "head", [(s, (s + step) % size) for s in range(size)])


def all_rows(own):
    size = lax.axis_size("head")
    me = lax.axis_index("head")
    got = [own] + [rolled(own, step) for step in range(1, size)]
    if size == 2:
        return [jnp.where(me == 0, got[0], got[1]), jnp.where(me == 0, got[1], got[0])]
    stacked = jnp.stack(got)
    return [stacked[(me - place) % size] for place in range(size)]


def sum_rows(parts):
    size = lax.axis_size("head")
    me = lax.axis_index("head")
    total = lax.dynamic_index_in_dim(parts, me, 0, keepdims=False).astype(F32)
    for step in range(1, size):
        sent = lax.dynamic_index_in_dim(parts, (me + step) % size, 0, keepdims=False)
        total = total + rolled(sent, step).astype(F32)
    return total


def sum_seq(value):
    size = lax.axis_size("seq")
    got = lax.all_to_all(value.astype(BF), "seq", 0, 0, tiled=True)
    mine = got.reshape((size, value.shape[0] // size) + value.shape[1:]).astype(F32).sum(0)
    full = jnp.broadcast_to(mine.astype(BF)[None], (size,) + mine.shape)
    return lax.all_to_all(full, "seq", 0, 0, tiled=True).reshape(value.shape).astype(F32)


def local(
    tokens,
    documents,
    offsets,
    in_proj,
    out_proj,
    up_proj,
    down_proj,
    first_gain,
    first_shift,
    second_gain,
    second_shift,
    cotangent,
):
    head_count = lax.axis_size("head")
    seq_id = lax.axis_index("seq")
    row_count, width = tokens.shape
    seq_len = row_count * head_count
    heads = offsets.shape[1]
    per_slot = row_count // SLOTS
    gelu_exact = partial(jax.nn.gelu, approximate=False)

    ids = lax.broadcasted_iota(jnp.int32, (row_count, row_count), 0)
    slot = reversed_bits(ids // per_slot, 4)
    source = ids % per_slot * SLOTS + slot
    order = (source == lax.broadcasted_iota(jnp.int32, (row_count, row_count), 1)).astype(BF)

    def sorted_rows(values):
        return jnp.dot(order, values, preferred_element_type=F32)

    def shard_rows(own):
        parts = [part.reshape(SLOTS, per_slot, -1) for part in all_rows(own)]
        return jnp.stack(parts, axis=1).reshape(seq_len, -1)

    def device_parts(values):
        split = values.reshape(SLOTS, head_count, per_slot, -1)
        return jnp.moveaxis(split, 1, 0).reshape(head_count, row_count, -1)

    x_rows = sorted_rows(tokens)
    cot_low = sorted_rows(cotangent).astype(BF)
    normed_one = norm_rows(x_rows, first_gain, first_shift)
    gathered_one = shard_rows(normed_one.astype(BF))
    cot_all = shard_rows(cot_low)

    my_docs = lax.dynamic_slice_in_dim(documents, seq_id * seq_len, seq_len)
    my_docs = my_docs.reshape(head_count, per_slot, 2, 2, 2, 2).transpose(5, 4, 3, 2, 0, 1).reshape(seq_len)
    bit_ids = jnp.arange(BIT_ROWS, dtype=jnp.int32)[:, None]
    doc_bit = my_docs[None, :] // 2 ** (bit_ids % DOC_BITS) % 2
    bits = jnp.where(bit_ids < DOC_BITS, doc_bit, jnp.where(bit_ids < 2 * DOC_BITS, 1 - doc_bit, 0))
    bits = bits.astype(BF)
    starts = jnp.stack([reversed_bits(offsets[b], b) for b in range(BRANCHES)])

    scales = jnp.array([E ** (-0.5) * LOG2E, 1.0, 1.0], F32)[:, None, None]
    projected = jnp.einsum("td,jdc->jct", gathered_one, in_proj, preferred_element_type=F32)
    projected = (projected * scales).astype(BF)
    place = seq_id.astype(jnp.int32).reshape(1)
    own, *sends = pack_heads(heads, starts, place, projected, bits)
    first_out, units, outs = exchange_forward(heads, own, sends)
    mixed, merged, lse = merge_heads(heads, starts, place, first_out, outs)

    attn_part = jnp.einsum("ct,cd->td", mixed, out_proj, preferred_element_type=F32).astype(BF)
    hidden_one = x_rows + sum_rows(device_parts(attn_part))
    normed_two = norm_rows(hidden_one, second_gain, second_shift)
    gathered_two = shard_rows(normed_two.astype(BF))
    pre_act = jnp.dot(gathered_two, up_proj, preferred_element_type=F32)
    hidden, gelu_pull = jax.vjp(gelu_exact, pre_act)
    hidden = hidden.astype(BF)
    down_part = jnp.dot(hidden, down_proj, preferred_element_type=F32).astype(BF)
    block_rows = hidden_one + sum_rows(device_parts(down_part))
    block_out = jnp.dot(order.T, block_rows.astype(BF), preferred_element_type=F32).astype(BF)

    grad_down = jnp.einsum("tf,td->fd", hidden, cot_all, preferred_element_type=F32).astype(BF)
    grad_act = jnp.einsum("td,fd->tf", cot_all, down_proj, preferred_element_type=F32)
    grad_pre = gelu_pull(grad_act)[0].astype(BF)
    grad_up = jnp.einsum("td,tf->df", gathered_two, grad_pre, preferred_element_type=F32).astype(BF)
    norm_part = jnp.einsum("tf,df->td", grad_pre, up_proj, preferred_element_type=F32).astype(BF)
    grad_normed_two = sum_rows(device_parts(norm_part))
    pull_two = jax.vjp(norm_rows, hidden_one, second_gain, second_shift)[1]
    grad_ln_two, grad_gain_two, grad_shift_two = pull_two(grad_normed_two)
    grad_hidden_one = cot_low.astype(F32) + grad_ln_two
    grad_attn = shard_rows(grad_hidden_one.astype(BF))
    grad_out = jnp.einsum("ct,td->cd", mixed, grad_attn, preferred_element_type=F32).astype(BF)
    grad_merged = jnp.einsum("td,cd->ct", grad_attn, out_proj, preferred_element_type=F32)

    own_g, *sends_g = spread_heads(heads, starts, place, grad_merged, merged, lse)
    first_grad, grads = exchange_backward(heads, own, own_g, units, sends_g)
    grad_qkv = gather_heads(heads, starts, place, first_grad, grads)

    grad_in = jnp.einsum("td,jct->jdc", gathered_one, grad_qkv, preferred_element_type=F32)
    one_part = jnp.einsum("jct,jdc->td", grad_qkv, in_proj, preferred_element_type=F32).astype(BF)
    grad_normed_one = sum_rows(device_parts(one_part))
    pull_one = jax.vjp(norm_rows, x_rows, first_gain, first_shift)[1]
    grad_ln_one, grad_gain_one, grad_shift_one = pull_one(grad_normed_one)
    grad_tokens = jnp.dot(
        order.T.astype(F32),
        grad_hidden_one + grad_ln_one,
        precision=lax.Precision.HIGHEST,
        preferred_element_type=F32,
    )

    middle = lax.psum((grad_out, grad_up, grad_down), "seq")
    flat_in = grad_in.reshape(3 * width, heads * E)
    grad_in = sum_seq(flat_in).reshape(3, width, heads * E)
    gains = jnp.stack([grad_gain_one, grad_shift_one, grad_gain_two, grad_shift_two])
    gains = lax.psum(gains, ("seq", "head"))
    return (
        block_out,
        grad_tokens,
        grad_in,
        middle[0].astype(F32),
        middle[1].astype(F32),
        middle[2].astype(F32),
        gains[0],
        gains[1],
        gains[2],
        gains[3],
    )


def solution(mesh):
    placed = (
        P(("seq", "head"), None),
        P(),
        P(None, "head"),
        P(None, None, "head"),
        P("head", None),
        P(None, "head"),
        P("head", None),
        P(),
        P(),
        P(),
        P(),
        P(("seq", "head"), None),
    )
    return jax.shard_map(
        local,
        mesh=mesh,
        in_specs=placed,
        out_specs=(
            P(("seq", "head"), None),
            P(("seq", "head"), None),
            P(None, None, "head"),
            P("head", None),
            P(None, "head"),
            P("head", None),
            P(),
            P(),
            P(),
            P(),
        ),
        check_vma=False,
    )
```

time: 649 us -> 507 us (0.78)
  blocking collectives: 118 us -> 62.8 us
  starting transfers between devices: 82.4 us -> 30.6 us
  local copies, waits for them, and re-layouts: 61.6 us -> 25.1 us
  Pallas kernels: 114 us -> 143 us
  waiting for transfers between devices: 147 us -> 122 us
    all_to_all x4 -> x0, blocking collectives: 55.6 us -> none  [exchange(): lax.all_to_all(value, 'seq', 0, 0, axis_index_groups=groups, tiled=True)]
    all_to_all x12 -> x0, starting transfers between devices: 50.6 us -> none  [exchange(): lax.all_to_all(value, 'seq', 0, 0, axis_index_groups=groups, tiled=True)]
    pallas_call x10 -> x2, Pallas kernels: 98 us -> 129 us  [the longest x1 67.1 us: exchange_backward(): pl.pallas_call(partial(exchange_backward_kernel, heads), in_specs=vmem_sp...]
    unnamed x196 -> x118, local copies, waits for them, and re-layouts: 41.4 us -> 15.3 us
    all_to_all x12 -> x0, waiting for transfers between devices: 19.3 us -> none  [exchange(): lax.all_to_all(value, 'seq', 0, 0, axis_index_groups=groups, tiled=True)]
    psum x1, waiting for transfers between devices: 94.3 us -> 86.6 us  [local(): middle = lax.psum((grad_out, grad_up, grad_down), 'seq')]
  transfers between devices with their start and end apart: 23 -> 11, of which waited for: 11 -> 4; matrix products, arithmetic and copies ran while one was open for 12% -> 12% of each run, Pallas kernels for 15% -> 0%
where the time goes in v2:
time: 507 us; the launch traced here: 501 us
  Pallas kernels  143 us (28%)
  waiting for transfers between devices  122 us (24%)
  matrix products  64.2 us (13%)
  blocking collectives  62.8 us (12%)
  other arithmetic  37.5 us (7%)
  starting transfers between devices  30.6 us (6%)
  local copies, waits for them, and re-layouts  25.1 us (5%)
  between operations  15.5 us (3%)
    psum x1, waiting for transfers between devices, local(): middle = lax.psum((grad_out, grad_up, grad_down), 'seq')  86.6 us
    pallas_call x1, Pallas kernels, exchange_backward(): pl.pallas_call(partial(exchange_backward_kernel, heads), in_specs=vmem_sp...  67.1 us
    psum x1, blocking collectives, local(): gains = lax.psum(gains, ('seq', 'head'))  62.8 us
    pallas_call x1, Pallas kernels, exchange_forward(): pl.pallas_call(partial(exchange_forward_kernel, heads), in_specs=vmem_spe...  61.8 us
    all_to_all x1, waiting for transfers between devices, sum_seq(): got = lax.all_to_all(value.astype(BF), 'seq', 0, 0, tiled=True)  33.7 us
    all_to_all x1, starting transfers between devices, sum_seq(): lax.all_to_all(full, 'seq', 0, 0, tiled=True).reshape(value.shape)  24.1 us
    dot_general x1, matrix products, local(): jnp.einsum('td,fd->tf', cot_all, down_proj, preferred_element_type=F32)  18 us
    unnamed x118, local copies, waits for them, and re-layouts  15.3 us
  transfers between devices with their start and end apart: 11, of which 4 were waited for; matrix products, arithmetic and copies ran while one was open for 12% of the time, Pallas kernels for 0%

profile of v2, /device:TPU:0, one launch (start us, length us, event | category | flops | bytes accessed | tf_op | source)
XLA Modules:
  0.0 501.2 jit_solution(17369648782246338480)
XLA Ops:
  7.3 2.9 fusion.81
  19.1 2.0 fusion.6.proj
  21.2 4.3 pack_heads.1
  26.5 61.8 %exchange_forward.1 = (bf16[1,8,64,1024]{3,2,1,0:T(8,128)(2,1)S(1)}, bf16[2,4,160,512]{3,2,1,0:T(8,128)(2,1)}, bf16[4,2,160,256]{3,2,1,0:T(8,128)(2,1)S(1)}, bf1...) custom-call(bf16[1,8,160,1024]{3,2,1,0:T(8,128)(2,1)} %get-tuple-ele, ...), custom_call_target="tpu_custom_call" | custom-call | flops 17179869184 | bytes 16384000 | tf_op jit(solution)/shard_map/exchange_forward/pallas_call | solution.py:335
  90.0 2.3 merge_heads.1
  95.2 3.4 convolution_convert_fusion.5
  98.7 2.2 fusion.79
  106.6 2.6 fusion.82
  109.3 18.0 %add_convert_fusion = (bf16[1024,1536]{1,0:T(8,128)(2,1)S(1)}, f32[1024,1536]{1,0:T(8,128)}) fusion(f32[1024,1536]{1,0:T(8,128)S(1)} %fusion.82, bf16[1024,768]{1,0:T(8,128)(2,1)S(1)} %bitcast.134, bf16[1536,768]{1,0:T(8,128)(2,1)S(1)} %copy-done), kind=kOutput, calls=%fused_computation.2 | convolution fusion | flops 2529165312 | bytes 19660800 | tf_op jit(solution)/shard_map/td,fd->tf/dot_general | solution.py:724
  127.3 2.6 convolution_convert_fusion.3
  134.1 2.0 fusion.37
  136.5 3.9 convolution_convert_fusion.1
  144.9 67.1 %exchange_backward.1 = (bf16[1,8,144,1024]{3,2,1,0:T(8,128)(2,1)}, bf16[2,4,144,512]{3,2,1,0:T(8,128)(2,1)}, bf16[4,2,144,256]{3,2,1,0:T(8,128)(2,1)S(1)}, bf16[...) custom-call(bf16[1,8,160,1024]{3,2,1,0:T(8,128)(2,1)} %get-tuple-element.37.own, ...), custom_call_target="tpu_custom_call" | custom-call | flops 42949672960 | bytes 16384000 | tf_op jit(solution)/shard_map/exchange_backward/pallas_call | solution.py:468
  213.3 5.7 %gather_heads.1 = bf16[3,384,1024]{2,1,0:T(8,128)(2,1)S(1)} custom-call(s32[5,8]{1,0:T(8,128)S(1)} %stack.12.starts, s32[1]{0:T(128)} %bitcast.place, bf16[1,8,144,1024]{3,2,1,0:T(8,128)(2,1)} %get-tuple-element.59.first, bf16[2,4,144,512]{3,2,1,0:T(8,128)(2,1)S(1)} %copy-done.4, bf16[4,2,144,256]{3,2,1,0:T(8,128)(2,1)S(1)} %get-tuple-element.61.refs_1_, ...), custom_call_target="tpu_custom_call" | custom-call | tf_op jit(solution)/shard_map/gather_heads/pallas_call | solution.py:603
  220.4 3.2 convert_bitcast_fusion
  223.6 3.9 copy.46
  227.5 4.4 all-to-all-start
  232.0 6.3 %multiply_convert_fusion = bf16[1024,1536]{1,0:T(8,128)(2,1)S(1)} fusion(f32[1024,1536]{1,0:T(8,128)} %get-tuple-element.82, f32[1024,1536]{1,0:T(8,128)} %copy-done.16), kind=kLoop, calls=%fused_computation.3 | loop fusion | flops 4718592 | bytes 15728640 | tf_op jit(solution)/shard_map/convert_element_type | solution.py:718
  238.3 4.2 convolution_convert_fusion
  244.2 4.5 convolution_convert_fusion.4
  250.9 33.7 %all-to-all-done = bf16[16,144,384]{2,1,0:T(8,128)(2,1)} async-done(((bf16[16,144,384]{2,1,0:T(8,128)(2,1)}), bf16[16,144,384]{2,1,0:T(8,128)(2,1)}, u32[]{:S(2)}, u32[]{:S(2)}) %all-to-all-start) | async-done | bytes 1769504 | tf_op jit(solution)/shard_map/all_to_all | solution.py:646
  287.7 24.1 %all-to-all-start.1 = ((bf16[16,144,384]{2,1,0:T(8,128)(2,1)}), bf16[16,144,384]{2,1,0:T(8,128)(2,1)}, u32[]{:S(2)}, u32[]{:S(2)}) async-start(bf16[16,144,384]{2,1,0:T(8,128)(2,1)} %broadcast_in_dim.38), calls=%async_computation.1 | async-start | bytes 3538944 | tf_op jit(solution)/shard_map/all_to_all | solution.py:649
  311.8 4.5 bitcast_convert_fusion
  318.8 3.7 convolution_convert_fusion.6
  323.4 62.8 %psum.31 = f32[4,768]{1,0:T(4,128)S(1)} all-reduce(f32[4,768]{1,0:T(4,128)S(1)} %pad_maximum_fusion.4), channel_id=1, replica_groups=mesh['seq'=16,'head'=2] {'seq','head'}, use_global_device_ids=true, to_apply=%region_16.17 | all-reduce | flops 3072 | bytes 24576 | tf_op jit(solution)/shard_map/psum | solution.py:756
  386.8 2.5 fusion.76
  389.3 5.1 %fusion.10 = f32[512,768]{1,0:T(8,128)} fusion(f32[512,768]{1,0:T(8,128)S(1)} %get-tuple-element.78, f32[512,768]{1,0:T(8,128)S(1)} %copy-done.18, bf16[512,768]{1,0:T(8,128)(2,1)} %convolution_convert_fusion.5, f32[512]{0:T(512)S(1)} %negate_multiply_fusion.1, f32[512]{0:T(512)S(1)} %negate_multiply_fusion.2, s32[512]{0:T(512)S(1)} %copy-done.45, ...), kind=kOutput, calls=%fused_computation.45 | convolution fusion | flops 2439643136 | bytes 5518336 | tf_op jit(solution)/shard_map/dot_general | solution.py:745
  394.4 86.6 %all-reduce.3.cloned.1.call-done = (bf16[384,768]{1,0:T(8,128)(2,1)}, bf16[768,1536]{1,0:T(8,128)(2,1)}, bf16[1536,768]{1,0:T(8,128)(2,1)}) async-done(((bf16[384,768]{1,0:T(8,128)(2,1)}, bf16[768,1536]{1,0:T(8,128)(2,1)}, bf16[1536,768]{1,0:T(8,128)(2,1)}), (bf16[384,768]{1,0:T(8,128)(2,1)}, bf16[768,1536]{1,0:T(8,128)(2,1)}, bf16[1536,768]{1,0:T(8,128)(2,1)})) %all-reduce.3.cloned.1.call-update) | async-done | bytes 5308432 | tf_op jit(solution)/shard_map/psum | solution.py:752
  481.0 2.2 convert_element_type.156
  483.1 4.6 convert_element_type.158
  487.8 2.5 convert_element_type.160
  490.3 3.5 convert.10
  (195 shorter events, 42.5 us)
Async XLA Ops:
  7.2 102.1 %copy-start = (bf16[1536,768]{1,0:T(8,128)(2,1)S(1)}, bf16[1536,768]{1,0:T(8,128)(2,1)}, u32[]{:S(2)}) copy-start(bf16[1536,768]{1,0:T(8,128)(2,1)} %param.19) | copy-start | bytes 7077892
  7.2 87.3 %copy-start.54 = (pred[512]{0:T(512)(128)(4,1)}, pred[512]{0:T(512)(128)(4,1)S(1)}, u32[]{:S(2)}) copy-start(pred[512]{0:T(512)(128)(4,1)S(1)} %get-tuple-element.99) | copy-start | bytes 1540
  7.2 87.3 %copy-start.56 = (pred[512]{0:T(512)(128)(4,1)}, pred[512]{0:T(512)(128)(4,1)S(1)}, u32[]{:S(2)}) copy-start(pred[512]{0:T(512)(128)(4,1)S(1)} %get-tuple-element.100) | copy-start | bytes 1540
  7.2 87.2 %copy-start.40 = (s32[512]{0:T(512)}, s32[512]{0:T(512)S(1)}, u32[]{:S(2)}) copy-start(s32[512]{0:T(512)S(1)} %get-tuple-element.105) | copy-start | bytes 6148
  7.2 87.2 %copy-start.42 = (s32[512]{0:T(512)}, s32[512]{0:T(512)S(1)}, u32[]{:S(2)}) copy-start(s32[512]{0:T(512)S(1)} %get-tuple-element.106) | copy-start | bytes 6148
  7.3 87.2 %copy-start.44 = (s32[512]{0:T(512)}, s32[512]{0:T(512)S(1)}, u32[]{:S(2)}) copy-start(s32[512]{0:T(512)S(1)} %get-tuple-element.103) | copy-start | bytes 6148
  7.3 87.2 %copy-start.46 = (s32[512]{0:T(512)}, s32[512]{0:T(512)S(1)}, u32[]{:S(2)}) copy-start(s32[512]{0:T(512)S(1)} %get-tuple-element.104) | copy-start | bytes 6148
  10.2 4.7 copy-start.29
  11.0 5.9 %copy-start.34 = (f32[512]{0:T(512)}, f32[512]{0:T(512)S(1)}, u32[]{:S(2)}) copy-start(f32[512]{0:T(512)S(1)} %fusion.52) | copy-start | bytes 6148
  12.2 2.8 collective-permute-start
  93.5 5.2 %copy-start.15 = (bf16[16,2,32,768]{3,2,0,1:T(8,128)(2,1)}, bf16[16,2,32,768]{3,2,0,1:T(8,128)(2,1)S(1)}, u32[]{:S(2)}) copy-start(bf16[16,2,32,768]{3,2,0,1:T(8,128)(2,1)S(1)} %copy.34) | copy-start | bytes 4718596
  94.5 4.2 collective-permute-start.1
  98.7 3.9 collective-permute-start.4
  100.8 32.4 %copy-start.12 = (f32[512,768]{1,0:T(8,128)}, f32[512,768]{1,0:T(8,128)S(1)}, u32[]{:S(2)}) copy-start(f32[512,768]{1,0:T(8,128)S(1)} %get-tuple-element.84) | copy-start | bytes 4718596
  102.0 2.5 collective-permute-start.2
  104.2 5.1 %copy-start.25 = (bf16[16,2,32,768]{3,2,1,0:T(8,128)(2,1)}, bf16[16,2,32,768]{3,2,1,0:T(8,128)(2,1)S(1)}, u32[]{:S(2)}) copy-start(bf16[16,2,32,768]{3,2,1,0:T(8,128)(2,1)S(1)} %pad_maximum_fusion.2) | copy-start | bytes 4718596
  109.2 18.0 %copy-start.16 = (f32[1024,1536]{1,0:T(8,128)}, f32[1024,1536]{1,0:T(8,128)S(1)}, u32[]{:S(2)}) copy-start(f32[1024,1536]{1,0:T(8,128)S(1)} %fusion.82) | copy-start | bytes 18874372
  130.1 2.4 collective-permute-start.5
  136.0 4.4 collective-permute-start.6
  213.3 7.1 %copy-start.24 = (bf16[16,2,32,768]{3,2,1,0:T(8,128)(2,1)S(1)}, bf16[16,2,32,768]{3,2,1,0:T(8,128)(2,1)}, u32[]{:S(2)}) copy-start(bf16[16,2,32,768]{3,2,1,0:T(8,128)(2,1)} %copy-done.23) | copy-start | bytes 4718596
  227.5 57.1 %all-to-all-start = ((bf16[16,144,384]{2,1,0:T(8,128)(2,1)}), bf16[16,144,384]{2,1,0:T(8,128)(2,1)}, u32[]{:S(2)}, u32[]{:S(2)}) async-start(bf16[16,144,384]{2,1,0:T(8,128)(2,1)} %bitcast.119), calls=%async_computation | async-start | bytes 3538944 | tf_op jit(solution)/shard_map/all_to_all | solution.py:646
  231.9 249.1 %all-reduce.3.cloned.1.call-start = ((), (), s32[]{:S(2)}) async-start(), calls=%async_computation.2 | async-start | bytes 10616832 | tf_op jit(solution)/shard_map/psum | solution.py:752
  232.0 6.3 %copy-start.26 = (bf16[16,2,32,768]{3,2,1,0:T(8,128)(2,1)S(1)}, bf16[16,2,32,768]{3,2,1,0:T(8,128)(2,1)}, u32[]{:S(2)}) copy-start(bf16[16,2,32,768]{3,2,1,0:T(8,128)(2,1)} %copy-done.25) | copy-start | bytes 4718596
  250.9 65.8 %collective-permute-start.3 = (bf16[512,768]{1,0:T(8,128)(2,1)}, bf16[512,768]{1,0:T(8,128)(2,1)}, u32[]{:S(2)}, u32[]{:S(2)}) collective-permute-start(bf16[512,768]{1,0:T(8,128)(2,1)} %dynamic-slice_bitcast_fusion.2), channel_id=1, source_target_pairs={{0,1},{1,0},{2,3},{3,2},{4,5},{5,4},{6,7},{7,6},{8,9},{9,8},{10,11... | collective-permute-start | bytes 2359304 | tf_op jit(solution)/shard_map/ppermute | solution.py:621
  287.7 202.6 %all-to-all-start.1 = ((bf16[16,144,384]{2,1,0:T(8,128)(2,1)}), bf16[16,144,384]{2,1,0:T(8,128)(2,1)}, u32[]{:S(2)}, u32[]{:S(2)}) async-start(bf16[16,144,384]{2,1,0:T(8,128)(2,1)} %broadcast_in_dim.38), calls=%async_computation.1 | async-start | bytes 3538944 | tf_op jit(solution)/shard_map/all_to_all | solution.py:649
  316.5 6.0 %copy-start.14 = (bf16[16,2,32,768]{3,2,0,1:T(8,128)(2,1)}, bf16[16,2,32,768]{3,2,0,1:T(8,128)(2,1)S(1)}, u32[]{:S(2)}) copy-start(bf16[16,2,32,768]{3,2,0,1:T(8,128)(2,1)S(1)} %copy.45) | copy-start | bytes 4718596
  316.6 5.9 %copy-start.11 = (f32[512,768]{1,0:T(8,128)S(1)}, f32[512,768]{1,0:T(8,128)}, u32[]{:S(2)}) copy-start(f32[512,768]{1,0:T(8,128)} %copy-done.10) | copy-start | bytes 4718596
  316.6 5.9 %copy-start.30 = (f32[512]{0:T(512)S(1)}, f32[512]{0:T(512)}, u32[]{:S(2)}) copy-start(f32[512]{0:T(512)} %copy-done.29) | copy-start | bytes 6148
  316.6 5.9 %copy-start.33 = (f32[768]{0:T(1024)S(1)}, f32[768]{0:T(1024)}, u32[]{:S(2)}) copy-start(f32[768]{0:T(1024)} %param.20) | copy-start | bytes 9220
  316.6 5.9 %copy-start.35 = (f32[512]{0:T(512)S(1)}, f32[512]{0:T(512)}, u32[]{:S(2)}) copy-start(f32[512]{0:T(512)} %copy-done.34) | copy-start | bytes 6148
  316.6 5.9 %collective-permute-start.7 = (bf16[512,768]{1,0:T(8,128)(2,1)S(1)}, bf16[512,768]{1,0:T(8,128)(2,1)S(1)}, u32[]{:S(2)}, u32[]{:S(2)}) collective-permute-start(bf16[512,768]{1,0:T(8,128)(2,1)S(1)} %dynamic-slice_bitcast_fusion), channel_id=1, source_target_pairs={{0,1},{1,0},{2,3},{3,2},{4,5},{5,4},{6,7},{7,6},{8,9},{9,8},{10,11... | collective-permute-start | bytes 2359304 | tf_op jit(solution)/shard_map/ppermute | solution.py:621
  322.5 64.3 %copy-start.37 = (f32[512]{0:T(512)S(1)}, f32[512]{0:T(512)}, u32[]{:S(2)}) copy-start(f32[512]{0:T(512)} %copy-done.36) | copy-start | bytes 6148
  (38 other events, 75.1 us)
Sparse Core Ops, SparseCore 0:
  244.3 236.6 all-reduce.2

commit v3 on v2

--- a/solution.py
+++ b/solution.py
@@ -189,21 +189,130 @@
     return me // stride * stride, me % stride
 
 
-def meet_group():
-    base, place = group_place(BRANCHES - 1)
-    size = 2 ** (BRANCHES - 1)
+def meet_axis():
+    size = lax.axis_size("seq")
+    me = lax.axis_index("seq")
     barrier = pltpu.get_barrier_semaphore()
 
     @pl.loop(1, size)
     def _(step):
         pl.semaphore_signal(
-            barrier,
-            inc=1,
-            device_id={"seq": base + (place + step) % size},
+            barrier, inc=1, device_id={"seq": (me + step) % size}, device_id_type=pl.DeviceIdType.MESH
+        )
+
+    pl.semaphore_wait(barrier, size - 1)
+
+
+class Reduction:
+    STEPS = 7
+
+    def __init__(self, order, parts, total, half, quarter, others, send, recv):
+        self.parts, self.total = parts, total
+        self.half, self.quarter, self.others = half, quarter, others
+        self.send, self.recv = send, recv
+        me = lax.axis_index("seq")
+        self.rest = lax.axis_size("seq") // 4
+        self.me = me
+        bits = (me % 2, me // 2 % 2)
+        self.bits = [bits[bit] for bit in order]
+        self.partners = [me + (1 - 2 * bits[bit]) * 2**bit for bit in order]
+        self.place = me // 4
+        self.flying = []
+
+    def copy(self, source, target, device, sem):
+        made = pltpu.make_async_remote_copy(
+            src_ref=source,
+            dst_ref=target,
+            send_sem=self.send.at[sem],
+            recv_sem=self.recv.at[sem],
+            device_id={"seq": device},
             device_id_type=pl.DeviceIdType.MESH,
         )
-
-    pl.semaphore_wait(barrier, size - 1)
+        made.start()
+
+        def wait():
+            made.wait()
+
+        self.flying.append(wait)
+
+    def land(self):
+        for wait in self.flying:
+            wait()
+        self.flying = []
+
+    def others_of(self):
+        for step in range(1, self.rest):
+            place = (self.place + step) % self.rest
+            yield step, place, place * 4 + self.me % 4
+
+    def step(self, number):
+        one, two = self.bits
+        rest = self.rest
+        if number == 0:
+            self.copy(self.parts.at[1 - one], self.half, self.partners[0], 0)
+            return
+        self.land()
+        if number == 1:
+
+            @pl.loop(0, 2 * rest)
+            def _(i):
+                j, z = i // rest, i % rest
+                mine = self.parts[one, j, z].astype(F32)
+                self.half[j, z] = (mine + self.half[j, z].astype(F32)).astype(BF)
+
+            self.copy(self.half.at[1 - two], self.quarter, self.partners[1], 1)
+        elif number == 2:
+
+            @pl.loop(0, rest)
+            def _(z):
+                mine = self.half[two, z].astype(F32)
+                self.quarter[z] = (mine + self.quarter[z].astype(F32)).astype(BF)
+
+            for step, place, device in self.others_of():
+                self.copy(self.quarter.at[place], self.others.at[step - 1], device, 1 + step)
+        elif number == 3:
+            mine = self.quarter[self.place].astype(F32)
+            for step in range(1, rest):
+                mine = mine + self.others[step - 1].astype(F32)
+            self.total[one, two, self.place] = mine.astype(BF)
+            block = self.total.at[one, two, self.place]
+            for step, place, device in self.others_of():
+                self.copy(block, block, device, rest + step)
+        elif number == 4:
+            block = self.total.at[one, two]
+            self.copy(block, block, self.partners[1], 2 * rest)
+        elif number == 5:
+            block = self.total.at[one]
+            self.copy(block, block, self.partners[0], 2 * rest + 1)
+
+    @staticmethod
+    def scratch(size, rows, columns):
+        rest = size // 4
+        count = 2 * rest + 2
+        return [
+            pltpu.VMEM((2, rest, rows, columns), BF),
+            pltpu.VMEM((rest, rows, columns), BF),
+            pltpu.VMEM((rest - 1, rows, columns), BF),
+            pltpu.SemaphoreType.DMA((count,)),
+            pltpu.SemaphoreType.DMA((count,)),
+        ]
+
+
+def reduction_parts(value, size):
+    rows, columns = value.shape
+    return value.reshape(2, 2, size // 4, rows // size, columns)
+
+
+def reduction_whole(value):
+    return value.reshape(-1, value.shape[-1])
+
+
+def make_reductions(orders, parts, totals, scratch):
+    out = []
+    for order, one, total in zip(orders, parts, totals):
+        out.append(Reduction(order, one, total, *scratch[:5]))
+        scratch = scratch[5:]
+    return out
 
 
 def group_copies(branch, source, target, source_block, send_sems, recv_sems, local_sem):
@@ -237,7 +346,7 @@
     outs, refs = refs[:count], refs[count:]
     x, q_aug, in_send, in_recv, in_local, out_send, out_recv, out_local = refs
     tile = 256
-    meet_group()
+    meet_axis()
     coming = {}
     for branch in range(1, BRANCHES):
         coming[branch] = group_copies(
@@ -384,17 +493,53 @@
     return (gk[...].T[:E] * LN2).astype(BF), gv[...].T[:E].astype(BF)
 
 
-def exchange_backward_kernel(heads, own, own_g, *refs):
+def reduction_plan(streams, blocks):
+    early = {
+        0: [(s, 0) for s in range(streams)],
+        6: [(1, 1)],
+        7: [(0, 1)],
+        9: [(1, 2), (0, 2)],
+        10: [(3, 1)],
+        11: [(2, 1), (4, 1), (1, 3), (0, 3)],
+        13: [(3, 2), (1, 4), (0, 4)],
+        14: [(2, 2), (4, 2)],
+        15: [(3, 3), (1, 5), (0, 5)],
+        16: [(2, 3), (4, 3)],
+    }
+    done = {s: 0 for s in range(streams)}
+    plan = {}
+    for block, events in early.items():
+        for stream, step in events:
+            if stream < streams:
+                plan.setdefault(block * blocks // 16, []).append((stream, step))
+                done[stream] = step + 1
+    last = []
+    for step in range(Reduction.STEPS):
+        last += [(s, step) for s in (1, 0, 3, 2, 4) if s < streams and step >= done[s]]
+    return plan, last
+
+
+def stream_orders(count):
+    return [((0, 1), (1, 0))[s % 2] for s in range(count)]
+
+
+def exchange_backward_kernel(heads, streams, own, own_g, *refs):
     count = BRANCHES - 1
     units_in, refs = refs[:count], refs[count:]
     sends, refs = refs[:count], refs[count:]
+    parts, refs = refs[:streams], refs[streams:]
     first, refs = refs[0], refs[1:]
     backs, refs = refs[:count], refs[count:]
+    totals, refs = refs[:streams], refs[streams:]
     gots, refs = refs[:count], refs[count:]
     outs, refs = refs[:count], refs[count:]
-    x, g, q_aug, gk, gv, in_send, in_recv, in_local, out_send, out_recv, out_local = refs
+    x, g, q_aug, gk, gv, in_send, in_recv, in_local, out_send, out_recv, out_local = refs[:11]
+    reductions = make_reductions(stream_orders(streams), parts, totals, refs[11:])
+    shapes = [branch_shape(b, heads) for b in range(BRANCHES)]
+    blocks = heads + sum(shape[2] for shape in shapes[1:])
+    plan, last = reduction_plan(streams, blocks)
     tile = 256
-    meet_group()
+    meet_axis()
     coming = {}
     for branch in range(1, BRANCHES):
         coming[branch] = group_copies(
@@ -403,31 +548,44 @@
         for copy in coming[branch]:
             copy.start()
 
-    def own_heads(low, high):
-        @pl.loop(low, high)
-        def _(head):
-            x[...] = own[0, head]
-            g[...] = own_g[0, head]
-
-            def put(column, value):
-                first[0, head, :E, column : column + tile] = value
-
-            k_cols, v_cols = backward_unit(x, g, q_aug, gk, gv, 0, SEG0, tile, put)
-            first[0, head, E : 2 * E, :] = k_cols
-            first[0, head, 2 * E :, :] = v_cols
-
-    own_heads(0, heads // 2)
+    def events(block):
+        for stream, step in plan.get(block, []):
+            reductions[stream].step(step)
+
+    def run_blocks(done, low, high, body):
+        size = high - low
+        marks = [i for i in range(1, size) if plan.get(done + i)]
+        edges = [0] + marks + [size]
+        for at, to in zip(edges, edges[1:]):
+            events(done + at)
+            if to - at == 1:
+                body(low + at)
+            else:
+                pl.loop(low + at, low + to)(body)
+        return done + size
+
+    def own_head(head):
+        x[...] = own[0, head]
+        g[...] = own_g[0, head]
+
+        def put(column, value):
+            first[0, head, :E, column : column + tile] = value
+
+        k_cols, v_cols = backward_unit(x, g, q_aug, gk, gv, 0, SEG0, tile, put)
+        first[0, head, E : 2 * E, :] = k_cols
+        first[0, head, 2 * E :, :] = v_cols
+
+    done = run_blocks(0, 0, heads // 2, own_head)
     leaving = []
     for branch in range(1, BRANCHES):
-        stride, lanes, units, split = branch_shape(branch, heads)
+        stride, lanes, units, split = shapes[branch]
         got, out, unit_in = gots[branch - 1], outs[branch - 1], units_in[branch - 1]
         for copy in coming[branch]:
             copy.wait()
         queries = SEG0 // split
         base = 0 if split == 1 else lax.axis_index("seq") % split * queries
 
-        @pl.loop(0, units)
-        def _(unit):
+        def other_head(unit):
             load_unit(unit_in, unit, lanes, x)
             load_unit(got, unit, lanes, g)
             if split == 1:
@@ -450,6 +608,7 @@
             store_unit(out, unit, slice(E, 2 * E), k_cols, 0, SEG0)
             store_unit(out, unit, slice(2 * E, 3 * E), v_cols, 0, SEG0)
 
+        done = run_blocks(done, 0, units, other_head)
         per = out.shape[-1] // lanes
         copies = group_copies(
             branch, out, backs[branch - 1], lambda m: m // per, out_send, out_recv, out_local
@@ -457,19 +616,27 @@
         for copy in copies:
             copy.start()
         leaving += copies
-    own_heads(heads // 2, heads)
+    done = run_blocks(done, heads // 2, heads, own_head)
+    events(done)
     for copy in leaving:
         copy.wait()
-
-
-def exchange_backward(heads, own, own_g, units, sends):
+    for stream, step in last:
+        reductions[stream].step(step)
+
+
+def exchange_backward(heads, own, own_g, units, sends, terms):
+    size = lax.axis_size("seq")
     backs = send_shapes(heads, 3 * E)[0]
     first = jax.ShapeDtypeStruct((1, heads, 3 * E, SEG0), BF)
+    parts = [reduction_parts(term, size) for term in terms]
+    scratch = []
+    for part in parts:
+        scratch += Reduction.scratch(size, *part.shape[-2:])
     results = pl.pallas_call(
-        partial(exchange_backward_kernel, heads),
-        in_specs=vmem_specs(2 + len(units) + len(sends)),
-        out_specs=vmem_specs(1 + len(backs)),
-        out_shape=[first] + backs,
+        partial(exchange_backward_kernel, heads, len(parts)),
+        in_specs=vmem_specs(2 + len(units) + len(sends) + len(parts)),
+        out_specs=vmem_specs(1 + len(backs) + len(parts)),
+        out_shape=[first] + backs + [jax.ShapeDtypeStruct(part.shape, BF) for part in parts],
         scratch_shapes=[pltpu.VMEM(shape.shape, BF) for shape in send_shapes(heads, ROWS_OUT)[0]]
         + [pltpu.VMEM(shape, BF) for shape in out_blocks(heads, 3 * E)]
         + [
@@ -479,12 +646,92 @@
             pltpu.VMEM((SEG0, ROWS_OUT), F32),
             pltpu.VMEM((SEG0, ROWS_OUT), F32),
         ]
-        + exchange_scratch(),
+        + exchange_scratch()
+        + scratch,
         compiler_params=params(collective_id=1, has_side_effects=True),
         cost_estimate=unit_cost(2 * heads, 5),
         name="exchange_backward",
-    )(own, own_g, *units, *sends)
-    return results[0], results[1:]
+    )(own, own_g, *units, *sends, *parts)
+    sums = [reduction_whole(total) for total in results[1 + len(backs) :]]
+    return results[0], results[1 : 1 + len(backs)], sums
+
+
+def last_sums_kernel(streams, gains, *refs):
+    parts, refs = refs[:streams], refs[streams:]
+    gains_out, refs = refs[0], refs[1:]
+    totals, refs = refs[:streams], refs[streams:]
+    one, two, others, send, recv = refs[:5]
+    reductions = make_reductions(stream_orders(streams), parts, totals, refs[5:])
+    me = lax.axis_index("seq")
+    rest = lax.axis_size("seq") // 4
+    place = me // 4
+
+    def copy(source, target, device, sem):
+        return pltpu.make_async_remote_copy(
+            src_ref=source,
+            dst_ref=target,
+            send_sem=send.at[sem],
+            recv_sem=recv.at[sem],
+            device_id={"seq": device},
+            device_id_type=pl.DeviceIdType.MESH,
+        )
+
+    meet_axis()
+    for reduction in reductions:
+        reduction.step(0)
+    swap = copy(gains, one, me + 1 - 2 * (me % 2), 0)
+    swap.start()
+    swap.wait()
+    one[...] += gains[...]
+    for reduction in reductions:
+        reduction.step(1)
+    swap = copy(one, two, me + 2 - 4 * (me // 2 % 2), 1)
+    swap.start()
+    swap.wait()
+    two[...] += one[...]
+    for reduction in reductions:
+        reduction.step(2)
+    others[place] = two[...]
+    swaps = []
+    for step in range(1, rest):
+        device = (place + step) % rest * 4 + me % 4
+        swaps.append(copy(two, others.at[place], device, 1 + step))
+        swaps[-1].start()
+    for swap in swaps:
+        swap.wait()
+    total = others[0]
+    for z in range(1, rest):
+        total = total + others[z]
+    gains_out[...] = total
+    for number in range(3, Reduction.STEPS):
+        for reduction in reductions:
+            reduction.step(number)
+
+
+def last_sums(gains, terms):
+    size = lax.axis_size("seq")
+    parts = [reduction_parts(term, size) for term in terms]
+    scratch = []
+    for part in parts:
+        scratch += Reduction.scratch(size, *part.shape[-2:])
+    results = pl.pallas_call(
+        partial(last_sums_kernel, len(parts)),
+        in_specs=vmem_specs(1 + len(parts)),
+        out_specs=vmem_specs(1 + len(parts)),
+        out_shape=[jax.ShapeDtypeStruct(gains.shape, F32)]
+        + [jax.ShapeDtypeStruct(part.shape, BF) for part in parts],
+        scratch_shapes=[
+            pltpu.VMEM(gains.shape, F32),
+            pltpu.VMEM(gains.shape, F32),
+            pltpu.VMEM((size // 4,) + gains.shape, F32),
+            pltpu.SemaphoreType.DMA((size // 4 + 1,)),
+            pltpu.SemaphoreType.DMA((size // 4 + 1,)),
+        ]
+        + scratch,
+        compiler_params=params(collective_id=2, has_side_effects=True),
+        name="last_sums",
+    )(gains, *parts)
+    return results[0], [reduction_whole(total) for total in results[1:]]
 
 
 def placed_part(value, count, start, place):
@@ -641,14 +888,6 @@
     return total
 
 
-def sum_seq(value):
-    size = lax.axis_size("seq")
-    got = lax.all_to_all(value.astype(BF), "seq", 0, 0, tiled=True)
-    mine = got.reshape((size, value.shape[0] // size) + value.shape[1:]).astype(F32).sum(0)
-    full = jnp.broadcast_to(mine.astype(BF)[None], (size,) + mine.shape)
-    return lax.all_to_all(full, "seq", 0, 0, tiled=True).reshape(value.shape).astype(F32)
-
-
 def local(
     tokens,
     documents,
@@ -720,10 +959,20 @@
     block_rows = hidden_one + sum_rows(device_parts(down_part))
     block_out = jnp.dot(order.T, block_rows.astype(BF), preferred_element_type=F32).astype(BF)
 
-    grad_down = jnp.einsum("tf,td->fd", hidden, cot_all, preferred_element_type=F32).astype(BF)
+    chunks = max(1, up_proj.shape[1] // width)
+
+    def columns(values):
+        return jnp.split(values, chunks, axis=1)
+
+    grad_down = [
+        jnp.einsum("tf,td->fd", part, cot_all, preferred_element_type=F32).astype(BF) for part in columns(hidden)
+    ]
     grad_act = jnp.einsum("td,fd->tf", cot_all, down_proj, preferred_element_type=F32)
     grad_pre = gelu_pull(grad_act)[0].astype(BF)
-    grad_up = jnp.einsum("td,tf->df", gathered_two, grad_pre, preferred_element_type=F32).astype(BF)
+    grad_up = [
+        jnp.einsum("td,tf->df", gathered_two, part, preferred_element_type=F32).astype(BF)
+        for part in columns(grad_pre)
+    ]
     norm_part = jnp.einsum("tf,df->td", grad_pre, up_proj, preferred_element_type=F32).astype(BF)
     grad_normed_two = sum_rows(device_parts(norm_part))
     pull_two = jax.vjp(norm_rows, hidden_one, second_gain, second_shift)[1]
@@ -734,7 +983,8 @@
     grad_merged = jnp.einsum("td,cd->ct", grad_attn, out_proj, preferred_element_type=F32)
 
     own_g, *sends_g = spread_heads(heads, starts, place, grad_merged, merged, lse)
-    first_grad, grads = exchange_backward(heads, own, own_g, units, sends_g)
+    terms = [term for pair in zip(grad_up, grad_down) for term in pair] + [grad_out]
+    first_grad, grads, sums = exchange_backward(heads, own, own_g, units, sends_g, terms)
     grad_qkv = gather_heads(heads, starts, place, first_grad, grads)
 
     grad_in = jnp.einsum("td,jct->jdc", gathered_one, grad_qkv, preferred_element_type=F32)
@@ -749,18 +999,17 @@
         preferred_element_type=F32,
     )
 
-    middle = lax.psum((grad_out, grad_up, grad_down), "seq")
-    flat_in = grad_in.reshape(3 * width, heads * E)
-    grad_in = sum_seq(flat_in).reshape(3, width, heads * E)
     gains = jnp.stack([grad_gain_one, grad_shift_one, grad_gain_two, grad_shift_two])
-    gains = lax.psum(gains, ("seq", "head"))
+    gains = jnp.concatenate([gains, jnp.zeros_like(gains)])
+    gains = sum(all_rows(gains))
+    gains, grad_in = last_sums(gains, [grad_in[j].astype(BF) for j in range(3)])
     return (
         block_out,
         grad_tokens,
-        grad_in,
-        middle[0].astype(F32),
-        middle[1].astype(F32),
-        middle[2].astype(F32),
+        jnp.stack(grad_in).astype(F32),
+        sums[-1].astype(F32),
+        jnp.concatenate(sums[:-1:2], axis=1).astype(F32),
+        jnp.concatenate(sums[1:-1:2], axis=0).astype(F32),
         gains[0],
         gains[1],
         gains[2],

time: 507 us -> 424 us (0.84)
  Pallas kernels: 143 us -> 300 us
  waiting for transfers between devices: 122 us -> 0.29 us
  blocking collectives: 62.8 us -> 0 us
  starting transfers between devices: 30.6 us -> 2.7 us
  between operations: 15.5 us -> 1.61 us
  other arithmetic: 37.5 us -> 29.6 us
    pallas_call x1 -> x2, Pallas kernels: 67.1 us -> 224 us  [the longest x1 162 us: exchange_backward(): pl.pallas_call(partial(exchange_backward_kernel, heads, len(parts)), in_s...]
    psum x1 -> x0, waiting for transfers between devices: 86.6 us -> none  [local(): middle = lax.psum((grad_out, grad_up, grad_down), 'seq')]
    psum x1 -> x0, blocking collectives: 62.8 us -> none  [local(): gains = lax.psum(gains, ('seq', 'head'))]
    all_to_all x2 -> x0, waiting for transfers between devices: 33.7 us -> none  [the longest x1 33.7 us: sum_seq(): got = lax.all_to_all(value.astype(BF), 'seq', 0, 0, tiled=True)]
    all_to_all x2 -> x0, starting transfers between devices: 28.5 us -> none  [the longest x1 24.1 us: sum_seq(): lax.all_to_all(full, 'seq', 0, 0, tiled=True).reshape(value.shape)]
    unnamed x118 -> x92, local copies, waits for them, and re-layouts: 15.3 us -> 15.2 us
  transfers between devices with their start and end apart: 11 -> 9, of which waited for: 4 -> 1; matrix products, arithmetic and copies ran while one was open for 12% -> 9% of each run, Pallas kernels for 0% -> 0%
where the time goes in v3:
time: 424 us; the launch traced here: 419 us
  Pallas kernels  300 us (71%)
  matrix products  61.4 us (14%)
  other arithmetic  29.6 us (7%)
  local copies, waits for them, and re-layouts  22.9 us (5%)
    pallas_call x1, Pallas kernels, exchange_backward(): pl.pallas_call(partial(exchange_backward_kernel, heads, len(parts)), in_s...  162 us
    pallas_call x1, Pallas kernels, last_sums(): pl.pallas_call(partial(last_sums_kernel, len(parts)), in_specs=vmem_specs...  62.5 us
    pallas_call x1, Pallas kernels, exchange_forward(): pl.pallas_call(partial(exchange_forward_kernel, heads), in_specs=vmem_spe...  61.7 us
    dot_general x1, matrix products, local(): jnp.einsum('td,fd->tf', cot_all, down_proj, preferred_element_type=F32)  16.4 us
    unnamed x92, local copies, waits for them, and re-layouts  15.2 us
  transfers between devices with their start and end apart: 9, of which 1 were waited for; matrix products, arithmetic and copies ran while one was open for 9% of the time, Pallas kernels for 0%

profile of v3, /device:TPU:0, one launch (start us, length us, event | category | flops | bytes accessed | tf_op | source)
XLA Modules:
  0.0 418.5 jit_solution(15572558201256761422)
XLA Ops:
  0.7 2.9 fusion.102
  8.3 1.9 broadcast_select_fusion.7
  10.6 1.9 copy-done.38
  12.5 2.0 fusion.6.proj
  14.5 4.2 %pack_heads.1 = (bf16[1,8,160,1024]{3,2,1,0:T(8,128)(2,1)}, bf16[2,4,160,512]{3,2,1,0:T(8,128)(2,1)S(1)}, bf16[4,2,160,256]{3,2,1,0:T(8,128)(2,1)S(1)}, bf16[8,1...) custom-call(s32[5,8]{1,0:T(8,128)S(1)} %stack.12.starts, s32[1]{0:T(128)} %bitcast.place, ...), custom_call_target="tpu_custom_call" | custom-call | tf_op jit(solution)/shard_map/pack_heads/pallas_call | solution.py:126
  19.8 61.7 %exchange_forward.1 = (bf16[1,8,64,1024]{3,2,1,0:T(8,128)(2,1)S(1)}, bf16[2,4,160,512]{3,2,1,0:T(8,128)(2,1)}, bf16[4,2,160,256]{3,2,1,0:T(8,128)(2,1)S(1)}, bf1...) custom-call(bf16[1,8,160,1024]{3,2,1,0:T(8,128)(2,1)} %get-tuple-ele, ...), custom_call_target="tpu_custom_call" | custom-call | flops 17179869184 | bytes 16384000 | tf_op jit(solution)/shard_map/exchange_forward/pallas_call | solution.py:444
  82.4 2.3 merge_heads.1
  87.7 3.2 convolution_convert_fusion.3
  90.9 2.2 fusion.99
  97.3 2.1 copy-done.37
  99.4 2.6 fusion.103
  102.0 16.4 %add_convert_fusion = (bf16[1024,1536]{1,0:T(8,128)(2,1)S(1)}, f32[1024,1536]{1,0:T(8,128)S(1)}) fusion(f32[1024,1536]{1,0:T(8,128)S(1)} %fusion.103, bf16[1024,768]{1,0:T(8,128)(2,1)S(1)} %bitcast.155, bf16[1536,768]{1,0:T(8,128)(2,1)S(1)} %copy-done), kind=kOutput, calls=%fused_computation.2 | convolution fusion | flops 2529165312 | bytes 19660800 | tf_op jit(solution)/shard_map/td,fd->tf/dot_general | solution.py:970
  118.4 4.1 convolution_convert_fusion.1
  122.5 2.5 fusion.21
  125.0 3.3 multiply_convert_fusion
  128.3 4.6 %convolution_convert_fusion.2 = bf16[1024,768]{1,0:T(8,128)(2,1)S(1)} fusion(bf16[1024,1536]{1,0:T(8,128)(2,1)} %multiply_convert_fusion, bf16[1536,768]{1,0:T(8,128)(2,1)S(1)} %copy-done), kind=kOutput, calls=%fused_computation.32 | convolution fusion | flops 2416705536 | bytes 7077888 | tf_op jit(solution)/shard_map/dot_general | solution.py:958
  133.0 2.5 fusion.24
  139.2 2.5 fusion.27
  141.7 2.5 fusion.30
  145.8 2.0 fusion.57
  148.2 2.7 convolution_convert_fusion.4
  154.4 1.8 spread_heads.1
  157.2 161.5 %exchange_backward.1 = (bf16[1,8,144,1024]{3,2,1,0:T(8,128)(2,1)}, bf16[2,4,144,512]{3,2,1,0:T(8,128)(2,1)}, bf16[4,2,144,256]{3,2,1,0:T(8,128)(2,1)S(1)}, bf16[...) custom-call(bf16[1,8,160,1024]{3,2,1,0:T(8,128)(2,1)} %get-tuple-ele, ...), custom_call_target="tpu_custom_call" | custom-call | flops 42949672960 | bytes 16384000 | tf_op jit(solution)/shard_map/exchange_backward/pallas_call | solution.py:635
  320.0 5.9 %gather_heads.1 = bf16[3,384,1024]{2,1,0:T(8,128)(2,1)S(1)} custom-call(s32[5,8]{1,0:T(8,128)S(1)} %stack.12.starts, s32[1]{0:T(128)} %bitcast.place, bf16[1,8,144,1024]{3,2,1,0:T(8,128)(2,1)} %get-tuple-element.68.first, bf16[2,4,144,512]{3,2,1,0:T(8,128)(2,1)S(1)} %copy-done.4, bf16[4,2,144,256]{3,2,1,0:T(8,128)(2,1)S(1)} %get-tuple-element.70.refs_1_, ...), custom_call_target="tpu_custom_call" | custom-call | tf_op jit(solution)/shard_map/gather_heads/pallas_call | solution.py:850
  326.0 2.2 bitcast_convert_fusion
  328.3 2.0 convert_bitcast_fusion
  335.5 4.6 %maximum_convert_fusion = f32[768,1536]{1,0:T(8,128)} fusion(bf16[768,768]{1,0:T(8,128)(2,1)} %bitcast.170, bf16[768,768]{1,0:T(8,128)(2,1)} %bitcast.169), kind=kLoop, calls=%fused_computation.26 | loop fusion | flops 4718592 | bytes 7077888 | tf_op jit(solution)/shard_map/convert_element_type | solution.py:1011
  340.2 2.6 maximum_convert_fusion.1
  344.0 1.8 fusion.96
  346.4 6.0 %fusion.18 = f32[512,768]{1,0:T(8,128)} fusion(f32[512,768]{1,0:T(8,128)} %get-tuple-element.93, f32[512,768]{1,0:T(8,128)} %copy-done.16, bf16[512,768]{1,0:T(8,128)(2,1)} %convolution_convert_fusion.3, f32[512]{0:T(512)S(1)} %negate_multiply_fusion.1, f32[512]{0:T(512)S(1)} %negate_multiply_fusion.2, s32[512]{0:T(512)S(1)} %get-tuple-element.121, ...), kind=kOutput, calls=%fused_computation.54 | convolution fusion | flops 2439643136 | bytes 5518336 | tf_op jit(solution)/shard_map/dot_general | solution.py:995
  352.4 62.5 %last_sums.1 = (f32[8,768]{1,0:T(8,128)S(1)}, bf16[2,2,4,48,384]{4,3,2,1,0:T(8,128)(2,1)S(1)}, bf16[2,2,4,48,384]{4,3,2,1,0:T(8,128)(2,1)S(1)}, bf16[2,2,4,48,384]{4,3,2,1,0:T(8,128)(2,1)S(1)}) custom-call(f32[8,768]{1,0:T(8,128)S(1)} %select_add_fusion.gains, bf16[2,2,4,48,384]{4,3,2,1,0:T(8,128)(2,1)S(1)} %bitcast.128, ...), custom_call_target="tpu_custom_call" | custom-call | tf_op jit(solution)/shard_map/last_sums/pallas_call | solution.py:717
  415.6 2.1 maximum_convert_fusion.2
  (169 shorter events, 33.7 us)
Async XLA Ops:
  0.6 101.3 %copy-start = (bf16[1536,768]{1,0:T(8,128)(2,1)S(1)}, bf16[1536,768]{1,0:T(8,128)(2,1)}, u32[]{:S(2)}) copy-start(bf16[1536,768]{1,0:T(8,128)(2,1)} %param.19) | copy-start | bytes 7077892
  3.6 4.7 %copy-start.25 = (f32[512]{0:T(512)}, f32[512]{0:T(512)S(1)}, u32[]{:S(2)}) copy-start(f32[512]{0:T(512)S(1)} %broadcast_multiply_fusion.1) | copy-start | bytes 6148
  3.9 3.2 copy-start.32
  3.9 3.5 copy-start.36
  4.4 5.9 %copy-start.30 = (f32[512]{0:T(512)}, f32[512]{0:T(512)S(1)}, u32[]{:S(2)}) copy-start(f32[512]{0:T(512)S(1)} %fusion.72) | copy-start | bytes 6148
  5.6 2.8 collective-permute-start
  10.6 3.9 copy-start.18
  82.4 3.4 copy-start.7
  82.4 2.3 copy-start.41
  86.0 4.9 %copy-start.15 = (bf16[16,2,32,768]{3,2,0,1:T(8,128)(2,1)}, bf16[16,2,32,768]{3,2,0,1:T(8,128)(2,1)S(1)}, u32[]{:S(2)}) copy-start(bf16[16,2,32,768]{3,2,0,1:T(8,128)(2,1)S(1)} %copy.37) | copy-start | bytes 4718596
  86.9 4.0 collective-permute-start.1
  90.9 3.8 collective-permute-start.4
  94.1 2.5 collective-permute-start.2
  97.3 25.2 %copy-start.20 = (bf16[16,2,32,768]{3,2,1,0:T(8,128)(2,1)}, bf16[16,2,32,768]{3,2,1,0:T(8,128)(2,1)S(1)}, u32[]{:S(2)}) copy-start(bf16[16,2,32,768]{3,2,1,0:T(8,128)(2,1)S(1)} %pad_maximum_fusion.1) | copy-start | bytes 4718596
  118.4 4.1 copy-start.44
  128.3 4.6 %copy-start.17 = (bf16[1024,1536]{1,0:T(8,128)(2,1)S(1)}, bf16[1024,1536]{1,0:T(8,128)(2,1)}, u32[]{:S(2)}) copy-start(bf16[1024,1536]{1,0:T(8,128)(2,1)} %multiply_convert_fusion) | copy-start | bytes 9437188
  137.0 7.1 %collective-permute-start.5 = (bf16[512,768]{1,0:T(8,128)(2,1)S(1)}, bf16[512,768]{1,0:T(8,128)(2,1)S(1)}, u32[]{:S(2)}, u32[]{:S(2)}) collective-permute-start(bf16[512,768]{1,0:T(8,128)(2,1)S(1)} %dynamic-slice_bitcast_fusion.1), channel_id=1, source_target_pairs={{0,1},{1,0},{2,3},{3,2},{4,5},{5,4},{6,7},{7,6},{8,9},{9,8},{10,11... | collective-permute-start | bytes 2359304 | tf_op jit(solution)/shard_map/ppermute | solution.py:868
  137.6 10.7 %collective-permute-start.3 = (bf16[512,768]{1,0:T(8,128)(2,1)S(1)}, bf16[512,768]{1,0:T(8,128)(2,1)S(1)}, u32[]{:S(2)}, u32[]{:S(2)}) collective-permute-start(bf16[512,768]{1,0:T(8,128)(2,1)S(1)} %dynamic-slice_bitcast_fusion.2), channel_id=1, source_target_pairs={{0,1},{1,0},{2,3},{3,2},{4,5},{5,4},{6,7},{7,6},{8,9},{9,8},{10,11... | collective-permute-start | bytes 2359304 | tf_op jit(solution)/shard_map/ppermute | solution.py:868
  147.7 3.2 collective-permute-start.6
  154.4 2.9 copy-start.8
  154.4 2.9 copy-start.10
  320.0 5.9 %copy-start.39 = (bf16[3,768,384]{2,1,0:T(8,128)(2,1)S(1)}, bf16[3,768,384]{2,1,0:T(8,128)(2,1)}, u32[]{:S(2)}) copy-start(bf16[3,768,384]{2,1,0:T(8,128)(2,1)} %param.16) | copy-start | bytes 5308420
  331.4 11.4 %collective-permute-start.7 = (bf16[512,768]{1,0:T(8,128)(2,1)}, bf16[512,768]{1,0:T(8,128)(2,1)S(1)}, u32[]{:S(2)}, u32[]{:S(2)}) collective-permute-start(bf16[512,768]{1,0:T(8,128)(2,1)} %dynamic-slice_bitcast_fusion), channel_id=1, source_target_pairs={{0,1},{1,0},{2,3},{3,2},{4,5},{5,4},{6,7},{7,6},{8,9},{9,8},{10,11... | collective-permute-start | bytes 2359304 | tf_op jit(solution)/shard_map/ppermute | solution.py:868
  335.5 4.6 %copy-start.23 = (bf16[2,2,4,48,768]{4,3,2,1,0:T(8,128)(2,1)S(1)}, bf16[2,2,4,48,768]{4,3,2,1,0:T(8,128)(2,1)}, u32[]{:S(2)}) copy-start(bf16[2,2,4,48,768]{4,3,2,1,0:T(8,128)(2,1)} %get-tuple-element.79) | copy-start | bytes 3538948
  335.5 4.6 %copy-start.24 = (bf16[2,2,4,48,768]{4,3,2,1,0:T(8,128)(2,1)S(1)}, bf16[2,2,4,48,768]{4,3,2,1,0:T(8,128)(2,1)}, u32[]{:S(2)}) copy-start(bf16[2,2,4,48,768]{4,3,2,1,0:T(8,128)(2,1)} %get-tuple-element.80) | copy-start | bytes 3538948
  340.1 2.7 copy-start.12
  340.1 3.2 copy-start.14
  340.1 3.1 copy-start.26
  340.1 3.1 copy-start.29
  340.1 3.1 copy-start.31
  345.9 6.6 %collective-permute-start.8 = (f32[8,768]{1,0:T(8,128)S(1)}, f32[8,768]{1,0:T(8,128)S(1)}, u32[]{:S(2)}, u32[]{:S(2)}) collective-permute-start(f32[8,768]{1,0:T(8,128)S(1)} %concatenate.9), channel_id=1, source_target_pairs={{0,1},{1,0},{2,3},{3,2},{4,5},{5,4},{6,7},{7,6},{8,9},{9,8},{10,11... | collective-permute-start | bytes 73736 | tf_op jit(solution)/shard_map/ppermute | solution.py:868
  415.6 2.7 copy-start.1
  (23 other events, 33.7 us)

commit v4 on v2

--- a/solution.py
+++ b/solution.py
@@ -189,21 +189,132 @@
     return me // stride * stride, me % stride
 
 
-def meet_group():
-    base, place = group_place(BRANCHES - 1)
-    size = 2 ** (BRANCHES - 1)
+def meet(*axes):
     barrier = pltpu.get_barrier_semaphore()
-
-    @pl.loop(1, size)
-    def _(step):
-        pl.semaphore_signal(
-            barrier,
-            inc=1,
-            device_id={"seq": base + (place + step) % size},
+    count = 0
+    for axis in axes:
+        size = lax.axis_size(axis)
+        me = lax.axis_index(axis)
+
+        @pl.loop(1, size)
+        def _(step):
+            pl.semaphore_signal(
+                barrier, inc=1, device_id={axis: (me + step) % size}, device_id_type=pl.DeviceIdType.MESH
+            )
+
+        count += size - 1
+    pl.semaphore_wait(barrier, count)
+
+
+class Reduction:
+    STEPS = 7
+
+    def __init__(self, order, total, half, quarter, others, send, recv):
+        self.total = total
+        self.half, self.quarter, self.others = half, quarter, others
+        self.send, self.recv = send, recv
+        me = lax.axis_index("seq")
+        self.rest = lax.axis_size("seq") // 4
+        self.me = me
+        bits = (me % 2, me // 2 % 2)
+        self.bits = [bits[bit] for bit in order]
+        self.partners = [me + (1 - 2 * bits[bit]) * 2**bit for bit in order]
+        self.place = me // 4
+
+    def copy(self, source, target, device, sem):
+        return pltpu.make_async_remote_copy(
+            src_ref=source,
+            dst_ref=target,
+            send_sem=self.send.at[sem],
+            recv_sem=self.recv.at[sem],
+            device_id={"seq": device},
             device_id_type=pl.DeviceIdType.MESH,
         )
 
-    pl.semaphore_wait(barrier, size - 1)
+    def copies(self, number):
+        one, two = self.bits
+        rest = self.rest
+        others = []
+        for step in range(1, rest):
+            place = (self.place + step) % rest
+            others.append((step, place, place * 4 + self.me % 4))
+        if number == 0:
+            return [self.copy(self.total.at[1 - one], self.half, self.partners[0], 0)]
+        if number == 1:
+            return [self.copy(self.half.at[1 - two], self.quarter, self.partners[1], 1)]
+        if number == 2:
+            return [
+                self.copy(self.quarter.at[place], self.others.at[step - 1], device, 1 + step)
+                for step, place, device in others
+            ]
+        if number == 3:
+            block = self.total.at[one, two, self.place]
+            return [self.copy(block, block, device, rest + step) for step, place, device in others]
+        if number == 4:
+            block = self.total.at[one, two]
+            return [self.copy(block, block, self.partners[1], 2 * rest)]
+        if number == 5:
+            block = self.total.at[one]
+            return [self.copy(block, block, self.partners[0], 2 * rest + 1)]
+        return []
+
+    def step(self, number):
+        one, two = self.bits
+        rest = self.rest
+        if number > 0:
+            for copy in self.copies(number - 1):
+                copy.wait()
+        if number == 1:
+
+            @pl.loop(0, 2 * rest)
+            def _(i):
+                j, z = i // rest, i % rest
+                mine = self.total[one, j, z].astype(F32)
+                self.half[j, z] = (mine + self.half[j, z].astype(F32)).astype(BF)
+
+        elif number == 2:
+
+            @pl.loop(0, rest)
+            def _(z):
+                mine = self.half[two, z].astype(F32)
+                self.quarter[z] = (mine + self.quarter[z].astype(F32)).astype(BF)
+
+        elif number == 3:
+            mine = self.quarter[self.place].astype(F32)
+            for step in range(1, rest):
+                mine = mine + self.others[step - 1].astype(F32)
+            self.total[one, two, self.place] = mine.astype(BF)
+        for copy in self.copies(number):
+            copy.start()
+
+    @staticmethod
+    def scratch(size, rows, columns):
+        rest = size // 4
+        count = 2 * rest + 2
+        return [
+            pltpu.VMEM((2, rest, rows, columns), BF),
+            pltpu.VMEM((rest, rows, columns), BF),
+            pltpu.VMEM((rest - 1, rows, columns), BF),
+            pltpu.SemaphoreType.DMA((count,)),
+            pltpu.SemaphoreType.DMA((count,)),
+        ]
+
+
+def reduction_parts(value, size):
+    rows, columns = value.shape
+    return value.reshape(2, 2, size // 4, rows // size, columns)
+
+
+def reduction_whole(value):
+    return value.reshape(-1, value.shape[-1])
+
+
+def make_reductions(orders, totals, scratch):
+    out = []
+    for order, total in zip(orders, totals):
+        out.append(Reduction(order, total, *scratch[:5]))
+        scratch = scratch[5:]
+    return out
 
 
 def group_copies(branch, source, target, source_block, send_sems, recv_sems, local_sem):
@@ -237,7 +348,7 @@
     outs, refs = refs[:count], refs[count:]
     x, q_aug, in_send, in_recv, in_local, out_send, out_recv, out_local = refs
     tile = 256
-    meet_group()
+    meet("seq")
     coming = {}
     for branch in range(1, BRANCHES):
         coming[branch] = group_copies(
@@ -347,7 +458,7 @@
     return results[0], results[1 : 1 + len(gots)], results[1 + len(gots) :]
 
 
-def backward_unit(x, g, q_aug, gk, gv, base, queries, tile, put):
+def backward_unit(x, g, q_aug, gk, gv, result, base, queries, tile):
     if isinstance(base, int):
         lanes = slice(base, base + queries)
     else:
@@ -366,13 +477,16 @@
     q_rows = jnp.concatenate([q, jnp.zeros((BIT_ROWS, queries), BF)], axis=0).T
     g_all = g[:, lanes]
     g_rows = g_all.T
+    if queries < SEG0:
+        result[0:E, :] = jnp.zeros((E, SEG0), BF)
     for step in range(queries // tile):
         column = step * tile
         span = slice(column, column + tile)
         p = jnp.exp2(jnp.dot(k_rows, q_aug[:, span], preferred_element_type=F32))
         gs = p * jnp.dot(v_rows, g_all[:, span], preferred_element_type=F32)
         p, gs = p.astype(BF), gs.astype(BF)
-        put(column, jnp.dot(k_aug, gs, preferred_element_type=F32)[:E].astype(BF))
+        target = span if isinstance(base, int) else pl.ds(pl.multiple_of(base + column, 128), tile)
+        result[0:E, target] = jnp.dot(k_aug, gs, preferred_element_type=F32)[:E].astype(BF)
         new_k = jnp.dot(gs, q_rows[span], preferred_element_type=F32)
         new_v = jnp.dot(p, g_rows[span], preferred_element_type=F32)
         if step == 0:
@@ -381,96 +495,372 @@
         else:
             gk[...] += new_k
             gv[...] += new_v
-    return (gk[...].T[:E] * LN2).astype(BF), gv[...].T[:E].astype(BF)
-
-
-def exchange_backward_kernel(heads, own, own_g, *refs):
-    count = BRANCHES - 1
-    units_in, refs = refs[:count], refs[count:]
-    sends, refs = refs[:count], refs[count:]
-    first, refs = refs[0], refs[1:]
-    backs, refs = refs[:count], refs[count:]
-    gots, refs = refs[:count], refs[count:]
-    outs, refs = refs[:count], refs[count:]
-    x, g, q_aug, gk, gv, in_send, in_recv, in_local, out_send, out_recv, out_local = refs
+    result[E : 2 * E, :] = (gk[...].T[:E] * LN2).astype(BF)
+    result[2 * E :, :] = gv[...].T[:E].astype(BF)
+
+
+def stream_orders(count):
+    return [((0, 1), (1, 0))[s % 2] for s in range(count)]
+
+
+class Names:
+    def __init__(self, refs):
+        self.refs = list(refs)
+
+    def take(self, count):
+        taken, self.refs = self.refs[:count], self.refs[count:]
+        return taken
+
+    def one(self):
+        return self.take(1)[0]
+
+
+EARLY = [
+    (6, 1, 1),
+    (7, 0, 1),
+    (9, 1, 2),
+    (9, 0, 2),
+    (10, 3, 1),
+    (11, 2, 1),
+    (11, 4, 1),
+    (11, 1, 3),
+    (11, 0, 3),
+    (13, 3, 2),
+    (13, 1, 4),
+    (13, 0, 4),
+    (14, 2, 2),
+    (14, 4, 2),
+    (15, 3, 3),
+    (15, 1, 5),
+    (15, 0, 5),
+]
+
+
+def backward_kernel(heads, streams, *refs):
+    branches = BRANCHES - 1
+    names = Names(refs)
+    starts, own, own_g = names.take(3)
+    units_in, sends, parts = names.take(branches), names.take(branches), names.take(streams)
+    normed, in_proj, x_rows, grad_hidden, gain, gains_two = names.take(6)
+    totals, in_totals = names.take(streams), names.take(3)
+    grad_tokens, gains_out = names.take(2)
+    first = names.one()
+    backs, gots, outs = names.take(branches), names.take(branches), names.take(branches)
+    x, g, q_aug, gk, gv, result = names.take(6)
+    total, grads, grads_t, normed_t, spread_rows, head_send, head_recv = names.take(7)
+    gain_head, gain_one, gain_two, gain_rest = names.take(4)
+    in_send, in_recv, in_local, out_send, out_recv, out_local = names.take(6)
+    part_sem, head_sems, gain_sems = names.take(3)
+    orders = stream_orders(streams)
+    reductions = make_reductions(orders, totals, names.take(5 * streams))
+    lasts = make_reductions([(1, 0), (0, 1), (1, 0)], in_totals, names.take(15))
+
+    shapes = [branch_shape(b, heads) for b in range(BRANCHES)]
+    size, head_size = lax.axis_size("seq"), lax.axis_size("head")
+    me, me_head = lax.axis_index("seq"), lax.axis_index("head")
+    rest = size // 4
     tile = 256
-    meet_group()
-    coming = {}
-    for branch in range(1, BRANCHES):
-        coming[branch] = group_copies(
+    per_slot = x_rows.shape[0] // SLOTS
+    width = x_rows.shape[1]
+
+    fills = [pltpu.make_async_copy(parts[s], totals[s], part_sem.at[s]) for s in range(streams)]
+    for fill in fills:
+        fill.start()
+    meet("seq", "head")
+
+    def coming(branch):
+        return group_copies(
             branch, sends[branch - 1], gots[branch - 1], lambda m: m, in_send, in_recv, in_local
         )
-        for copy in coming[branch]:
-            copy.start()
-
-    def own_heads(low, high):
-        @pl.loop(low, high)
-        def _(head):
-            x[...] = own[0, head]
-            g[...] = own_g[0, head]
-
-            def put(column, value):
-                first[0, head, :E, column : column + tile] = value
-
-            k_cols, v_cols = backward_unit(x, g, q_aug, gk, gv, 0, SEG0, tile, put)
-            first[0, head, E : 2 * E, :] = k_cols
-            first[0, head, 2 * E :, :] = v_cols
-
-    own_heads(0, heads // 2)
-    leaving = []
-    for branch in range(1, BRANCHES):
-        stride, lanes, units, split = branch_shape(branch, heads)
-        got, out, unit_in = gots[branch - 1], outs[branch - 1], units_in[branch - 1]
-        for copy in coming[branch]:
-            copy.wait()
-        queries = SEG0 // split
-        base = 0 if split == 1 else lax.axis_index("seq") % split * queries
-
-        @pl.loop(0, units)
-        def _(unit):
-            load_unit(unit_in, unit, lanes, x)
-            load_unit(got, unit, lanes, g)
-            if split == 1:
-
-                def put(column, value):
-                    store_unit(out, unit, slice(0, E), value, column, value.shape[1])
-
-            else:
-                empty = jnp.zeros((E, 128), BF)
-                for block in range(SEG0 // 128):
-                    store_unit(out, unit, slice(0, E), empty, block * 128, 128)
-
-                def put(column, value):
-                    width = out.shape[-1]
-                    for start in range(0, value.shape[1], width):
-                        block = (base + column + start) // width
-                        out[block, unit, :E, :] = value[:, start : start + width]
-
-            k_cols, v_cols = backward_unit(x, g, q_aug, gk, gv, base, queries, min(tile, queries), put)
-            store_unit(out, unit, slice(E, 2 * E), k_cols, 0, SEG0)
-            store_unit(out, unit, slice(2 * E, 3 * E), v_cols, 0, SEG0)
-
-        per = out.shape[-1] // lanes
-        copies = group_copies(
+
+    def leaving(branch):
+        out = outs[branch - 1]
+        per = out.shape[-1] // shapes[branch][1]
+        return group_copies(
             branch, out, backs[branch - 1], lambda m: m // per, out_send, out_recv, out_local
         )
-        for copy in copies:
+
+    for branch in range(1, BRANCHES):
+        for copy in coming(branch):
             copy.start()
-        leaving += copies
-    own_heads(heads // 2, heads)
-    for copy in leaving:
-        copy.wait()
-
-
-def exchange_backward(heads, own, own_g, units, sends):
-    backs = send_shapes(heads, 3 * E)[0]
-    first = jax.ShapeDtypeStruct((1, heads, 3 * E, SEG0), BF)
+    for s in range(streams):
+        fills[s].wait()
+        reductions[s].step(0)
+
+    def split_branch(branch):
+        stride, lanes, units, split = shapes[branch]
+        queries = SEG0 // split
+        for copy in coming(branch):
+            copy.wait()
+        load_unit(units_in[branch - 1], 0, lanes, x)
+        load_unit(gots[branch - 1], 0, lanes, g)
+        backward_unit(x, g, q_aug, gk, gv, result, me % split * queries, queries, min(tile, queries))
+        store_unit(outs[branch - 1], 0, slice(None), result, 0, SEG0)
+
+    runs, at = [(0, 0, 0, heads // 2)], heads // 2
+    split_at = None
+    for branch in range(1, BRANCHES):
+        if shapes[branch][3] == 1:
+            runs.append((branch, at, 0, shapes[branch][2]))
+            at += shapes[branch][2]
+    split_at = at
+    runs.append((0, at, heads // 2, heads - heads // 2))
+    blocks = at + heads - heads // 2
+    plan = {}
+    for block, stream, step in EARLY:
+        if stream < streams:
+            plan.setdefault(block * blocks // 16, []).append((stream, step))
+
+    @pl.loop(0, blocks)
+    def _(block):
+        for after, events in plan.items():
+
+            @pl.when(block == after)
+            def _(events=events):
+                for stream, step in events:
+                    reductions[stream].step(step)
+
+        @pl.when(block == split_at)
+        def _():
+            for branch in range(1, BRANCHES):
+                if shapes[branch][3] > 1:
+                    split_branch(branch)
+                    for copy in leaving(branch):
+                        copy.start()
+
+        for branch, low, unit, count in runs:
+
+            @pl.when((block >= low) & (block < low + count))
+            def _(branch=branch, low=low, unit=unit):
+                if branch == 0:
+                    x[...] = own[0, block - low + unit]
+                    g[...] = own_g[0, block - low + unit]
+                else:
+
+                    @pl.when(block == low)
+                    def _():
+                        for copy in coming(branch):
+                            copy.wait()
+
+                    load_unit(units_in[branch - 1], block - low, shapes[branch][1], x)
+                    load_unit(gots[branch - 1], block - low, shapes[branch][1], g)
+
+        backward_unit(x, g, q_aug, gk, gv, result, 0, SEG0, tile)
+        for branch, low, unit, count in runs:
+
+            @pl.when((block >= low) & (block < low + count))
+            def _(branch=branch, low=low, unit=unit, count=count):
+                if branch == 0:
+                    first[block - low + unit] = result[...]
+                else:
+                    store_unit(outs[branch - 1], block - low, slice(None), result, 0, SEG0)
+
+                    @pl.when(block == low + count - 1)
+                    def _():
+                        for copy in leaving(branch):
+                            copy.start()
+
+    for branch in range(1, BRANCHES):
+        for copy in leaving(branch):
+            copy.wait()
+
+    later = []
+    done = {s: 1 for s in range(streams)}
+    for _, stream, step in EARLY:
+        if stream < streams:
+            done[stream] = step + 1
+    for step in range(Reduction.STEPS):
+        later += [(s, step) for s in (1, 0, 3, 2, 4) if s < streams and step >= done[s]]
+
+    def advance(count):
+        for stream, step in later[:count]:
+            reductions[stream].step(step)
+        del later[:count]
+
+    @pl.loop(0, heads)
+    def _(head):
+        total[...] = first[head].astype(F32)
+        for branch in range(1, BRANCHES):
+            stride, lanes, per, split = shapes[branch]
+            back, start = backs[branch - 1], starts[branch, head]
+            if split == 1:
+                value = back[head // per, head % per].astype(F32)
+            else:
+                value = back[head * split, 0].astype(F32)
+                for copy in range(1, split):
+                    value = value + back[head * split + copy, 0].astype(F32)
+            if lanes < 128:
+                share = 128 // lanes
+                value = moved_part(value, lanes, me % share, start % share)
+                start = start // share
+                lanes = 128
+            for block in range(SEG0 // lanes):
+                span = slice(block * lanes, (block + 1) * lanes)
+                total[:, span] += jnp.where(start == block, value, 0.0)
+        grads[0, head] = (total[0:E, :] * E ** (-0.5)).astype(BF)
+        grads[1, head] = total[E : 2 * E, :].astype(BF)
+        grads[2, head] = total[2 * E :, :].astype(BF)
+
+    normed_t[...] = normed[...].T
+    rows_in = in_totals[0].shape[3]
+    chunk = width // 2
+    for j in range(3):
+        grads_t[j] = grads[j].reshape(heads * E, SEG0).T
+        for half in range(2):
+            value = jnp.dot(
+                normed_t[half * chunk : (half + 1) * chunk], grads_t[j], preferred_element_type=F32
+            ).astype(BF)
+            for part in range(chunk // rows_in):
+                index = half * (chunk // rows_in) + part
+                in_totals[j][index // (2 * rest), index // rest % 2, index % rest] = value[
+                    part * rows_in : (part + 1) * rows_in
+                ]
+        lasts[j].step(0)
+    advance(3)
+
+    for half in range(2):
+        rows = slice(half * SEG0 // 2, (half + 1) * SEG0 // 2)
+        value = jnp.zeros((SEG0 // 2, width), F32)
+        for j in range(3):
+            value = value + lax.dot_general(
+                grads_t[j, rows], in_proj[j], (((1,), (1,)), ((), ())), preferred_element_type=F32
+            )
+        value = value.astype(BF)
+        for slot in range(SLOTS // 2):
+            for device in range(head_size):
+                begin = (slot * head_size + device) * per_slot
+                place = (half * SLOTS // 2 + slot) * per_slot
+                head_send[device, place : place + per_slot] = value[begin : begin + per_slot]
+    swaps = []
+    for step in range(1, head_size):
+        device = (me_head + step) % head_size
+        swaps.append(
+            pltpu.make_async_remote_copy(
+                src_ref=head_send.at[device],
+                dst_ref=head_recv.at[step - 1],
+                send_sem=head_sems.at[0, step - 1],
+                recv_sem=head_sems.at[1, step - 1],
+                device_id={"head": device},
+                device_id_type=pl.DeviceIdType.MESH,
+            )
+        )
+        swaps[-1].start()
+    advance(3)
+    for swap in swaps:
+        swap.wait()
+
+    gain_head[me_head] = jnp.zeros(gains_out.shape, F32)
+    gain_head[me_head, 2:4] = gains_two[...]
+
+    @pl.loop(0, SLOTS)
+    def _(slot):
+        rows = pl.ds(pl.multiple_of(slot * per_slot, per_slot), per_slot)
+        grad = head_send[me_head, rows].astype(F32)
+        for step in range(1, head_size):
+            grad = grad + head_recv[step - 1, rows].astype(F32)
+        values = x_rows[rows]
+        centred = values - jnp.mean(values, axis=-1, keepdims=True)
+        scale = lax.rsqrt(jnp.mean(centred * centred, axis=-1, keepdims=True) + EPS)
+        unit = centred * scale
+        scaled = grad * gain[...]
+        inner = jnp.mean(scaled * unit, axis=-1, keepdims=True)
+        out = grad_hidden[rows] + scale * (scaled - jnp.mean(scaled, axis=-1, keepdims=True) - unit * inner)
+        place = slot % 2 * 8 + slot // 2 % 2 * 4 + slot // 4 % 2 * 2 + slot // 8
+        for column in range(width // 128):
+            lanes = slice(column * 128, (column + 1) * 128)
+            spread_rows[column, pl.ds(place, per_slot, stride=SLOTS), :] = out[:, lanes]
+        gain_head[me_head, 0:1] += jnp.sum(grad * unit, axis=0, keepdims=True)
+        gain_head[me_head, 1:2] += jnp.sum(grad, axis=0, keepdims=True)
+
+    for column in range(width // 128):
+        grad_tokens[:, column * 128 : (column + 1) * 128] = spread_rows[column]
+
+    def gain_copy(source, target, axis, device, sem):
+        made = pltpu.make_async_remote_copy(
+            src_ref=source,
+            dst_ref=target,
+            send_sem=gain_sems.at[0, sem],
+            recv_sem=gain_sems.at[1, sem],
+            device_id={axis: device},
+            device_id_type=pl.DeviceIdType.MESH,
+        )
+        made.start()
+        return made
+
+    mine = gain_head.at[me_head]
+    swaps = [
+        gain_copy(mine, mine, "head", (me_head + step) % head_size, step - 1) for step in range(1, head_size)
+    ]
+    advance(3)
+    for swap in swaps:
+        swap.wait()
+    value = gain_head[0]
+    for device in range(1, head_size):
+        value = value + gain_head[device]
+    gain_one[0] = value
+    swap = gain_copy(gain_one.at[0], gain_one.at[1], "seq", me + 1 - 2 * (me % 2), head_size)
+    for last in lasts:
+        last.step(1)
+    advance(2)
+    swap.wait()
+    gain_two[0] = gain_one[0] + gain_one[1]
+    swap = gain_copy(gain_two.at[0], gain_two.at[1], "seq", me + 2 - 4 * (me // 2 % 2), head_size + 1)
+    advance(2)
+    for last in lasts:
+        last.step(2)
+    swap.wait()
+    spot = me // 4
+    gain_rest[spot] = gain_two[0] + gain_two[1]
+    block = gain_rest.at[spot]
+    swaps = [
+        gain_copy(block, block, "seq", (spot + step) % rest * 4 + me % 4, head_size + 1 + step)
+        for step in range(1, rest)
+    ]
+    advance(2)
+    for last in lasts:
+        last.step(3)
+    for swap in swaps:
+        swap.wait()
+    value = gain_rest[0]
+    for z in range(1, rest):
+        value = value + gain_rest[z]
+    gains_out[...] = value
+    advance(2)
+    for last in lasts:
+        last.step(4)
+    advance(2)
+    for last in lasts:
+        last.step(5)
+    advance(len(later))
+    for last in lasts:
+        last.step(6)
+
+
+def backward(heads, starts, own, own_g, units, sends, terms, normed, in_proj, x_rows, grad_hidden, gain, gains_two):
+    size, head_size = lax.axis_size("seq"), lax.axis_size("head")
+    rest = size // 4
+    rows, width = x_rows.shape
+    parts = [reduction_parts(term, size) for term in terms]
+    in_shape = (2, 2, rest, width // size, heads * E)
+    scratch = []
+    for part in parts:
+        scratch += Reduction.scratch(size, *part.shape[-2:])
+    for _ in range(3):
+        scratch += Reduction.scratch(size, *in_shape[-2:])
+    streams = len(parts)
     results = pl.pallas_call(
-        partial(exchange_backward_kernel, heads),
-        in_specs=vmem_specs(2 + len(units) + len(sends)),
-        out_specs=vmem_specs(1 + len(backs)),
-        out_shape=[first] + backs,
-        scratch_shapes=[pltpu.VMEM(shape.shape, BF) for shape in send_shapes(heads, ROWS_OUT)[0]]
+        partial(backward_kernel, heads, streams),
+        in_specs=[pl.BlockSpec(memory_space=pltpu.SMEM)]
+        + vmem_specs(2 + len(units) + len(sends))
+        + [pl.BlockSpec(memory_space=pl.ANY)] * streams
+        + vmem_specs(6),
+        out_specs=vmem_specs(streams + 5),
+        out_shape=[jax.ShapeDtypeStruct(part.shape, BF) for part in parts]
+        + [jax.ShapeDtypeStruct(in_shape, BF)] * 3
+        + [jax.ShapeDtypeStruct((rows, width), F32), jax.ShapeDtypeStruct((8, width), F32)],
+        scratch_shapes=[pltpu.VMEM((heads, 3 * E, SEG0), BF)]
+        + [pltpu.VMEM(shape.shape, BF) for shape in send_shapes(heads, 3 * E)[0]]
+        + [pltpu.VMEM(shape.shape, BF) for shape in send_shapes(heads, ROWS_OUT)[0]]
         + [pltpu.VMEM(shape, BF) for shape in out_blocks(heads, 3 * E)]
         + [
             pltpu.VMEM((ROWS_IN, SEG0), BF),
@@ -478,13 +868,34 @@
             pltpu.VMEM((ROWS_OUT, SEG0), BF),
             pltpu.VMEM((SEG0, ROWS_OUT), F32),
             pltpu.VMEM((SEG0, ROWS_OUT), F32),
+            pltpu.VMEM((3 * E, SEG0), BF),
+            pltpu.VMEM((3 * E, SEG0), F32),
+            pltpu.VMEM((3, heads, E, SEG0), BF),
+            pltpu.VMEM((3, SEG0, heads * E), BF),
+            pltpu.VMEM((width, SEG0), BF),
+            pltpu.VMEM((width // 128, rows, 128), F32),
+            pltpu.VMEM((head_size, rows, width), BF),
+            pltpu.VMEM((head_size - 1, rows, width), BF),
+            pltpu.VMEM((head_size, 8, width), F32),
+            pltpu.VMEM((2, 8, width), F32),
+            pltpu.VMEM((2, 8, width), F32),
+            pltpu.VMEM((rest, 8, width), F32),
         ]
-        + exchange_scratch(),
-        compiler_params=params(collective_id=1, has_side_effects=True),
+        + exchange_scratch()
+        + [
+            pltpu.SemaphoreType.DMA((streams,)),
+            pltpu.SemaphoreType.DMA((2, head_size - 1)),
+            pltpu.SemaphoreType.DMA((2, head_size + 1 + rest)),
+        ]
+        + scratch,
+        compiler_params=pltpu.CompilerParams(
+            vmem_limit_bytes=60 * 2**20, collective_id=1, has_side_effects=True
+        ),
         cost_estimate=unit_cost(2 * heads, 5),
-        name="exchange_backward",
-    )(own, own_g, *units, *sends)
-    return results[0], results[1:]
+        name="backward",
+    )(starts, own, own_g, *units, *sends, *parts, normed, in_proj, x_rows, grad_hidden, gain, gains_two)
+    sums = [reduction_whole(total) for total in results[: streams + 3]]
+    return sums[:streams], sums[streams:], results[-2], results[-1]
 
 
 def placed_part(value, count, start, place):
@@ -579,43 +990,6 @@
     )(starts, place, grad, merged, lse)
 
 
-def gather_kernel(heads, starts, place, first, *refs):
-    seconds, (out, total) = refs[: BRANCHES - 1], refs[BRANCHES - 1 :]
-    head = pl.program_id(0)
-    total[...] = first[0, 0].astype(F32)
-    for branch in range(1, BRANCHES):
-        got = seconds[branch - 1]
-        count = branch_shape(branch, heads)[1]
-        start = starts[branch, head]
-        lanes = aligned(start, count)
-        value = got[0, 0].astype(F32)
-        for copy in range(1, got.shape[0]):
-            value += got[copy, 0].astype(F32)
-        value = placed_part(value, count, start, place[0])[0]
-        total[:, lanes] += value
-    out[0] = (total[0:E, :] * E ** (-0.5)).astype(BF)
-    out[1] = total[E : 2 * E, :].astype(BF)
-    out[2] = total[2 * E :, :].astype(BF)
-
-
-def gather_heads(heads, starts, place, first, seconds):
-    span = first.shape[-1]
-    return pl.pallas_call(
-        partial(gather_kernel, heads),
-        grid_spec=pltpu.PrefetchScalarGridSpec(
-            num_scalar_prefetch=2,
-            grid=(heads,),
-            in_specs=[pl.BlockSpec((1, 1, 3 * E, span), lambda h, s, t: (0, h, 0, 0))]
-            + send_shapes(heads, 3 * E)[1],
-            out_specs=pl.BlockSpec((3, E, span), lambda h, s, t: (0, h, 0)),
-            scratch_shapes=[pltpu.VMEM((3 * E, span), F32)],
-        ),
-        out_shape=jax.ShapeDtypeStruct((3, heads * E, span), BF),
-        compiler_params=params(),
-        name="gather_heads",
-    )(starts, place, first, *seconds)
-
-
 def rolled(value, step):
     size = lax.axis_size("head")
     return lax.ppermute(value, "head", [(s, (s + step) % size) for s in range(size)])
@@ -639,14 +1013,6 @@
         sent = lax.dynamic_index_in_dim(parts, (me + step) % size, 0, keepdims=False)
         total = total + rolled(sent, step).astype(F32)
     return total
-
-
-def sum_seq(value):
-    size = lax.axis_size("seq")
-    got = lax.all_to_all(value.astype(BF), "seq", 0, 0, tiled=True)
-    mine = got.reshape((size, value.shape[0] // size) + value.shape[1:]).astype(F32).sum(0)
-    full = jnp.broadcast_to(mine.astype(BF)[None], (size,) + mine.shape)
-    return lax.all_to_all(full, "seq", 0, 0, tiled=True).reshape(value.shape).astype(F32)
 
 
 def local(
@@ -720,10 +1086,20 @@
     block_rows = hidden_one + sum_rows(device_parts(down_part))
     block_out = jnp.dot(order.T, block_rows.astype(BF), preferred_element_type=F32).astype(BF)
 
-    grad_down = jnp.einsum("tf,td->fd", hidden, cot_all, preferred_element_type=F32).astype(BF)
+    chunks = max(1, up_proj.shape[1] // width)
+
+    def columns(values):
+        return jnp.split(values, chunks, axis=1)
+
+    grad_down = [
+        jnp.einsum("tf,td->fd", part, cot_all, preferred_element_type=F32).astype(BF) for part in columns(hidden)
+    ]
     grad_act = jnp.einsum("td,fd->tf", cot_all, down_proj, preferred_element_type=F32)
     grad_pre = gelu_pull(grad_act)[0].astype(BF)
-    grad_up = jnp.einsum("td,tf->df", gathered_two, grad_pre, preferred_element_type=F32).astype(BF)
+    grad_up = [
+        jnp.einsum("td,tf->df", gathered_two, part, preferred_element_type=F32).astype(BF)
+        for part in columns(grad_pre)
+    ]
     norm_part = jnp.einsum("tf,df->td", grad_pre, up_proj, preferred_element_type=F32).astype(BF)
     grad_normed_two = sum_rows(device_parts(norm_part))
     pull_two = jax.vjp(norm_rows, hidden_one, second_gain, second_shift)[1]
@@ -734,33 +1110,19 @@
     grad_merged = jnp.einsum("td,cd->ct", grad_attn, out_proj, preferred_element_type=F32)
 
     own_g, *sends_g = spread_heads(heads, starts, place, grad_merged, merged, lse)
-    first_grad, grads = exchange_backward(heads, own, own_g, units, sends_g)
-    grad_qkv = gather_heads(heads, starts, place, first_grad, grads)
-
-    grad_in = jnp.einsum("td,jct->jdc", gathered_one, grad_qkv, preferred_element_type=F32)
-    one_part = jnp.einsum("jct,jdc->td", grad_qkv, in_proj, preferred_element_type=F32).astype(BF)
-    grad_normed_one = sum_rows(device_parts(one_part))
-    pull_one = jax.vjp(norm_rows, x_rows, first_gain, first_shift)[1]
-    grad_ln_one, grad_gain_one, grad_shift_one = pull_one(grad_normed_one)
-    grad_tokens = jnp.dot(
-        order.T.astype(F32),
-        grad_hidden_one + grad_ln_one,
-        precision=lax.Precision.HIGHEST,
-        preferred_element_type=F32,
+    terms = [term for pair in zip(grad_up, grad_down) for term in pair] + [grad_out]
+    gains_two = jnp.stack([grad_gain_two, grad_shift_two])
+    sums, grad_in, grad_tokens, gains = backward(
+        heads, starts, own, own_g, units, sends_g, terms,
+        gathered_one, in_proj, x_rows, grad_hidden_one, first_gain[None, :], gains_two,
     )
-
-    middle = lax.psum((grad_out, grad_up, grad_down), "seq")
-    flat_in = grad_in.reshape(3 * width, heads * E)
-    grad_in = sum_seq(flat_in).reshape(3, width, heads * E)
-    gains = jnp.stack([grad_gain_one, grad_shift_one, grad_gain_two, grad_shift_two])
-    gains = lax.psum(gains, ("seq", "head"))
     return (
         block_out,
         grad_tokens,
-        grad_in,
-        middle[0].astype(F32),
-        middle[1].astype(F32),
-        middle[2].astype(F32),
+        jnp.stack(grad_in).astype(F32),
+        sums[-1].astype(F32),
+        jnp.concatenate(sums[:-1:2], axis=1).astype(F32),
+        jnp.concatenate(sums[1:-1:2], axis=0).astype(F32),
         gains[0],
         gains[1],
         gains[2],

time: 507 us -> 391 us (0.77)
  Pallas kernels: 143 us -> 279 us
  waiting for transfers between devices: 122 us -> 0.02 us
  blocking collectives: 62.8 us -> 0 us
  starting transfers between devices: 30.6 us -> 1.74 us
  between operations: 15.5 us -> 1.69 us
  matrix products: 64.2 us -> 51.8 us
  other arithmetic: 37.5 us -> 28.9 us
    pallas_call x2 -> x1, Pallas kernels: 72.8 us -> 209 us  [backward(): pl.pallas_call(partial(backward_kernel, heads, streams), in_specs=[pl.Blo...]
    psum x1 -> x0, waiting for transfers between devices: 86.6 us -> none  [local(): middle = lax.psum((grad_out, grad_up, grad_down), 'seq')]
    psum x1 -> x0, blocking collectives: 62.8 us -> none  [local(): gains = lax.psum(gains, ('seq', 'head'))]
    all_to_all x2 -> x0, waiting for transfers between devices: 33.7 us -> none  [the longest x1 33.7 us: sum_seq(): got = lax.all_to_all(value.astype(BF), 'seq', 0, 0, tiled=True)]
    all_to_all x2 -> x0, starting transfers between devices: 28.5 us -> none  [the longest x1 24.1 us: sum_seq(): lax.all_to_all(full, 'seq', 0, 0, tiled=True).reshape(value.shape)]
    dot_general x5 -> x4, matrix products: 21 us -> 9.97 us  [the longest x2 5.02 us: local(): jnp.einsum('tf,td->fd', part, cot_all, preferred_element_type=F32)]
    unnamed x118 -> x85, local copies, waits for them, and re-layouts: 15.3 us -> 18 us
  transfers between devices with their start and end apart: 11 -> 7, of which waited for: 4 -> 0; matrix products, arithmetic and copies ran while one was open for 12% -> 6% of each run, Pallas kernels for 0% -> 0%
where the time goes in v4:
time: 391 us; the launch traced here: 386 us
  Pallas kernels  279 us (71%)
  matrix products  51.8 us (13%)
  other arithmetic  28.9 us (7%)
  local copies, waits for them, and re-layouts  22.2 us (6%)
    pallas_call x1, Pallas kernels, backward(): pl.pallas_call(partial(backward_kernel, heads, streams), in_specs=[pl.Blo...  209 us
    pallas_call x1, Pallas kernels, exchange_forward(): pl.pallas_call(partial(exchange_forward_kernel, heads), in_specs=vmem_spe...  61.7 us
    unnamed x85, local copies, waits for them, and re-layouts  18 us
    dot_general x1, matrix products, local(): jnp.einsum('td,fd->tf', cot_all, down_proj, preferred_element_type=F32)  16.4 us
  transfers between devices with their start and end apart: 7, of which 0 were waited for; matrix products, arithmetic and copies ran while one was open for 6% of the time, Pallas kernels for 0%

profile of v4, /device:TPU:0, one launch (start us, length us, event | category | flops | bytes accessed | tf_op | source)
XLA Modules:
  0.0 385.5 jit_solution(7361527845804433684)
XLA Ops:
  0.7 2.9 fusion.92
  4.3 1.2 add_convert_fusion.2
  8.3 1.9 broadcast_select_fusion.7
  10.6 1.9 copy-done.35
  12.4 2.0 fusion.6.proj
  14.5 4.6 %pack_heads.1 = (bf16[1,8,160,1024]{3,2,1,0:T(8,128)(2,1)}, bf16[2,4,160,512]{3,2,1,0:T(8,128)(2,1)S(1)}, bf16[4,2,160,256]{3,2,1,0:T(8,128)(2,1)S(1)}, bf16[8,1...) custom-call(s32[5,8]{1,0:T(8,128)S(1)} %stack.27.starts.refs_0_, s32[1]{0:T(128)} %bitcast.place, ...), custom_call_target="tpu_custom_call" | custom-call | tf_op jit(solution)/shard_map/pack_heads/pallas_call | solution.py:126
  20.1 61.7 %exchange_forward.1 = (bf16[1,8,64,1024]{3,2,1,0:T(8,128)(2,1)S(1)}, bf16[2,4,160,512]{3,2,1,0:T(8,128)(2,1)}, bf16[4,2,160,256]{3,2,1,0:T(8,128)(2,1)S(1)}, bf1...) custom-call(bf16[1,8,160,1024]{3,2,1,0:T(8,128)(2,1)} %get-tuple-ele, ...), custom_call_target="tpu_custom_call" | custom-call | flops 17179869184 | bytes 16384000 | tf_op jit(solution)/shard_map/exchange_forward/pallas_call | solution.py:446
  83.4 2.3 merge_heads.1
  88.7 3.2 convolution_convert_fusion.3
  91.9 2.2 fusion.90
  96.3 1.5 broadcast_select_fusion.3
  98.6 2.1 copy-done.34
  100.7 2.6 fusion.93
  103.3 16.4 %add_convert_fusion = (bf16[1024,1536]{1,0:T(8,128)(2,1)S(1)}, f32[1024,1536]{1,0:T(8,128)S(1)}) fusion(f32[1024,1536]{1,0:T(8,128)S(1)} %fusion.93, bf16[1024,768]{1,0:T(8,128)(2,1)S(1)} %bitcast.121, bf16[1536,768]{1,0:T(8,128)(2,1)S(1)} %copy-done), kind=kOutput, calls=%fused_computation.2 | convolution fusion | flops 2529165312 | bytes 19660800 | tf_op jit(solution)/shard_map/td,fd->tf/dot_general | solution.py:1097
  119.7 3.9 %convolution_convert_fusion.1 = bf16[1024,768]{1,0:T(8,128)(2,1)} fusion(bf16[1024,1536]{1,0:T(8,128)(2,1)S(1)} %get-tuple-element.85, bf16[768,1536]{1,0:T(8,128)(2,1)S(1)} %copy-done.34), kind=kOutput, calls=%fused_computation.28 | convolution fusion | flops 2416705536 | bytes 7077888 | tf_op jit(solution)/shard_map/tf,df->td/dot_general | solution.py:1103
  123.6 2.5 fusion.18
  126.1 3.3 multiply_convert_fusion
  129.4 4.6 %convolution_convert_fusion.2 = bf16[1024,768]{1,0:T(8,128)(2,1)S(1)} fusion(bf16[1024,1536]{1,0:T(8,128)(2,1)} %multiply_convert_fusion, bf16[1536,768]{1,0:T(8,128)(2,1)S(1)} %copy-done), kind=kOutput, calls=%fused_computation.29 | convolution fusion | flops 2416705536 | bytes 7077888 | tf_op jit(solution)/shard_map/dot_general | solution.py:1085
  134.1 2.5 fusion.21
  136.7 1.3 copy-done.21
  140.4 2.5 fusion.24
  142.8 2.5 fusion.27
  146.9 2.5 fusion.87
  150.2 2.8 convolution_convert_fusion.4
  155.0 1.6 convolution_convert_fusion.5
  156.6 1.8 spread_heads.1
  162.3 208.7 %backward.1 = (bf16[2,2,4,48,768]{4,3,2,1,0:T(8,128)(2,1)}, bf16[2,2,4,48,768]{4,3,2,1,0:T(8,128)(2,1)}, bf16[2,2,4,48,768]{4,3,2,1,0:T(8,128)(2,1)}, bf16[2,2,4...) custom-call(s32[5,8]{1,0:T(8,128)} %copy-done.4, ...), custom_call_target="tpu_custom_call" | custom-call | flops 42949672960 | bytes 16384000 | tf_op jit(solution)/shard_map/backward/pallas_call | solution.py:851
  371.0 2.3 bitcast_convert_fusion
  373.9 4.2 %maximum_convert_fusion = f32[768,1536]{1,0:T(8,128)} fusion(bf16[768,768]{1,0:T(8,128)(2,1)} %bitcast.135, bf16[768,768]{1,0:T(8,128)(2,1)S(1)} %bitcast.134), kind=kLoop, calls=%fused_computation.24 | loop fusion | flops 4718592 | bytes 7077888 | tf_op jit(solution)/shard_map/convert_element_type | solution.py:1124
  378.1 2.5 maximum_convert_fusion.1
  380.7 2.1 maximum_convert_fusion.2
  382.8 1.1 copy.45
  (140 shorter events, 24.6 us)
Async XLA Ops:
  0.6 102.6 %copy-start = (bf16[1536,768]{1,0:T(8,128)(2,1)S(1)}, bf16[1536,768]{1,0:T(8,128)(2,1)}, u32[]{:S(2)}) copy-start(bf16[1536,768]{1,0:T(8,128)(2,1)} %param.19) | copy-start | bytes 7077892
  3.6 2.0 copy-start.14
  3.9 3.5 copy-start.33
  5.5 2.8 collective-permute-start
  7.5 149.1 %copy-start.4 = (s32[5,8]{1,0:T(8,128)}, s32[5,8]{1,0:T(8,128)S(1)}, u32[]{:S(2)}) copy-start(s32[5,8]{1,0:T(8,128)S(1)} %stack.27.starts.refs_0_) | copy-start | bytes 484
  10.4 2.0 copy-start.35
  10.4 2.0 copy-start.39
  10.6 3.9 %copy-start.17 = (bf16[16,2,32,768]{3,2,1,0:T(8,128)(2,1)}, bf16[16,2,32,768]{3,2,1,0:T(8,128)(2,1)S(1)}, u32[]{:S(2)}) copy-start(bf16[16,2,32,768]{3,2,1,0:T(8,128)(2,1)S(1)} %copy.29) | copy-start | bytes 4718596
  83.4 3.4 copy-start.11
  83.4 2.4 copy-start.37
  87.0 4.9 %copy-start.15 = (bf16[16,2,32,768]{3,2,0,1:T(8,128)(2,1)}, bf16[16,2,32,768]{3,2,0,1:T(8,128)(2,1)S(1)}, u32[]{:S(2)}) copy-start(bf16[16,2,32,768]{3,2,0,1:T(8,128)(2,1)S(1)} %copy.32) | copy-start | bytes 4718596
  88.0 4.0 %collective-permute-start.1 = (bf16[512,768]{1,0:T(8,128)(2,1)}, bf16[512,768]{1,0:T(8,128)(2,1)}, u32[]{:S(2)}, u32[]{:S(2)}) collective-permute-start(bf16[512,768]{1,0:T(8,128)(2,1)} %dynamic-slice_bitcast_fusion.2), channel_id=1, source_target_pairs={{0,1},{1,0},{2,3},{3,2},{4,5},{5,4},{6,7},{7,6},{8,9},{9,8},{10,11... | collective-permute-start | bytes 2359304 | tf_op jit(solution)/shard_map/ppermute | solution.py:995
  91.9 4.4 %collective-permute-start.4 = (bf16[512,768]{1,0:T(8,128)(2,1)}, bf16[512,768]{1,0:T(8,128)(2,1)}, u32[]{:S(2)}, u32[]{:S(2)}) collective-permute-start(bf16[512,768]{1,0:T(8,128)(2,1)} %convolution_convert_fusion.3), channel_id=1, source_target_pairs={{0,1},{1,0},{2,3},{3,2},{4,5},{5,4},{6,7},{7,6},{8,9},{9,8},{10,11... | collective-permute-start | bytes 2359304 | tf_op jit(solution)/shard_map/ppermute | solution.py:995
  95.1 2.8 collective-permute-start.2
  98.4 2.2 copy-start.34
  98.6 25.0 %copy-start.19 = (bf16[16,2,32,768]{3,2,1,0:T(8,128)(2,1)}, bf16[16,2,32,768]{3,2,1,0:T(8,128)(2,1)S(1)}, u32[]{:S(2)}) copy-start(bf16[16,2,32,768]{3,2,1,0:T(8,128)(2,1)S(1)} %pad_maximum_fusion.1) | copy-start | bytes 4718596
  119.7 3.9 %copy-start.40 = (bf16[1024,1536]{1,0:T(8,128)(2,1)}, bf16[1024,1536]{1,0:T(8,128)(2,1)S(1)}, u32[]{:S(2)}) copy-start(bf16[1024,1536]{1,0:T(8,128)(2,1)S(1)} %get-tuple-element.85) | copy-start | bytes 9437188
  129.4 4.6 %copy-start.16 = (bf16[1024,1536]{1,0:T(8,128)(2,1)S(1)}, bf16[1024,1536]{1,0:T(8,128)(2,1)}, u32[]{:S(2)}) copy-start(bf16[1024,1536]{1,0:T(8,128)(2,1)} %multiply_convert_fusion) | copy-start | bytes 9437188
  138.0 1.9 copy-start.41
  138.1 2.3 copy-start.20
  138.2 7.2 %collective-permute-start.5 = (bf16[512,768]{1,0:T(8,128)(2,1)S(1)}, bf16[512,768]{1,0:T(8,128)(2,1)S(1)}, u32[]{:S(2)}, u32[]{:S(2)}) collective-permute-start(bf16[512,768]{1,0:T(8,128)(2,1)S(1)} %dynamic-slice_bitcast_fusion), channel_id=1, source_target_pairs={{0,1},{1,0},{2,3},{3,2},{4,5},{5,4},{6,7},{7,6},{8,9},{9,8},{10,11... | collective-permute-start | bytes 2359304 | tf_op jit(solution)/shard_map/ppermute | solution.py:995
  138.4 11.8 %collective-permute-start.3 = (bf16[512,768]{1,0:T(8,128)(2,1)S(1)}, bf16[512,768]{1,0:T(8,128)(2,1)S(1)}, u32[]{:S(2)}, u32[]{:S(2)}) collective-permute-start(bf16[512,768]{1,0:T(8,128)(2,1)S(1)} %dynamic-slice_bitcast_fusion.1), channel_id=1, source_target_pairs={{0,1},{1,0},{2,3},{3,2},{4,5},{5,4},{6,7},{7,6},{8,9},{9,8},{10,11... | collective-permute-start | bytes 2359304 | tf_op jit(solution)/shard_map/ppermute | solution.py:995
  149.5 3.5 collective-permute-start.6
  371.0 2.3 copy-start.32
  371.0 2.9 copy-start.24
  373.9 4.3 %copy-start.22 = (bf16[2,2,4,48,768]{4,3,2,1,0:T(8,128)(2,1)S(1)}, bf16[2,2,4,48,768]{4,3,2,1,0:T(8,128)(2,1)}, u32[]{:S(2)}) copy-start(bf16[2,2,4,48,768]{4,3,2,1,0:T(8,128)(2,1)} %get-tuple-element.71) | copy-start | bytes 3538948
  373.9 4.3 %copy-start.23 = (bf16[2,2,4,48,768]{4,3,2,1,0:T(8,128)(2,1)S(1)}, bf16[2,2,4,48,768]{4,3,2,1,0:T(8,128)(2,1)}, u32[]{:S(2)}) copy-start(bf16[2,2,4,48,768]{4,3,2,1,0:T(8,128)(2,1)} %get-tuple-element.72) | copy-start | bytes 3538948
  378.1 2.6 copy-start.25
  378.1 2.6 copy-start.26
  378.1 2.6 copy-start.27
  380.7 2.1 copy-start.18
  382.8 2.2 copy-start.1
  (17 other events, 16.3 us)

commit v5 on v4

--- a/solution.py
+++ b/solution.py
@@ -499,10 +499,6 @@
     result[2 * E :, :] = gv[...].T[:E].astype(BF)
 
 
-def stream_orders(count):
-    return [((0, 1), (1, 0))[s % 2] for s in range(count)]
-
-
 class Names:
     def __init__(self, refs):
         self.refs = list(refs)
@@ -515,25 +511,27 @@
         return self.take(1)[0]
 
 
+ORDERS = {
+    'u1': (1, 0), 'u2': (0, 1), 'd1': (1, 0), 'd2': (1, 0), 'o': (1, 0), 'i0': (1, 0), 'i1': (0, 1), 'i2': (0,
+    1),
+}
 EARLY = [
-    (6, 1, 1),
-    (7, 0, 1),
-    (9, 1, 2),
-    (9, 0, 2),
-    (10, 3, 1),
-    (11, 2, 1),
-    (11, 4, 1),
-    (11, 1, 3),
-    (11, 0, 3),
-    (13, 3, 2),
-    (13, 1, 4),
-    (13, 0, 4),
-    (14, 2, 2),
-    (14, 4, 2),
-    (15, 3, 3),
-    (15, 1, 5),
-    (15, 0, 5),
+    (2, 'o', 0), (3, 'u1', 0), (3, 'u2', 0), (5, 'o', 1), (5, 'd1', 0), (8, 'u1', 1), (8, 'u2', 1), (8, 'o',
+    2), (10, 'o', 3), (13, 'o', 4), (13, 'd2', 0), (13, 'd1', 1), (13, 'u1', 2), (13, 'u2', 2),
 ]
+TAIL = [
+    ('u1', 3), 'gather', 'in1', ('i1', 0), ('o', 5), ('u2', 3), ('d1', 2), 'in0', ('i0', 0), ('d2', 1), ('i1',
+    1), ('u1', 4), ('d2', 2), ('u2', 4), ('i0', 1), 'in2', ('d1', 3), ('o', 6), ('i2', 0), ('u1', 5), ('i0',
+    2), 'one', ('d1', 4), ('i0', 3), ('d2', 3), ('i2', 1), ('i0', 4), ('d1', 5), ('u2', 5), ('i2', 2), 'norm',
+    ('i0', 5), 'gain0', ('i1', 2), ('d2', 4), 'gain1', ('i2', 3), ('i1', 3), 'gain2', ('i1', 4), ('d1', 6),
+    'gain3', ('i0', 6), ('i2', 4), 'gain4', ('i1', 5), ('d2', 5), ('i2', 5), ('u1', 6), ('i2', 6), ('i1', 6),
+    ('d2', 6), ('u2', 6),
+]
+
+
+def stream_names(streams):
+    pairs = streams // 2
+    return [kind + str(i + 1) for i in range(pairs) for kind in "ud"] + ["o"]
 
 
 def backward_kernel(heads, streams, *refs):
@@ -551,9 +549,11 @@
     gain_head, gain_one, gain_two, gain_rest = names.take(4)
     in_send, in_recv, in_local, out_send, out_recv, out_local = names.take(6)
     part_sem, head_sems, gain_sems = names.take(3)
-    orders = stream_orders(streams)
-    reductions = make_reductions(orders, totals, names.take(5 * streams))
-    lasts = make_reductions([(1, 0), (0, 1), (1, 0)], in_totals, names.take(15))
+    labels = stream_names(streams) + ["i0", "i1", "i2"]
+    reductions = make_reductions(
+        [ORDERS[label] for label in labels], list(totals) + list(in_totals), names.take(5 * streams + 15)
+    )
+    reductions = dict(zip(labels, reductions))
 
     shapes = [branch_shape(b, heads) for b in range(BRANCHES)]
     size, head_size = lax.axis_size("seq"), lax.axis_size("head")
@@ -583,9 +583,8 @@
     for branch in range(1, BRANCHES):
         for copy in coming(branch):
             copy.start()
-    for s in range(streams):
-        fills[s].wait()
-        reductions[s].step(0)
+    for fill in fills:
+        fill.wait()
 
     def split_branch(branch):
         stride, lanes, units, split = shapes[branch]
@@ -608,8 +607,8 @@
     blocks = at + heads - heads // 2
     plan = {}
     for block, stream, step in EARLY:
-        if stream < streams:
-            plan.setdefault(block * blocks // 16, []).append((stream, step))
+        if stream in labels:
+            plan.setdefault(block * blocks // 15, []).append((stream, step))
 
     @pl.loop(0, blocks)
     def _(block):
@@ -660,51 +659,46 @@
                         for copy in leaving(branch):
                             copy.start()
 
-    for branch in range(1, BRANCHES):
-        for copy in leaving(branch):
-            copy.wait()
-
-    later = []
-    done = {s: 1 for s in range(streams)}
-    for _, stream, step in EARLY:
-        if stream < streams:
-            done[stream] = step + 1
-    for step in range(Reduction.STEPS):
-        later += [(s, step) for s in (1, 0, 3, 2, 4) if s < streams and step >= done[s]]
-
-    def advance(count):
-        for stream, step in later[:count]:
-            reductions[stream].step(step)
-        del later[:count]
-
-    @pl.loop(0, heads)
-    def _(head):
-        total[...] = first[head].astype(F32)
+    tasks = {}
+
+    def task(work):
+        tasks[work.__name__] = work
+
+    @task
+    def gather():
         for branch in range(1, BRANCHES):
-            stride, lanes, per, split = shapes[branch]
-            back, start = backs[branch - 1], starts[branch, head]
-            if split == 1:
-                value = back[head // per, head % per].astype(F32)
-            else:
-                value = back[head * split, 0].astype(F32)
-                for copy in range(1, split):
-                    value = value + back[head * split + copy, 0].astype(F32)
-            if lanes < 128:
-                share = 128 // lanes
-                value = moved_part(value, lanes, me % share, start % share)
-                start = start // share
-                lanes = 128
-            for block in range(SEG0 // lanes):
-                span = slice(block * lanes, (block + 1) * lanes)
-                total[:, span] += jnp.where(start == block, value, 0.0)
-        grads[0, head] = (total[0:E, :] * E ** (-0.5)).astype(BF)
-        grads[1, head] = total[E : 2 * E, :].astype(BF)
-        grads[2, head] = total[2 * E :, :].astype(BF)
-
-    normed_t[...] = normed[...].T
-    rows_in = in_totals[0].shape[3]
-    chunk = width // 2
-    for j in range(3):
+            for copy in leaving(branch):
+                copy.wait()
+
+        @pl.loop(0, heads)
+        def _(head):
+            total[...] = first[head].astype(F32)
+            for branch in range(1, BRANCHES):
+                stride, lanes, per, split = shapes[branch]
+                back, start = backs[branch - 1], starts[branch, head]
+                if split == 1:
+                    value = back[head // per, head % per].astype(F32)
+                else:
+                    value = back[head * split, 0].astype(F32)
+                    for copy in range(1, split):
+                        value = value + back[head * split + copy, 0].astype(F32)
+                if lanes < 128:
+                    share = 128 // lanes
+                    value = moved_part(value, lanes, me % share, start % share)
+                    start = start // share
+                    lanes = 128
+                for block in range(SEG0 // lanes):
+                    span = slice(block * lanes, (block + 1) * lanes)
+                    total[:, span] += jnp.where(start == block, value, 0.0)
+            grads[0, head] = (total[0:E, :] * E ** (-0.5)).astype(BF)
+            grads[1, head] = total[E : 2 * E, :].astype(BF)
+            grads[2, head] = total[2 * E :, :].astype(BF)
+
+        normed_t[...] = normed[...].T
+
+    def in_gradient(j):
+        rows_in = in_totals[0].shape[3]
+        chunk = width // 2
         grads_t[j] = grads[j].reshape(heads * E, SEG0).T
         for half in range(2):
             value = jnp.dot(
@@ -715,68 +709,78 @@
                 in_totals[j][index // (2 * rest), index // rest % 2, index % rest] = value[
                     part * rows_in : (part + 1) * rows_in
                 ]
-        lasts[j].step(0)
-    advance(3)
-
-    for half in range(2):
-        rows = slice(half * SEG0 // 2, (half + 1) * SEG0 // 2)
-        value = jnp.zeros((SEG0 // 2, width), F32)
-        for j in range(3):
-            value = value + lax.dot_general(
-                grads_t[j, rows], in_proj[j], (((1,), (1,)), ((), ())), preferred_element_type=F32
+
+    for j in range(3):
+        tasks[f"in{j}"] = partial(in_gradient, j)
+
+    def head_swaps():
+        swaps = []
+        for step in range(1, head_size):
+            device = (me_head + step) % head_size
+            swaps.append(
+                pltpu.make_async_remote_copy(
+                    src_ref=head_send.at[device],
+                    dst_ref=head_recv.at[step - 1],
+                    send_sem=head_sems.at[0, step - 1],
+                    recv_sem=head_sems.at[1, step - 1],
+                    device_id={"head": device},
+                    device_id_type=pl.DeviceIdType.MESH,
+                )
             )
-        value = value.astype(BF)
-        for slot in range(SLOTS // 2):
-            for device in range(head_size):
-                begin = (slot * head_size + device) * per_slot
-                place = (half * SLOTS // 2 + slot) * per_slot
-                head_send[device, place : place + per_slot] = value[begin : begin + per_slot]
-    swaps = []
-    for step in range(1, head_size):
-        device = (me_head + step) % head_size
-        swaps.append(
-            pltpu.make_async_remote_copy(
-                src_ref=head_send.at[device],
-                dst_ref=head_recv.at[step - 1],
-                send_sem=head_sems.at[0, step - 1],
-                recv_sem=head_sems.at[1, step - 1],
-                device_id={"head": device},
-                device_id_type=pl.DeviceIdType.MESH,
+        return swaps
+
+    @task
+    def one():
+        for half in range(2):
+            rows = slice(half * SEG0 // 2, (half + 1) * SEG0 // 2)
+            value = jnp.zeros((SEG0 // 2, width), F32)
+            for j in range(3):
+                value = value + lax.dot_general(
+                    grads_t[j, rows], in_proj[j], (((1,), (1,)), ((), ())), preferred_element_type=F32
+                )
+            value = value.astype(BF)
+            for slot in range(SLOTS // 2):
+                for device in range(head_size):
+                    begin = (slot * head_size + device) * per_slot
+                    place = (half * SLOTS // 2 + slot) * per_slot
+                    head_send[device, place : place + per_slot] = value[begin : begin + per_slot]
+        for swap in head_swaps():
+            swap.start()
+
+    @task
+    def norm():
+        for swap in head_swaps():
+            swap.wait()
+        gain_head[me_head] = jnp.zeros(gains_out.shape, F32)
+        gain_head[me_head, 2:4] = gains_two[...]
+
+        @pl.loop(0, SLOTS)
+        def _(slot):
+            rows = pl.ds(pl.multiple_of(slot * per_slot, per_slot), per_slot)
+            grad = head_send[me_head, rows].astype(F32)
+            for step in range(1, head_size):
+                grad = grad + head_recv[step - 1, rows].astype(F32)
+            values = x_rows[rows]
+            centred = values - jnp.mean(values, axis=-1, keepdims=True)
+            scale = lax.rsqrt(jnp.mean(centred * centred, axis=-1, keepdims=True) + EPS)
+            unit = centred * scale
+            scaled = grad * gain[...]
+            inner = jnp.mean(scaled * unit, axis=-1, keepdims=True)
+            out = grad_hidden[rows] + scale * (
+                scaled - jnp.mean(scaled, axis=-1, keepdims=True) - unit * inner
             )
-        )
-        swaps[-1].start()
-    advance(3)
-    for swap in swaps:
-        swap.wait()
-
-    gain_head[me_head] = jnp.zeros(gains_out.shape, F32)
-    gain_head[me_head, 2:4] = gains_two[...]
-
-    @pl.loop(0, SLOTS)
-    def _(slot):
-        rows = pl.ds(pl.multiple_of(slot * per_slot, per_slot), per_slot)
-        grad = head_send[me_head, rows].astype(F32)
-        for step in range(1, head_size):
-            grad = grad + head_recv[step - 1, rows].astype(F32)
-        values = x_rows[rows]
-        centred = values - jnp.mean(values, axis=-1, keepdims=True)
-        scale = lax.rsqrt(jnp.mean(centred * centred, axis=-1, keepdims=True) + EPS)
-        unit = centred * scale
-        scaled = grad * gain[...]
-        inner = jnp.mean(scaled * unit, axis=-1, keepdims=True)
-        out = grad_hidden[rows] + scale * (scaled - jnp.mean(scaled, axis=-1, keepdims=True) - unit * inner)
-        place = slot % 2 * 8 + slot // 2 % 2 * 4 + slot // 4 % 2 * 2 + slot // 8
+            place = slot % 2 * 8 + slot // 2 % 2 * 4 + slot // 4 % 2 * 2 + slot // 8
+            for column in range(width // 128):
+                lanes = slice(column * 128, (column + 1) * 128)
+                spread_rows[column, pl.ds(place, per_slot, stride=SLOTS), :] = out[:, lanes]
+            gain_head[me_head, 0:1] += jnp.sum(grad * unit, axis=0, keepdims=True)
+            gain_head[me_head, 1:2] += jnp.sum(grad, axis=0, keepdims=True)
+
         for column in range(width // 128):
-            lanes = slice(column * 128, (column + 1) * 128)
-            spread_rows[column, pl.ds(place, per_slot, stride=SLOTS), :] = out[:, lanes]
-        gain_head[me_head, 0:1] += jnp.sum(grad * unit, axis=0, keepdims=True)
-        gain_head[me_head, 1:2] += jnp.sum(grad, axis=0, keepdims=True)
-
-    for column in range(width // 128):
-        grad_tokens[:, column * 128 : (column + 1) * 128] = spread_rows[column]
+            grad_tokens[:, column * 128 : (column + 1) * 128] = spread_rows[column]
 
     def gain_copy(source, target, axis, device, sem):
-        made = pltpu.make_async_remote_copy(
+        return pltpu.make_async_remote_copy(
             src_ref=source,
             dst_ref=target,
             send_sem=gain_sems.at[0, sem],
@@ -784,56 +788,56 @@
             device_id={axis: device},
             device_id_type=pl.DeviceIdType.MESH,
         )
-        made.start()
-        return made
-
-    mine = gain_head.at[me_head]
-    swaps = [
-        gain_copy(mine, mine, "head", (me_head + step) % head_size, step - 1) for step in range(1, head_size)
-    ]
-    advance(3)
-    for swap in swaps:
-        swap.wait()
-    value = gain_head[0]
-    for device in range(1, head_size):
-        value = value + gain_head[device]
-    gain_one[0] = value
-    swap = gain_copy(gain_one.at[0], gain_one.at[1], "seq", me + 1 - 2 * (me % 2), head_size)
-    for last in lasts:
-        last.step(1)
-    advance(2)
-    swap.wait()
-    gain_two[0] = gain_one[0] + gain_one[1]
-    swap = gain_copy(gain_two.at[0], gain_two.at[1], "seq", me + 2 - 4 * (me // 2 % 2), head_size + 1)
-    advance(2)
-    for last in lasts:
-        last.step(2)
-    swap.wait()
-    spot = me // 4
-    gain_rest[spot] = gain_two[0] + gain_two[1]
-    block = gain_rest.at[spot]
-    swaps = [
-        gain_copy(block, block, "seq", (spot + step) % rest * 4 + me % 4, head_size + 1 + step)
-        for step in range(1, rest)
-    ]
-    advance(2)
-    for last in lasts:
-        last.step(3)
-    for swap in swaps:
-        swap.wait()
-    value = gain_rest[0]
-    for z in range(1, rest):
-        value = value + gain_rest[z]
-    gains_out[...] = value
-    advance(2)
-    for last in lasts:
-        last.step(4)
-    advance(2)
-    for last in lasts:
-        last.step(5)
-    advance(len(later))
-    for last in lasts:
-        last.step(6)
+
+    def gain_copies(stage):
+        if stage == 0:
+            mine = gain_head.at[me_head]
+            return [
+                gain_copy(mine, mine, "head", (me_head + step) % head_size, step - 1)
+                for step in range(1, head_size)
+            ]
+        if stage == 1:
+            return [gain_copy(gain_one.at[0], gain_one.at[1], "seq", me + 1 - 2 * (me % 2), head_size)]
+        if stage == 2:
+            device = me + 2 - 4 * (me // 2 % 2)
+            return [gain_copy(gain_two.at[0], gain_two.at[1], "seq", device, head_size + 1)]
+        spot = me // 4
+        block = gain_rest.at[spot]
+        return [
+            gain_copy(block, block, "seq", (spot + step) % rest * 4 + me % 4, head_size + 1 + step)
+            for step in range(1, rest)
+        ]
+
+    def summed(ref, count):
+        value = ref[0]
+        for index in range(1, count):
+            value = value + ref[index]
+        return value
+
+    def gain_stage(stage):
+        if stage > 0:
+            for swap in gain_copies(stage - 1):
+                swap.wait()
+        if stage == 1:
+            gain_one[0] = summed(gain_head, head_size)
+        elif stage == 2:
+            gain_two[0] = summed(gain_one, 2)
+        elif stage == 3:
+            gain_rest[me // 4] = summed(gain_two, 2)
+        elif stage == 4:
+            gains_out[...] = summed(gain_rest, rest)
+            return
+        for swap in gain_copies(stage):
+            swap.start()
+
+    for stage in range(5):
+        tasks[f"gain{stage}"] = partial(gain_stage, stage)
+
+    for item in TAIL:
+        if isinstance(item, str):
+            tasks[item]()
+        elif item[0] in labels:
+            reductions[item[0]].step(item[1])
 
 
 def backward(heads, starts, own, own_g, units, sends, terms, normed, in_proj, x_rows, grad_hidden, gain, gains_two):

time: 391 us -> 353 us (0.903)
  Pallas kernels: 279 us -> 242 us
    pallas_call x1, Pallas kernels: 209 us -> 171 us  [backward(): pl.pallas_call(partial(backward_kernel, heads, streams), in_specs=[pl.Blo...]
  transfers between devices with their start and end apart: 7 -> 7, of which waited for: 0 -> 0; matrix products, arithmetic and copies ran while one was open for 6% -> 7% of each run, Pallas kernels for 0% -> 0%
where the time goes in v5:
time: 353 us; the launch traced here: 348 us
  Pallas kernels  242 us (69%)
  matrix products  51.8 us (15%)
  other arithmetic  28.9 us (8%)
  local copies, waits for them, and re-layouts  22.2 us (6%)
    pallas_call x1, Pallas kernels, backward(): pl.pallas_call(partial(backward_kernel, heads, streams), in_specs=[pl.Blo...  171 us
    pallas_call x1, Pallas kernels, exchange_forward(): pl.pallas_call(partial(exchange_forward_kernel, heads), in_specs=vmem_spe...  61.7 us
    unnamed x85, local copies, waits for them, and re-layouts  18 us
    dot_general x1, matrix products, local(): jnp.einsum('td,fd->tf', cot_all, down_proj, preferred_element_type=F32)  16.4 us
  transfers between devices with their start and end apart: 7, of which 0 were waited for; matrix products, arithmetic and copies ran while one was open for 7% of the time, Pallas kernels for 0%

profile of v5, /device:TPU:0, one launch (start us, length us, event | category | flops | bytes accessed | tf_op | source)
XLA Modules:
  0.0 348.0 jit_solution(13111940915423249918)
XLA Ops:
  0.7 2.9 fusion.92
  4.3 1.2 add_convert_fusion.2
  8.3 1.9 broadcast_select_fusion.7
  10.6 1.9 copy-done.35
  12.4 2.0 fusion.6.proj
  14.5 4.6 %pack_heads.1 = (bf16[1,8,160,1024]{3,2,1,0:T(8,128)(2,1)}, bf16[2,4,160,512]{3,2,1,0:T(8,128)(2,1)S(1)}, bf16[4,2,160,256]{3,2,1,0:T(8,128)(2,1)S(1)}, bf16[8,1...) custom-call(s32[5,8]{1,0:T(8,128)S(1)} %stack.27.starts.refs_0_, s32[1]{0:T(128)} %bitcast.place, ...), custom_call_target="tpu_custom_call" | custom-call | tf_op jit(solution)/shard_map/pack_heads/pallas_call | solution.py:126
  20.1 61.7 %exchange_forward.1 = (bf16[1,8,64,1024]{3,2,1,0:T(8,128)(2,1)S(1)}, bf16[2,4,160,512]{3,2,1,0:T(8,128)(2,1)}, bf16[4,2,160,256]{3,2,1,0:T(8,128)(2,1)S(1)}, bf1...) custom-call(bf16[1,8,160,1024]{3,2,1,0:T(8,128)(2,1)} %get-tuple-ele, ...), custom_call_target="tpu_custom_call" | custom-call | flops 17179869184 | bytes 16384000 | tf_op jit(solution)/shard_map/exchange_forward/pallas_call | solution.py:446
  83.4 2.3 merge_heads.1
  88.7 3.2 convolution_convert_fusion.3
  91.9 2.2 fusion.90
  96.3 1.5 broadcast_select_fusion.3
  98.6 2.1 copy-done.34
  100.7 2.6 fusion.93
  103.3 16.4 %add_convert_fusion = (bf16[1024,1536]{1,0:T(8,128)(2,1)S(1)}, f32[1024,1536]{1,0:T(8,128)S(1)}) fusion(f32[1024,1536]{1,0:T(8,128)S(1)} %fusion.93, bf16[1024,768]{1,0:T(8,128)(2,1)S(1)} %bitcast.121, bf16[1536,768]{1,0:T(8,128)(2,1)S(1)} %copy-done), kind=kOutput, calls=%fused_computation.2 | convolution fusion | flops 2529165312 | bytes 19660800 | tf_op jit(solution)/shard_map/td,fd->tf/dot_general | solution.py:1101
  119.7 3.9 %convolution_convert_fusion.1 = bf16[1024,768]{1,0:T(8,128)(2,1)} fusion(bf16[1024,1536]{1,0:T(8,128)(2,1)S(1)} %get-tuple-element.85, bf16[768,1536]{1,0:T(8,128)(2,1)S(1)} %copy-done.34), kind=kOutput, calls=%fused_computation.28 | convolution fusion | flops 2416705536 | bytes 7077888 | tf_op jit(solution)/shard_map/tf,df->td/dot_general | solution.py:1107
  123.6 2.5 fusion.18
  126.1 3.3 multiply_convert_fusion
  129.4 4.6 %convolution_convert_fusion.2 = bf16[1024,768]{1,0:T(8,128)(2,1)S(1)} fusion(bf16[1024,1536]{1,0:T(8,128)(2,1)} %multiply_convert_fusion, bf16[1536,768]{1,0:T(8,128)(2,1)S(1)} %copy-done), kind=kOutput, calls=%fused_computation.29 | convolution fusion | flops 2416705536 | bytes 7077888 | tf_op jit(solution)/shard_map/dot_general | solution.py:1089
  134.1 2.5 fusion.21
  136.7 1.3 copy-done.21
  140.4 2.5 fusion.24
  142.8 2.5 fusion.27
  146.9 2.5 fusion.87
  150.2 2.8 convolution_convert_fusion.4
  155.0 1.6 convolution_convert_fusion.5
  156.6 1.8 spread_heads.1
  162.3 171.1 %backward.1 = (bf16[2,2,4,48,768]{4,3,2,1,0:T(8,128)(2,1)}, bf16[2,2,4,48,768]{4,3,2,1,0:T(8,128)(2,1)}, bf16[2,2,4,48,768]{4,3,2,1,0:T(8,128)(2,1)}, bf16[2,2,4...) custom-call(s32[5,8]{1,0:T(8,128)} %copy-done.4, ...), custom_call_target="tpu_custom_call" | custom-call | flops 42949672960 | bytes 16384000 | tf_op jit(solution)/shard_map/backward/pallas_call | solution.py:855
  333.4 2.3 bitcast_convert_fusion
  336.3 4.2 %maximum_convert_fusion = f32[768,1536]{1,0:T(8,128)} fusion(bf16[768,768]{1,0:T(8,128)(2,1)} %bitcast.135, bf16[768,768]{1,0:T(8,128)(2,1)S(1)} %bitcast.134), kind=kLoop, calls=%fused_computation.24 | loop fusion | flops 4718592 | bytes 7077888 | tf_op jit(solution)/shard_map/convert_element_type | solution.py:1128
  340.6 2.5 maximum_convert_fusion.1
  343.1 2.1 maximum_convert_fusion.2
  345.2 1.1 copy.45
  (140 shorter events, 24.6 us)
Async XLA Ops:
  0.6 102.6 %copy-start = (bf16[1536,768]{1,0:T(8,128)(2,1)S(1)}, bf16[1536,768]{1,0:T(8,128)(2,1)}, u32[]{:S(2)}) copy-start(bf16[1536,768]{1,0:T(8,128)(2,1)} %param.19) | copy-start | bytes 7077892
  3.6 2.0 copy-start.14
  3.9 3.5 %copy-start.33 = (s32[5,8]{1,0:T(8,128)S(1)}, s32[5,8]{1,0:T(8,128)}, u32[]{:S(2)}) copy-start(s32[5,8]{1,0:T(8,128)} %param.15) | copy-start | bytes 484
  5.5 2.8 collective-permute-start
  7.5 149.1 %copy-start.4 = (s32[5,8]{1,0:T(8,128)}, s32[5,8]{1,0:T(8,128)S(1)}, u32[]{:S(2)}) copy-start(s32[5,8]{1,0:T(8,128)S(1)} %stack.27.starts.refs_0_) | copy-start | bytes 484
  10.4 2.0 copy-start.35
  10.4 2.0 copy-start.39
  10.6 3.9 %copy-start.17 = (bf16[16,2,32,768]{3,2,1,0:T(8,128)(2,1)}, bf16[16,2,32,768]{3,2,1,0:T(8,128)(2,1)S(1)}, u32[]{:S(2)}) copy-start(bf16[16,2,32,768]{3,2,1,0:T(8,128)(2,1)S(1)} %copy.29) | copy-start | bytes 4718596
  83.4 3.4 copy-start.11
  83.4 2.4 copy-start.37
  87.0 4.9 %copy-start.15 = (bf16[16,2,32,768]{3,2,0,1:T(8,128)(2,1)}, bf16[16,2,32,768]{3,2,0,1:T(8,128)(2,1)S(1)}, u32[]{:S(2)}) copy-start(bf16[16,2,32,768]{3,2,0,1:T(8,128)(2,1)S(1)} %copy.32) | copy-start | bytes 4718596
  88.0 4.0 %collective-permute-start.1 = (bf16[512,768]{1,0:T(8,128)(2,1)}, bf16[512,768]{1,0:T(8,128)(2,1)}, u32[]{:S(2)}, u32[]{:S(2)}) collective-permute-start(bf16[512,768]{1,0:T(8,128)(2,1)} %dynamic-slice_bitcast_fusion.2), channel_id=1, source_target_pairs={{0,1},{1,0},{2,3},{3,2},{4,5},{5,4},{6,7},{7,6},{8,9},{9,8},{10,11... | collective-permute-start | bytes 2359304 | tf_op jit(solution)/shard_map/ppermute | solution.py:999
  91.9 4.4 %collective-permute-start.4 = (bf16[512,768]{1,0:T(8,128)(2,1)}, bf16[512,768]{1,0:T(8,128)(2,1)}, u32[]{:S(2)}, u32[]{:S(2)}) collective-permute-start(bf16[512,768]{1,0:T(8,128)(2,1)} %convolution_convert_fusion.3), channel_id=1, source_target_pairs={{0,1},{1,0},{2,3},{3,2},{4,5},{5,4},{6,7},{7,6},{8,9},{9,8},{10,11... | collective-permute-start | bytes 2359304 | tf_op jit(solution)/shard_map/ppermute | solution.py:999
  95.1 2.8 collective-permute-start.2
  98.4 2.2 copy-start.34
  98.6 25.0 %copy-start.19 = (bf16[16,2,32,768]{3,2,1,0:T(8,128)(2,1)}, bf16[16,2,32,768]{3,2,1,0:T(8,128)(2,1)S(1)}, u32[]{:S(2)}) copy-start(bf16[16,2,32,768]{3,2,1,0:T(8,128)(2,1)S(1)} %pad_maximum_fusion.1) | copy-start | bytes 4718596
  119.7 3.9 %copy-start.40 = (bf16[1024,1536]{1,0:T(8,128)(2,1)}, bf16[1024,1536]{1,0:T(8,128)(2,1)S(1)}, u32[]{:S(2)}) copy-start(bf16[1024,1536]{1,0:T(8,128)(2,1)S(1)} %get-tuple-element.85) | copy-start | bytes 9437188
  129.4 4.6 %copy-start.16 = (bf16[1024,1536]{1,0:T(8,128)(2,1)S(1)}, bf16[1024,1536]{1,0:T(8,128)(2,1)}, u32[]{:S(2)}) copy-start(bf16[1024,1536]{1,0:T(8,128)(2,1)} %multiply_convert_fusion) | copy-start | bytes 9437188
  138.0 1.9 copy-start.41
  138.1 2.3 copy-start.20
  138.2 7.2 %collective-permute-start.5 = (bf16[512,768]{1,0:T(8,128)(2,1)S(1)}, bf16[512,768]{1,0:T(8,128)(2,1)S(1)}, u32[]{:S(2)}, u32[]{:S(2)}) collective-permute-start(bf16[512,768]{1,0:T(8,128)(2,1)S(1)} %dynamic-slice_bitcast_fusion), channel_id=1, source_target_pairs={{0,1},{1,0},{2,3},{3,2},{4,5},{5,4},{6,7},{7,6},{8,9},{9,8},{10,11... | collective-permute-start | bytes 2359304 | tf_op jit(solution)/shard_map/ppermute | solution.py:999
  138.4 11.8 %collective-permute-start.3 = (bf16[512,768]{1,0:T(8,128)(2,1)S(1)}, bf16[512,768]{1,0:T(8,128)(2,1)S(1)}, u32[]{:S(2)}, u32[]{:S(2)}) collective-permute-start(bf16[512,768]{1,0:T(8,128)(2,1)S(1)} %dynamic-slice_bitcast_fusion.1), channel_id=1, source_target_pairs={{0,1},{1,0},{2,3},{3,2},{4,5},{5,4},{6,7},{7,6},{8,9},{9,8},{10,11... | collective-permute-start | bytes 2359304 | tf_op jit(solution)/shard_map/ppermute | solution.py:999
  149.5 3.5 %collective-permute-start.6 = (bf16[512,768]{1,0:T(8,128)(2,1)S(1)}, bf16[512,768]{1,0:T(8,128)(2,1)S(1)}, u32[]{:S(2)}, u32[]{:S(2)}) collective-permute-start(bf16[512,768]{1,0:T(8,128)(2,1)S(1)} %get-tuple-element.81), channel_id=1, source_target_pairs={{0,1},{1,0},{2,3},{3,2},{4,5},{5,4},{6,7},{7,6},{8,9},{9,8},{10,11... | collective-permute-start | bytes 2359304 | tf_op jit(solution)/shard_map/ppermute | solution.py:999
  333.4 2.3 copy-start.32
  333.4 2.9 copy-start.24
  336.3 4.3 %copy-start.22 = (bf16[2,2,4,48,768]{4,3,2,1,0:T(8,128)(2,1)S(1)}, bf16[2,2,4,48,768]{4,3,2,1,0:T(8,128)(2,1)}, u32[]{:S(2)}) copy-start(bf16[2,2,4,48,768]{4,3,2,1,0:T(8,128)(2,1)} %get-tuple-element.71) | copy-start | bytes 3538948
  336.3 4.3 %copy-start.23 = (bf16[2,2,4,48,768]{4,3,2,1,0:T(8,128)(2,1)S(1)}, bf16[2,2,4,48,768]{4,3,2,1,0:T(8,128)(2,1)}, u32[]{:S(2)}) copy-start(bf16[2,2,4,48,768]{4,3,2,1,0:T(8,128)(2,1)} %get-tuple-element.72) | copy-start | bytes 3538948
  340.6 2.6 copy-start.25
  340.6 2.6 copy-start.26
  340.6 2.6 copy-start.27
  343.1 2.1 copy-start.18
  345.2 2.2 copy-start.1
  (17 other events, 16.3 us)

commit v6 on v5

--- a/solution.py
+++ b/solution.py
@@ -209,8 +209,8 @@
 class Reduction:
     STEPS = 7
 
-    def __init__(self, order, total, half, quarter, others, send, recv):
-        self.total = total
+    def __init__(self, order, total, half, quarter, others, send, recv, begun=False):
+        self.total, self.begun = total, begun
         self.half, self.quarter, self.others = half, quarter, others
         self.send, self.recv = send, recv
         me = lax.axis_index("seq")
@@ -258,21 +258,29 @@
             return [self.copy(block, block, self.partners[0], 2 * rest + 1)]
         return []
 
+    def finish_first(self):
+        one, rest = self.bits[0], self.rest
+        for copy in self.copies(0):
+            copy.wait()
+
+        @pl.loop(0, 2 * rest)
+        def _(i):
+            j, z = i // rest, i % rest
+            mine = self.total[one, j, z].astype(F32)
+            self.half[j, z] = (mine + self.half[j, z].astype(F32)).astype(BF)
+
     def step(self, number):
         one, two = self.bits
         rest = self.rest
-        if number > 0:
+        if number == 0 and self.begun:
+            return
+        if number == 1:
+            if not self.begun:
+                self.finish_first()
+        elif number > 0:
             for copy in self.copies(number - 1):
                 copy.wait()
-        if number == 1:
-
-            @pl.loop(0, 2 * rest)
-            def _(i):
-                j, z = i // rest, i % rest
-                mine = self.total[one, j, z].astype(F32)
-                self.half[j, z] = (mine + self.half[j, z].astype(F32)).astype(BF)
-
-        elif number == 2:
+        if number == 2:
 
             @pl.loop(0, rest)
             def _(z):
@@ -512,20 +520,21 @@
 
 
 ORDERS = {
-    'u1': (1, 0), 'u2': (0, 1), 'd1': (1, 0), 'd2': (1, 0), 'o': (1, 0), 'i0': (1, 0), 'i1': (0, 1), 'i2': (0,
+    'u1': (0, 1), 'u2': (0, 1), 'd1': (1, 0), 'd2': (1, 0), 'o': (0, 1), 'i0': (1, 0), 'i1': (1, 0), 'i2': (0,
     1),
 }
 EARLY = [
-    (2, 'o', 0), (3, 'u1', 0), (3, 'u2', 0), (5, 'o', 1), (5, 'd1', 0), (8, 'u1', 1), (8, 'u2', 1), (8, 'o',
-    2), (10, 'o', 3), (13, 'o', 4), (13, 'd2', 0), (13, 'd1', 1), (13, 'u1', 2), (13, 'u2', 2),
+    (0, 'd1', 0), (0, 'u1', 0), (0, 'd1', 1), (0, 'u2', 0), (0, 'u1', 1), (2, 'o', 0), (4, 'u2', 1), (5, 'u1',
+    2), (7, 'd1', 2), (9, 'u1', 3), (10, 'd2', 0), (12, 'd2', 1), (12, 'o', 1), (12, 'd1', 3), (13, 'u2', 2),
+    (14, 'u1', 4),
 ]
 TAIL = [
-    ('u1', 3), 'gather', 'in1', ('i1', 0), ('o', 5), ('u2', 3), ('d1', 2), 'in0', ('i0', 0), ('d2', 1), ('i1',
-    1), ('u1', 4), ('d2', 2), ('u2', 4), ('i0', 1), 'in2', ('d1', 3), ('o', 6), ('i2', 0), ('u1', 5), ('i0',
-    2), 'one', ('d1', 4), ('i0', 3), ('d2', 3), ('i2', 1), ('i0', 4), ('d1', 5), ('u2', 5), ('i2', 2), 'norm',
-    ('i0', 5), 'gain0', ('i1', 2), ('d2', 4), 'gain1', ('i2', 3), ('i1', 3), 'gain2', ('i1', 4), ('d1', 6),
-    'gain3', ('i0', 6), ('i2', 4), 'gain4', ('i1', 5), ('d2', 5), ('i2', 5), ('u1', 6), ('i2', 6), ('i1', 6),
-    ('d2', 6), ('u2', 6),
+    'gather', ('d1', 4), 'in1', ('i1', 0), ('d2', 2), 'in2', ('u2', 3), ('i2', 0), 'in0', ('i0', 0), ('d2',
+    3), ('i1', 1), ('i2', 1), ('u1', 5), ('u2', 4), ('d2', 4), ('d1', 5), ('o', 2), ('i2', 2), ('i0', 1),
+    ('i1', 2), ('i2', 3), 'one', ('d2', 5), ('o', 3), ('i1', 3), ('u1', 6), ('u2', 5), 'norm', ('i2', 4),
+    'gain0', ('i0', 2), ('i1', 4), ('i0', 3), 'gain1', ('o', 4), ('i0', 4), ('i2', 5), 'gain2', ('i1', 5),
+    ('o', 5), ('i0', 5), 'gain3', ('i0', 6), ('d2', 6), ('u2', 6), 'gain4', ('d1', 6), ('i1', 6), ('i2', 6),
+    ('o', 6),
 ]
 
 
@@ -554,6 +563,8 @@
         [ORDERS[label] for label in labels], list(totals) + list(in_totals), names.take(5 * streams + 15)
     )
     reductions = dict(zip(labels, reductions))
+    for label in labels[: streams - 1]:
+        reductions[label].begun = True
 
     shapes = [branch_shape(b, heads) for b in range(BRANCHES)]
     size, head_size = lax.axis_size("seq"), lax.axis_size("head")
@@ -563,7 +574,9 @@
     per_slot = x_rows.shape[0] // SLOTS
     width = x_rows.shape[1]
 
-    fills = [pltpu.make_async_copy(parts[s], totals[s], part_sem.at[s]) for s in range(streams)]
+    fills = [
+        pltpu.make_async_copy(parts[s], reductions[labels[s]].half, part_sem.at[s]) for s in range(streams - 1)
+    ] + [pltpu.make_async_copy(parts[-1], totals[-1], part_sem.at[streams - 1])]
     for fill in fills:
         fill.start()
     meet("seq", "head")
@@ -840,11 +853,10 @@
             reductions[item[0]].step(item[1])
 
 
-def backward(heads, starts, own, own_g, units, sends, terms, normed, in_proj, x_rows, grad_hidden, gain, gains_two):
+def backward(heads, starts, own, own_g, units, sends, parts, normed, in_proj, x_rows, grad_hidden, gain, gains_two):
     size, head_size = lax.axis_size("seq"), lax.axis_size("head")
     rest = size // 4
     rows, width = x_rows.shape
-    parts = [reduction_parts(term, size) for term in terms]
     in_shape = (2, 2, rest, width // size, heads * E)
     scratch = []
     for part in parts:
@@ -859,7 +871,7 @@
         + [pl.BlockSpec(memory_space=pl.ANY)] * streams
         + vmem_specs(6),
         out_specs=vmem_specs(streams + 5),
-        out_shape=[jax.ShapeDtypeStruct(part.shape, BF) for part in parts]
+        out_shape=[jax.ShapeDtypeStruct((2, 2, rest) + part.shape[-2:], BF) for part in parts]
         + [jax.ShapeDtypeStruct(in_shape, BF)] * 3
         + [jax.ShapeDtypeStruct((rows, width), F32), jax.ShapeDtypeStruct((8, width), F32)],
         scratch_shapes=[pltpu.VMEM((heads, 3 * E, SEG0), BF)]
@@ -910,88 +922,316 @@
     return moved_part(value, count, place % per, start % per), lanes // count == start % per
 
 
-def merge_kernel(heads, starts, place, first, *refs):
-    seconds, (mixed, merged, lse) = refs[: BRANCHES - 1], refs[BRANCHES - 1 :]
-    head = pl.program_id(0)
-    extra = first[0, 0, E:, :].astype(F32)
-    merged[0] = first[0, 0, :E, :].astype(F32)
-    lse[0] = extra[0:1] + extra[1:2] + extra[2:3]
-    for branch in range(1, BRANCHES):
-        got = seconds[branch - 1]
-        count = branch_shape(branch, heads)[1]
-        start = starts[branch, head]
-        lanes = aligned(start, count)
-        for copy in range(got.shape[0]):
-            value, mask = placed_part(got[copy, 0].astype(F32), count, start, place[0])
-            new_lse = value[E : E + 1] + value[E + 1 : E + 2] + value[E + 2 : E + 3]
-            if mask is not None:
-                new_lse = jnp.where(mask, new_lse, -FAR)
-            old_lse = lse[0, :, lanes]
-            top = jnp.maximum(old_lse, new_lse)
-            both = top + jnp.log2(jnp.exp2(old_lse - top) + jnp.exp2(new_lse - top))
-            old_w = jnp.exp2(old_lse - both)
-            new_w = jnp.exp2(new_lse - both)
-            merged[0, :, lanes] = merged[0, :, lanes] * old_w + value[:E] * new_w
-            lse[0, :, lanes] = both
-    mixed[...] = merged[0].astype(BF)
-
-
-def merge_heads(heads, starts, place, first, seconds):
-    span = first.shape[-1]
-    return pl.pallas_call(
-        partial(merge_kernel, heads),
-        grid_spec=pltpu.PrefetchScalarGridSpec(
-            num_scalar_prefetch=2,
-            grid=(heads,),
-            in_specs=[pl.BlockSpec((1, 1, ROWS_OUT, span), lambda h, s, t: (0, h, 0, 0))]
-            + send_shapes(heads, ROWS_OUT)[1],
-            out_specs=[
-                pl.BlockSpec((E, span), lambda h, s, t: (h, 0)),
-                pl.BlockSpec((1, E, span), lambda h, s, t: (h, 0, 0)),
-                pl.BlockSpec((1, 1, span), lambda h, s, t: (h, 0, 0)),
-            ],
+def middle_kernel(heads, *refs):
+    branches = BRANCHES - 1
+    names = Names(refs)
+    starts, first = names.take(2)
+    backs = names.take(branches)
+    x_rows, cot, out_proj, up, down, gain, shift = names.take(7)
+    block_out, grad_hidden, gains_two, own_g = names.take(4)
+    sends = names.take(branches)
+    chunks = up.shape[1] // min(up.shape[1], x_rows.shape[1])
+    halves = names.take(2 * chunks)
+    out_total = names.one()
+    merged, lse, mixed, turned, part, got, part_two, got_two = names.take(8)
+    hidden_one, normed_own, normed, spread_rows, normed_t, cot_t = names.take(6)
+    down_sum, norm_sum, up_grad, down_grad, totals = names.take(5)
+    head_sems, first_sems = names.take(2)
+
+    head_size, me_head = lax.axis_size("head"), lax.axis_index("head")
+    me = lax.axis_index("seq")
+    rest = lax.axis_size("seq") // 4
+    width = x_rows.shape[1]
+    per_slot = x_rows.shape[0] // SLOTS
+    tile = 256
+
+    meet("seq", "head")
+
+    @pl.loop(0, heads)
+    def _(head):
+        own = first[0, head].astype(F32)
+        merged[head] = own[:E]
+        lse[head] = own[E : E + 1] + own[E + 1 : E + 2] + own[E + 2 : E + 3]
+        for branch in range(1, BRANCHES):
+            stride, lanes, per, split = branch_shape(branch, heads)
+            back, start = backs[branch - 1], starts[branch, head]
+            share = max(1, 128 // lanes)
+            for copy in range(split):
+                if split == 1:
+                    value = back[head // per, head % per].astype(F32)
+                else:
+                    value = back[head * split + copy, 0].astype(F32)
+                if share > 1:
+                    value = moved_part(value, lanes, me % share, start % share)
+                new_lse = value[E : E + 1] + value[E + 1 : E + 2] + value[E + 2 : E + 3]
+                if share > 1:
+                    ids = lax.broadcasted_iota(jnp.int32, new_lse.shape, 1)
+                    new_lse = jnp.where(ids // lanes == start % share, new_lse, -FAR)
+                span = lanes * share
+                for block in range(SEG0 // span):
+                    at = slice(block * span, (block + 1) * span)
+                    new = jnp.where(start // share == block, new_lse, -FAR)
+                    old = lse[head, :, at]
+                    top = jnp.maximum(old, new)
+                    both = top + jnp.log2(jnp.exp2(old - top) + jnp.exp2(new - top))
+                    lse[head, :, at] = both
+                    merged[head, :, at] = merged[head, :, at] * jnp.exp2(old - both) + value[:E] * jnp.exp2(
+                        new - both
+                    )
+        mixed[head] = merged[head].astype(BF)
+
+    def head_copies(kind, source, target, sem):
+        copies = []
+        for step in range(1, head_size):
+            device = (me_head + step) % head_size
+            copies.append(
+                pltpu.make_async_remote_copy(
+                    src_ref=source.at[:, device] if kind == 0 else source,
+                    dst_ref=target.at[step - 1] if kind == 0 else target.at[:, me_head],
+                    send_sem=head_sems.at[0, sem, step - 1],
+                    recv_sem=head_sems.at[1, sem, step - 1],
+                    device_id={"head": device},
+                    device_id_type=pl.DeviceIdType.MESH,
+                )
+            )
+        return copies
+
+    def rows_of(ref):
+        return ref[...].reshape(SEG0, width)
+
+    turned[...] = mixed[...].reshape(heads * E, SEG0).T
+    for step in range(SEG0 // tile):
+        at = slice(step * tile // (head_size * per_slot), (step + 1) * tile // (head_size * per_slot))
+        value = jnp.dot(turned[step * tile : (step + 1) * tile], out_proj[...], preferred_element_type=F32)
+        part[at] = value.astype(BF).reshape(-1, head_size, per_slot, width)
+    for copy in head_copies(0, part, got, 0):
+        copy.start()
+    cot_t[...] = rows_of(cot).T
+    for copy in head_copies(0, part, got, 0):
+        copy.wait()
+
+    def norm_of(values):
+        centred = values - jnp.mean(values, axis=-1, keepdims=True)
+        scale = lax.rsqrt(jnp.mean(centred * centred, axis=-1, keepdims=True) + EPS)
+        return centred * scale, scale
+
+    def rows_at(slot):
+        return pl.ds(pl.multiple_of(slot * per_slot, per_slot), per_slot)
+
+    @pl.loop(0, SLOTS)
+    def _(slot):
+        value = x_rows[rows_at(slot)] + part[slot, me_head].astype(F32)
+        for step in range(1, head_size):
+            value = value + got[step - 1, slot].astype(F32)
+        hidden_one[rows_at(slot)] = value
+        unit, scale = norm_of(value)
+        low = (unit * gain[...] + shift[...]).astype(BF)
+        normed_own[slot] = low
+        normed[slot, me_head] = low
+
+    for copy in head_copies(1, normed_own, normed, 1):
+        copy.start()
+    for copy in head_copies(1, normed_own, normed, 1):
+        copy.wait()
+    normed_t[...] = rows_of(normed).T
+
+    chunk_width = up.shape[1] // chunks
+    orders = {0: ORDERS["u1"], 1: ORDERS["d1"]}
+    firsts = []
+    for chunk in range(chunks):
+        for kind in range(2):
+            index = 2 * chunk + kind
+            firsts.append(
+                Reduction(
+                    orders[kind], totals.at[index], halves[index], None, None,
+                    first_sems.at[0, pl.ds(index, 1)], first_sems.at[1, pl.ds(index, 1)],
+                )
+            )
+    down_sum[...] = jnp.zeros_like(down_sum)
+    norm_sum[...] = jnp.zeros_like(norm_sum)
+    slots = tile // (head_size * per_slot)
+    contract_last = (((1,), (1,)), ((), ()))
+
+    for chunk in range(chunks):
+        units = slice(chunk * chunk_width, (chunk + 1) * chunk_width)
+        up_grad[...] = jnp.zeros_like(up_grad)
+        down_grad[...] = jnp.zeros_like(down_grad)
+
+        @pl.loop(0, SEG0 // tile)
+        def _(step):
+            rows = pl.ds(pl.multiple_of(step * tile, tile), tile)
+            low = normed[pl.ds(step * slots, slots)].reshape(tile, width)
+            back = cot[pl.ds(step * slots, slots)].reshape(tile, width)
+            pre = jnp.dot(low, up[:, units], preferred_element_type=F32)
+            grad = lax.dot_general(back, down[units], contract_last, preferred_element_type=F32)
+            share = 0.5 + 0.5 * lax.erf(pre * math.sqrt(0.5))
+            density = jnp.exp2(pre * pre * (-0.5 * LOG2E)) * (1.0 / math.sqrt(2.0 * math.pi))
+            hidden = (pre * share).astype(BF)
+            grad = (grad * (share + pre * density)).astype(BF)
+            down_sum[rows] += jnp.dot(hidden, down[units], preferred_element_type=F32)
+            norm_sum[rows] += lax.dot_general(grad, up[:, units], contract_last, preferred_element_type=F32)
+            up_grad[...] += jnp.dot(normed_t[:, rows], grad, preferred_element_type=F32)
+            down_grad[...] += jnp.dot(cot_t[:, rows], hidden, preferred_element_type=F32)
+
+        pieces = totals.shape[3] * 4
+        size = totals.shape[4]
+        turned_down = down_grad[...].T
+        for piece in range(pieces):
+            spot = (piece // (2 * rest), piece // rest % 2, piece % rest)
+            span = slice(piece * size, (piece + 1) * size)
+            totals[(2 * chunk,) + spot] = up_grad[span].astype(BF)
+            totals[(2 * chunk + 1,) + spot] = turned_down[span].astype(BF)
+        firsts[2 * chunk].step(0)
+        firsts[2 * chunk + 1].step(0)
+
+    for ref, value in ((part, down_sum), (part_two, norm_sum)):
+
+        @pl.loop(0, SLOTS)
+        def _(slot):
+            for device in range(head_size):
+                begin = pl.multiple_of((slot * head_size + device) * per_slot, per_slot)
+                ref[slot, device] = value[pl.ds(begin, per_slot)].astype(BF)
+
+    for copy in head_copies(0, part_two, got_two, 2) + head_copies(0, part, got, 3):
+        copy.start()
+    for copy in head_copies(0, part_two, got_two, 2):
+        copy.wait()
+    gains_two[...] = jnp.zeros_like(gains_two)
+
+    @pl.loop(0, SLOTS)
+    def _(slot):
+        grad = part_two[slot, me_head].astype(F32)
+        for step in range(1, head_size):
+            grad = grad + got_two[step - 1, slot].astype(F32)
+        unit, scale = norm_of(hidden_one[rows_at(slot)])
+        scaled = grad * gain[...]
+        inner = jnp.mean(scaled * unit, axis=-1, keepdims=True)
+        out = cot[slot, me_head].astype(F32) + scale * (
+            scaled - jnp.mean(scaled, axis=-1, keepdims=True) - unit * inner
+        )
+        grad_hidden[rows_at(slot)] = out
+        normed_own[slot] = out.astype(BF)
+        normed[slot, me_head] = out.astype(BF)
+        gains_two[0:1] += jnp.sum(grad * unit, axis=0, keepdims=True)
+        gains_two[1:2] += jnp.sum(grad, axis=0, keepdims=True)
+
+    for copy in head_copies(1, normed_own, normed, 4):
+        copy.start()
+    for copy in head_copies(0, part, got, 3):
+        copy.wait()
+
+    @pl.loop(0, SLOTS)
+    def _(slot):
+        value = hidden_one[rows_at(slot)] + part[slot, me_head].astype(F32)
+        for step in range(1, head_size):
+            value = value + got[step - 1, slot].astype(F32)
+        place = slot % 2 * 8 + slot // 2 % 2 * 4 + slot // 4 % 2 * 2 + slot // 8
+        for column in range(width // 128):
+            lanes = slice(column * 128, (column + 1) * 128)
+            spread_rows[column, pl.ds(place, per_slot, stride=SLOTS), :] = value[:, lanes]
+
+    for column in range(width // 128):
+        block_out[:, column * 128 : (column + 1) * 128] = spread_rows[column].astype(BF)
+    for copy in head_copies(1, normed_own, normed, 4):
+        copy.wait()
+
+    value = jnp.dot(mixed[...].reshape(heads * E, SEG0), rows_of(normed), preferred_element_type=F32)
+    size = out_total.shape[3]
+    for piece in range(4 * rest):
+        spot = (piece // (2 * rest), piece // rest % 2, piece % rest)
+        out_total[spot] = value[piece * size : (piece + 1) * size].astype(BF)
+
+    @pl.loop(0, heads)
+    def _(head):
+        rows = pl.ds(pl.multiple_of(head * E, 16), E)
+        grad = lax.dot_general(out_proj[rows], rows_of(normed), contract_last, preferred_element_type=F32)
+        low = grad.astype(BF)
+        dots = jnp.sum(low.astype(F32) * merged[head], axis=0, keepdims=True)
+        own_g[0, head, :E, :] = low
+        d = pieces_of(-dots)
+        m = pieces_of(-lse[head])
+        placed = {0: d[0], 1: d[1], 2: d[2], 12: m[0], 13: m[1], 14: m[2]}
+        own_g[0, head, E:, :] = row_block(placed, SEG0).astype(BF)
+        own = jnp.concatenate([low.astype(F32), row_block(placed, SEG0)], axis=0)
+        for branch in range(1, BRANCHES):
+            stride, lanes, per, split = branch_shape(branch, heads)
+            send, start = sends[branch - 1], starts[branch, head]
+            share = max(1, 128 // lanes)
+            span = lanes * share
+            block = own[:, :span]
+            for part_at in range(1, SEG0 // span):
+                block = jnp.where(start // share == part_at, own[:, part_at * span : (part_at + 1) * span], block)
+            if share > 1:
+                block = moved_part(block, lanes, start % share, me % share)
+            block = block.astype(BF)
+            if split == 1:
+                send[head // per, head % per] = block
+            else:
+                for copy in range(split):
+                    send[head * split + copy, 0] = block
+
+    for reduction in firsts:
+        reduction.finish_first()
+
+
+def middle(heads, starts, first, backs, x_rows, cot, out_proj, up, down, gain, shift):
+    size, head_size = lax.axis_size("seq"), lax.axis_size("head")
+    rest = size // 4
+    rows, width = x_rows.shape
+    per_slot = rows // SLOTS
+    chunks = max(1, up.shape[1] // width)
+    shard = (SLOTS, head_size, per_slot, width)
+    own = (SLOTS, per_slot, width)
+    got = (head_size - 1,) + own
+    sends = send_shapes(heads, ROWS_OUT)[0]
+    piece = (2, rest, width // size, up.shape[1] // chunks)
+    out_piece = (2, 2, rest, heads * E // size, width)
+    results = pl.pallas_call(
+        partial(middle_kernel, heads),
+        in_specs=[pl.BlockSpec(memory_space=pltpu.SMEM)] + vmem_specs(1 + len(backs) + 7),
+        out_specs=vmem_specs(4 + len(sends) + 2 * chunks + 1),
+        out_shape=[
+            jax.ShapeDtypeStruct((rows, width), BF),
+            jax.ShapeDtypeStruct((rows, width), F32),
+            jax.ShapeDtypeStruct((2, width), F32),
+            jax.ShapeDtypeStruct((1, heads, ROWS_OUT, SEG0), BF),
+        ]
+        + sends
+        + [jax.ShapeDtypeStruct(piece, BF)] * (2 * chunks)
+        + [jax.ShapeDtypeStruct(out_piece, BF)],
+        scratch_shapes=[
+            pltpu.VMEM((heads, E, SEG0), F32),
+            pltpu.VMEM((heads, 1, SEG0), F32),
+            pltpu.VMEM((heads, E, SEG0), BF),
+            pltpu.VMEM((SEG0, heads * E), BF),
+            pltpu.VMEM(shard, BF),
+            pltpu.VMEM(got, BF),
+            pltpu.VMEM(shard, BF),
+            pltpu.VMEM(got, BF),
+            pltpu.VMEM((rows, width), F32),
+            pltpu.VMEM(own, BF),
+            pltpu.VMEM(shard, BF),
+            pltpu.VMEM((width // 128, rows, 128), F32),
+            pltpu.VMEM((width, SEG0), BF),
+            pltpu.VMEM((width, SEG0), BF),
+            pltpu.VMEM((SEG0, width), F32),
+            pltpu.VMEM((SEG0, width), F32),
+            pltpu.VMEM((width, up.shape[1] // chunks), F32),
+            pltpu.VMEM((width, up.shape[1] // chunks), F32),
+            pltpu.VMEM((2 * chunks, 2) + piece, BF),
+            pltpu.SemaphoreType.DMA((2, 5, head_size - 1)),
+            pltpu.SemaphoreType.DMA((2, 2 * chunks)),
+        ],
+        compiler_params=pltpu.CompilerParams(
+            vmem_limit_bytes=60 * 2**20, collective_id=2, has_side_effects=True
         ),
-        out_shape=[
-            jax.ShapeDtypeStruct((heads * E, span), BF),
-            jax.ShapeDtypeStruct((heads, E, span), F32),
-            jax.ShapeDtypeStruct((heads, 1, span), F32),
-        ],
-        compiler_params=params(),
-        name="merge_heads",
-    )(starts, place, first, *seconds)
-
-
-def spread_kernel(heads, starts, place, grad, merged, lse, own, *sends):
-    head = pl.program_id(0)
-    low = grad[...].astype(BF)
-    dots = jnp.sum(low.astype(F32) * merged[0], axis=0, keepdims=True)
-    own[0, 0, :E, :] = low
-    d = pieces_of(-dots)
-    m = pieces_of(-lse[0])
-    placed = {0: d[0], 1: d[1], 2: d[2], 12: m[0], 13: m[1], 14: m[2]}
-    own[0, 0, E:, :] = row_block(placed, grad.shape[-1]).astype(BF)
-    send_blocks(heads, head, starts, place, own, sends)
-
-
-def spread_heads(heads, starts, place, grad, merged, lse):
-    span = grad.shape[-1]
-    sends, send_specs = send_shapes(heads, ROWS_OUT)
-    return pl.pallas_call(
-        partial(spread_kernel, heads),
-        grid_spec=pltpu.PrefetchScalarGridSpec(
-            num_scalar_prefetch=2,
-            grid=(heads,),
-            in_specs=[
-                pl.BlockSpec((E, span), lambda h, s, t: (h, 0)),
-                pl.BlockSpec((1, E, span), lambda h, s, t: (h, 0, 0)),
-                pl.BlockSpec((1, 1, span), lambda h, s, t: (h, 0, 0)),
-            ],
-            out_specs=[pl.BlockSpec((1, 1, ROWS_OUT, span), lambda h, s, t: (0, h, 0, 0))] + send_specs,
+        cost_estimate=pl.CostEstimate(
+            flops=14 * SEG0 * width * up.shape[1], transcendentals=0, bytes_accessed=40 * 2**20
         ),
-        out_shape=[jax.ShapeDtypeStruct((1, heads, ROWS_OUT, span), BF)] + sends,
-        compiler_params=params(),
-        name="spread_heads",
-    )(starts, place, grad, merged, lse)
+        name="middle",
+    )(starts, first, *backs, x_rows, cot.reshape(shard), out_proj, up, down, gain, shift)
+    block_out, grad_hidden, gains_two, own_g = results[:4]
+    return block_out, grad_hidden, gains_two, own_g, results[4 : 4 + len(sends)], results[4 + len(sends) :]
 
 
 def rolled(value, step):
@@ -1039,7 +1279,6 @@
     seq_len = row_count * head_count
     heads = offsets.shape[1]
     per_slot = row_count // SLOTS
-    gelu_exact = partial(jax.nn.gelu, approximate=False)
 
     ids = lax.broadcasted_iota(jnp.int32, (row_count, row_count), 0)
     slot = reversed_bits(ids // per_slot, 4)
@@ -1077,48 +1316,13 @@
     place = seq_id.astype(jnp.int32).reshape(1)
     own, *sends = pack_heads(heads, starts, place, projected, bits)
     first_out, units, outs = exchange_forward(heads, own, sends)
-    mixed, merged, lse = merge_heads(heads, starts, place, first_out, outs)
-
-    attn_part = jnp.einsum("ct,cd->td", mixed, out_proj, preferred_element_type=F32).astype(BF)
-    hidden_one = x_rows + sum_rows(device_parts(attn_part))
-    normed_two = norm_rows(hidden_one, second_gain, second_shift)
-    gathered_two = shard_rows(normed_two.astype(BF))
-    pre_act = jnp.dot(gathered_two, up_proj, preferred_element_type=F32)
-    hidden, gelu_pull = jax.vjp(gelu_exact, pre_act)
-    hidden = hidden.astype(BF)
-    down_part = jnp.dot(hidden, down_proj, preferred_element_type=F32).astype(BF)
-    block_rows = hidden_one + sum_rows(device_parts(down_part))
-    block_out = jnp.dot(order.T, block_rows.astype(BF), preferred_element_type=F32).astype(BF)
-
-    chunks = max(1, up_proj.shape[1] // width)
-
-    def columns(values):
-        return jnp.split(values, chunks, axis=1)
-
-    grad_down = [
-        jnp.einsum("tf,td->fd", part, cot_all, preferred_element_type=F32).astype(BF) for part in columns(hidden)
-    ]
-    grad_act = jnp.einsum("td,fd->tf", cot_all, down_proj, preferred_element_type=F32)
-    grad_pre = gelu_pull(grad_act)[0].astype(BF)
-    grad_up = [
-        jnp.einsum("td,tf->df", gathered_two, part, preferred_element_type=F32).astype(BF)
-        for part in columns(grad_pre)
-    ]
-    norm_part = jnp.einsum("tf,df->td", grad_pre, up_proj, preferred_element_type=F32).astype(BF)
-    grad_normed_two = sum_rows(device_parts(norm_part))
-    pull_two = jax.vjp(norm_rows, hidden_one, second_gain, second_shift)[1]
-    grad_ln_two, grad_gain_two, grad_shift_two = pull_two(grad_normed_two)
-    grad_hidden_one = cot_low.astype(F32) + grad_ln_two
-    grad_attn = shard_rows(grad_hidden_one.astype(BF))
-    grad_out = jnp.einsum("ct,td->cd", mixed, grad_attn, preferred_element_type=F32).astype(BF)
-    grad_merged = jnp.einsum("td,cd->ct", grad_attn, out_proj, preferred_element_type=F32)
-
-    own_g, *sends_g = spread_heads(heads, starts, place, grad_merged, merged, lse)
-    terms = [term for pair in zip(grad_up, grad_down) for term in pair] + [grad_out]
-    gains_two = jnp.stack([grad_gain_two, grad_shift_two])
+    block_out, grad_hidden, gains_two, own_g, sends_g, parts = middle(
+        heads, starts, first_out, outs, x_rows, cot_all, out_proj, up_proj, down_proj,
+        second_gain[None, :], second_shift[None, :],
+    )
     sums, grad_in, grad_tokens, gains = backward(
-        heads, starts, own, own_g, units, sends_g, terms,
-        gathered_one, in_proj, x_rows, grad_hidden_one, first_gain[None, :], gains_two,
+        heads, starts, own, own_g, units, sends_g, parts,
+        gathered_one, in_proj, x_rows, grad_hidden, first_gain[None, :], gains_two,
     )
     return (
         block_out,

time: 353 us -> 320 us (0.907)
  matrix products: 51.8 us -> 6.86 us
  Pallas kernels: 242 us -> 275 us
  other arithmetic: 28.9 us -> 17.5 us
  local copies, waits for them, and re-layouts: 22.2 us -> 16.2 us
    pallas_call x2 -> x1, Pallas kernels: 4.17 us -> 61.7 us  [middle(): pl.pallas_call(partial(middle_kernel, heads), in_specs=[pl.BlockSpec(memo...]
    dot_general x12 -> x0, matrix products: 43.7 us -> none  [the longest x1 16.4 us: local(): jnp.einsum('td,fd->tf', cot_all, down_proj, preferred_element_type=F32)]
    pallas_call x1, Pallas kernels: 171 us -> 147 us  [backward(): pl.pallas_call(partial(backward_kernel, heads, streams), in_specs=[pl.Blo...]
    convert_element_type x3 -> x0, other arithmetic: 6.15 us -> none  [the longest x1 3.3 us: local(): hidden = hidden.astype(BF)]
    unnamed x85 -> x62, local copies, waits for them, and re-layouts: 18 us -> 12.4 us
    reduce_sum x3 -> x0, other arithmetic: 3.74 us -> none  [the longest x1 2.18 us: norm_rows(): centre = jnp.mean(values, axis=-1, keepdims=True)]
  transfers between devices with their start and end apart: 7 -> 2, of which waited for: 0 -> 0; matrix products, arithmetic and copies ran while one was open for 7% -> 2% of each run, Pallas kernels for 0% -> 0%
where the time goes in v6:
time: 320 us; the launch traced here: 317 us
  Pallas kernels  275 us (86%)
  other arithmetic  17.5 us (5%)
  local copies, waits for them, and re-layouts  16.2 us (5%)
  matrix products  6.86 us (2%)
    pallas_call x1, Pallas kernels, backward(): pl.pallas_call(partial(backward_kernel, heads, streams), in_specs=[pl.Blo...  147 us
    pallas_call x1, Pallas kernels, exchange_forward(): pl.pallas_call(partial(exchange_forward_kernel, heads), in_specs=vmem_spe...  62.1 us
    pallas_call x1, Pallas kernels, middle(): pl.pallas_call(partial(middle_kernel, heads), in_specs=[pl.BlockSpec(memo...  61.7 us
    unnamed x62, local copies, waits for them, and re-layouts  12.4 us
  transfers between devices with their start and end apart: 2, of which 0 were waited for; matrix products, arithmetic and copies ran while one was open for 2% of the time, Pallas kernels for 0%

profile of v6, /device:TPU:0, one launch (start us, length us, event | category | flops | bytes accessed | tf_op | source)
XLA Modules:
  0.0 316.9 jit_solution(12035283792604788756)
XLA Ops:
  0.7 1.1 copy-done
  1.8 1.6 fusion.51
  4.1 1.2 add_convert_fusion
  5.8 3.2 %convolution_convert_fusion = bf16[512,768]{1,0:T(8,128)(2,1)} fusion(bf16[512,768]{1,0:T(8,128)(2,1)S(1)} %copy-done.28, s32[512]{0:T(512)S(1)} %get-tuple-element.98, s32[512]{0:T(512)S(1)} %get-tuple-element.101, s32[512]{0:T(512)S(1)} %get-tuple-element.99, s32[512]{0:T(512)S(1)} %get-tuple-element.100, pred[512]{0:T(512)(128)(4,1)S(1)} %get-tuple-element.102, ...), kind=kOutput, calls=%fused_computation.32 | convolution fusion | flops 424804352 | bytes 1582080 | tf_op jit(solution)/shard_map/dot_general | solution.py:1289
  9.6 0.7 dynamic_slice.3
  11.0 0.6 broadcast_in_dim.39.refs_11_
  12.3 0.8 select_convert_fusion.bits
  13.8 2.0 broadcast_select_fusion.1
  15.9 1.3 pad_maximum_fusion.1.refs_7_
  17.2 0.7 copy-done.27
  17.9 2.1 fusion.proj
  20.0 4.1 %pack_heads.1 = (bf16[1,8,160,1024]{3,2,1,0:T(8,128)(2,1)}, bf16[2,4,160,512]{3,2,1,0:T(8,128)(2,1)S(1)}, bf16[4,2,160,256]{3,2,1,0:T(8,128)(2,1)S(1)}, bf16[8,1...) custom-call(s32[5,8]{1,0:T(8,128)S(1)} %stack.16.starts.refs_0_, s32[1]{0:T(128)} %bitcast.place, ...), custom_call_target="tpu_custom_call" | custom-call | tf_op jit(solution)/shard_map/pack_heads/pallas_call | solution.py:126
  24.1 1.1 copy-done.2
  25.2 62.1 %exchange_forward.1 = (bf16[1,8,64,1024]{3,2,1,0:T(8,128)(2,1)S(1)}, bf16[2,4,160,512]{3,2,1,0:T(8,128)(2,1)}, bf16[4,2,160,256]{3,2,1,0:T(8,128)(2,1)S(1)}, bf1...) custom-call(bf16[1,8,160,1024]{3,2,1,0:T(8,128)(2,1)} %get-tuple-ele, ...), custom_call_target="tpu_custom_call" | custom-call | flops 17179869184 | bytes 16384000 | tf_op jit(solution)/shard_map/exchange_forward/pallas_call | solution.py:454
  87.3 1.0 copy-done.3
  88.2 0.8 copy-done.4
  89.1 0.8 copy-done.5
  89.9 0.8 copy-done.6
  90.7 0.7 copy-done.7
  91.4 0.7 copy-done.8
  92.1 0.7 copy-done.9
  92.8 0.7 copy-done.10
  93.5 61.7 %middle.1 = (bf16[512,768]{1,0:T(8,128)(2,1)}, f32[512,768]{1,0:T(8,128)}, f32[2,768]{1,0:T(2,128)}, bf16[1,8,64,1024]{3,2,1,0:T(8,128)(2,1)}, bf16[2,4,64,512]{...) custom-call(s32[5,8]{1,0:T(8,128)} %copy-done.1, ...), custom_call_target="tpu_custom_call" | custom-call | flops 16911433728 | bytes 41943040 | tf_op jit(solution)/shard_map/middle/pallas_call | solution.py:1189
  155.2 146.9 %backward.1 = (bf16[2,2,4,48,768]{4,3,2,1,0:T(8,128)(2,1)}, bf16[2,2,4,48,768]{4,3,2,1,0:T(8,128)(2,1)}, bf16[2,2,4,48,768]{4,3,2,1,0:T(8,128)(2,1)}, bf16[2,2,4...) custom-call(s32[5,8]{1,0:T(8,128)} %copy-done.1, ...), custom_call_target="tpu_custom_call" | custom-call | flops 42949672960 | bytes 16384000 | tf_op jit(solution)/shard_map/backward/pallas_call | solution.py:867
  302.1 2.3 bitcast_convert_fusion
  304.3 0.6 slice_reduce_fusion
  305.0 4.2 %maximum_convert_fusion = f32[768,1536]{1,0:T(8,128)} fusion(bf16[768,768]{1,0:T(8,128)(2,1)} %bitcast.38, bf16[768,768]{1,0:T(8,128)(2,1)S(1)} %bitcast.37), kind=kLoop, calls=%fused_computation.6 | loop fusion | flops 4718592 | bytes 7077888 | tf_op jit(solution)/shard_map/convert_element_type | solution.py:1332
  309.2 2.5 maximum_convert_fusion.1
  311.8 2.1 maximum_convert_fusion.2
  313.9 0.9 copy.33
  314.8 0.8 copy-done.13
  315.6 1.1 copy.34
  (71 shorter events, 4.0 us)
Async XLA Ops:
  0.6 1.1 copy-start
  3.4 9.7 %copy-start.11 = (f32[512,768]{1,0:T(8,128)}, f32[512,768]{1,0:T(8,128)S(1)}, u32[]{:S(2)}) copy-start(f32[512,768]{1,0:T(8,128)S(1)} %get-tuple-element.97.refs_6_.refs_18_) | copy-start | bytes 4718596
  3.4 0.7 copy-start.21
  3.4 0.7 copy-start.22
  3.7 2.1 copy-start.28
  5.3 5.7 %copy-start.24 = (f32[768]{0:T(1024)S(1)}, f32[768]{0:T(1024)}, u32[]{:S(2)}) copy-start(f32[768]{0:T(1024)} %param.22) | copy-start | bytes 9220
  5.3 6.3 %copy-start.25 = (f32[768]{0:T(1024)S(1)}, f32[768]{0:T(1024)}, u32[]{:S(2)}) copy-start(f32[768]{0:T(1024)} %param.23) | copy-start | bytes 9220
  5.3 6.9 %copy-start.26 = (s32[5,8]{1,0:T(8,128)S(1)}, s32[5,8]{1,0:T(8,128)}, u32[]{:S(2)}) copy-start(s32[5,8]{1,0:T(8,128)} %param.15) | copy-start | bytes 484
  5.3 7.8 %collective-permute-start = (bf16[512,768]{1,0:T(8,128)(2,1)}, bf16[512,768]{1,0:T(8,128)(2,1)S(1)}, u32[]{:S(2)}, u32[]{:S(2)}) collective-permute-start(bf16[512,768]{1,0:T(8,128)(2,1)} %add_convert_fusion), channel_id=1, source_target_pairs={{0,1},{1,0},{2,3},{3,2},{4,5},{5,4},{6,7},{7,6},{8,9},{9,8},{10,11... | collective-permute-start | bytes 2359304 | tf_op jit(solution)/shard_map/ppermute | solution.py:1239
  9.0 4.8 %collective-permute-start.1 = (bf16[512,768]{1,0:T(8,128)(2,1)}, bf16[512,768]{1,0:T(8,128)(2,1)}, u32[]{:S(2)}, u32[]{:S(2)}) collective-permute-start(bf16[512,768]{1,0:T(8,128)(2,1)} %convolution_convert_fusion), channel_id=1, source_target_pairs={{0,1},{1,0},{2,3},{3,2},{4,5},{5,4},{6,7},{7,6},{8,9},{9,8},{10,11... | collective-permute-start | bytes 2359304 | tf_op jit(solution)/shard_map/ppermute | solution.py:1239
  12.3 7.7 %copy-start.1 = (s32[5,8]{1,0:T(8,128)}, s32[5,8]{1,0:T(8,128)S(1)}, u32[]{:S(2)}) copy-start(s32[5,8]{1,0:T(8,128)S(1)} %stack.16.starts.refs_0_) | copy-start | bytes 484
  13.8 3.4 %copy-start.12 = (bf16[16,2,32,768]{3,2,1,0:T(8,128)(2,1)}, bf16[16,2,32,768]{3,2,1,0:T(8,128)(2,1)S(1)}, u32[]{:S(2)}) copy-start(bf16[16,2,32,768]{3,2,1,0:T(8,128)(2,1)S(1)} %pad_maximum_fusion) | copy-start | bytes 4718596
  15.9 2.0 copy-start.27
  15.9 2.0 copy-start.29
  24.1 1.1 copy-start.2
  87.2 1.0 copy-start.3
  88.2 0.8 copy-start.4
  89.1 0.8 copy-start.5
  89.9 0.8 copy-start.6
  90.7 0.7 copy-start.7
  91.4 0.7 copy-start.8
  92.1 0.7 copy-start.9
  92.8 0.7 copy-start.10
  302.1 2.3 copy-start.23
  302.1 2.9 copy-start.16
  305.0 4.3 %copy-start.14 = (bf16[2,2,4,48,768]{4,3,2,1,0:T(8,128)(2,1)S(1)}, bf16[2,2,4,48,768]{4,3,2,1,0:T(8,128)(2,1)}, u32[]{:S(2)}) copy-start(bf16[2,2,4,48,768]{4,3,2,1,0:T(8,128)(2,1)} %get-tuple-element.81) | copy-start | bytes 3538948
  305.0 4.3 %copy-start.15 = (bf16[2,2,4,48,768]{4,3,2,1,0:T(8,128)(2,1)S(1)}, bf16[2,2,4,48,768]{4,3,2,1,0:T(8,128)(2,1)}, u32[]{:S(2)}) copy-start(bf16[2,2,4,48,768]{4,3,2,1,0:T(8,128)(2,1)} %get-tuple-element.82) | copy-start | bytes 3538948
  309.2 2.6 copy-start.18
  309.2 2.6 copy-start.19
  309.2 2.6 copy-start.20
  311.8 2.1 copy-start.17
  313.9 1.7 copy-start.13
